TPU v7x, 128 devices: a whole 4x4x4 slice. The times are simulated.
128 devices in a mesh: pair: 2 (over x_hi), gx: 8 (over y, x_lo), gy: 8 (over z, core).
Axes of the slice: x: 4 (x_hi: 2, x_lo: 2; x = x_hi * 2 + x_lo), y: 4, z: 4, core: 2. Of those that a mesh axis runs over, the one named last changes fastest.
Arguments:
- sound_speed_sq: float32 [64, 64, 1024], P('gx', 'gy'), may hold values from 0.5 to 2
- wind_profile: float32 [3, 1024], replicated, may hold values from -0.6 to 0.6
- forward_field: bfloat16 [4, 4, 64, 64, 1024], P(None, None, 'gx', 'gy'), may hold values from -6 to 6
- adjoint_state: float32 [2, 4, 64, 64, 1024], P('pair', None, 'gx', 'gy'), may hold values from -0.3125 to 0.3125
- pair_counts: int32 [2], P('pair'), may hold values from 64 to 256, as said below
- source_cells: int32 [512, 3], P('pair'), may hold values from 0 to 1023, as said below
- receiver_cells: int32 [512, 3], P('pair'), may hold values from 0 to 1023, as said below
- residuals: float32 [512, 4], P('pair'), may hold values from -16 to 16
Outputs:
- kernels: float32 [4, 64, 64, 1024], P(None, 'gx', 'gy', 'pair')
- final_state: float32 [2, 4, 64, 64, 1024], P('pair', None, 'gx', 'gy')
Inputs may be any that keep to these rules, and one draw needn't show every extreme that they name: `pair_counts`: one group in every draw has exactly 256 live pairs. `source_cells`: columns are the cell along the first, second and third dimension, each within the grid. `receiver_cells`: columns are the cell along the first, second and third dimension, each within the grid; several pairs may share a cell.
All inputs are finite; a program needn't handle non-finite values.
Results may differ from a plain program's by a relative error of at most 0.00115.
Values may be sent and summed in bfloat16 or wider, within the bound.
A program may use at most 128 MiB of HBM per device.

v0:
```python
import jax
import jax.numpy as jnp
from jax import lax
from jax.sharding import PartitionSpec as P

step_length = 0.25


def extended(shard, sides, width):
    for axis, dim in sides:
        size, length = (lax.axis_size(axis), shard.shape[dim])
        up = [(i, (i + 1) % size) for i in range(size - 1)]
        down = [(j, i) for i, j in up]
        last = lax.slice_in_dim(shard, length - width, length, axis=dim)
        initial = lax.slice_in_dim(shard, 0, width, axis=dim)
        before = lax.ppermute(last, axis, up)
        after = lax.ppermute(initial, axis, down)
        shard = jnp.concatenate([before, shard, after], axis=dim)
    return shard


def central(padded):
    dims = padded.ndim
    east_diff = (padded[..., 2:, 1:-1, :] - padded[..., :-2, 1:-1, :]) * 0.5
    north_diff = (padded[..., 1:-1, 2:, :] - padded[..., 1:-1, :-2, :]) * 0.5
    center = padded[..., 1:-1, 1:-1, :]
    vertical = jnp.pad(center, [(0, 0)] * (dims - 1) + [(1, 1)])
    up_diff = (vertical[..., 2:] - vertical[..., :-2]) * 0.5
    return (east_diff, north_diff, up_diff, center)


def local_flat(cells, width_x, width_y, depth):
    local_x = cells[:, 0] - lax.axis_index("gx") * width_x
    local_y = cells[:, 1] - lax.axis_index("gy") * width_y
    inside = (local_x >= 0) & (local_x < width_x) & (local_y >= 0) & (local_y < width_y)
    flat = (
        jnp.clip(local_x, 0, width_x - 1) * width_y + jnp.clip(local_y, 0, width_y - 1)
    ) * depth + cells[:, 2]
    return (flat, inside.astype(jnp.float32))


def shards(
    sound_speed_sq,
    wind_profile,
    forward_field,
    adjoint_state,
    pair_counts,
    source_cells,
    receiver_cells,
    residuals,
):
    steps_total = forward_field.shape[0]
    width_x, width_y, depth = sound_speed_sq.shape
    slots = residuals.shape[0]
    east_wind = wind_profile[0]
    north_wind = wind_profile[1]
    vertical_wind = wind_profile[2]
    live = (jnp.arange(slots, dtype=jnp.int32) < pair_counts[0]).astype(jnp.float32)
    src_flat, src_inside = local_flat(source_cells, width_x, width_y, depth)
    rcv_flat, rcv_inside = local_flat(receiver_cells, width_x, width_y, depth)
    pressure_snaps = forward_field[:, 0].reshape(steps_total, -1)
    local_samples = (
        jnp.take(pressure_snaps, src_flat, axis=1).astype(jnp.float32) * src_inside[None, :]
    )
    samples = lax.psum(local_samples, ("gx", "gy"))
    state = adjoint_state[0]
    kernel_local = jnp.zeros((4, width_x, width_y, depth), jnp.float32)
    for step in range(steps_total):
        snap = steps_total - 1 - step
        amplitude = residuals[:, snap] * samples[snap] * live * rcv_inside
        injected = (
            jnp.zeros((width_x * width_y * depth,), jnp.float32)
            .at[rcv_flat]
            .add(amplitude)
            .reshape(width_x, width_y, depth)
        )
        padded = extended(state, (("gx", 1), ("gy", 2)), 1)
        east_diff, north_diff, up_diff, center = central(padded)
        pressure = center[0]
        velocity = center[1:]
        divergence = east_diff[1] + north_diff[2] + up_diff[3]
        p_new = (
            pressure
            + step_length
            * (
                sound_speed_sq * divergence
                + east_wind * east_diff[0]
                + north_wind * north_diff[0]
                + vertical_wind * up_diff[0]
            )
            + injected
        )
        p_padded = extended(p_new, (("gx", 0), ("gy", 1)), 1)
        p_east, p_north, p_up, unused_center = central(p_padded)
        gradient = jnp.stack([p_east, p_north, p_up])
        a_new = velocity + step_length * (
            gradient
            + east_wind * east_diff[1:]
            + north_wind * north_diff[1:]
            + vertical_wind * up_diff[1:]
        )
        forward_rim = extended(forward_field[snap], (("gx", 1), ("gy", 2)), 1).astype(jnp.float32)
        f_east, f_north, f_up, unused_forward = central(forward_rim)
        pieces = [p_new * (f_east[1] + f_north[2] + f_up[3])]
        for along in (f_east, f_north, f_up):
            pieces.append(
                p_new * along[0] + a_new[0] * along[1] + a_new[1] * along[2] + a_new[2] * along[3]
            )
        increment = jnp.stack(pieces)
        kernel_local = kernel_local + increment
        state = jnp.concatenate([p_new[None], a_new], axis=0)
    kernels = lax.psum_scatter(kernel_local, "pair", scatter_dimension=3, tiled=True)
    return (kernels, state[None])


def solution(mesh):
    in_specs = (
        P("gx", "gy", None),
        P(),
        P(None, None, "gx", "gy", None),
        P("pair", None, "gx", "gy", None),
        P("pair"),
        P("pair", None),
        P("pair", None),
        P("pair", None),
    )
    out_specs = (P(None, "gx", "gy", "pair"), P("pair", None, "gx", "gy", None))
    return jax.shard_map(shards, mesh=mesh, in_specs=in_specs, out_specs=out_specs, check_vma=False)
```

profile of v0, /device:TPU:0, one launch (start us, length us, event | category | flops | bytes accessed | tf_op | source)
XLA Modules:
  0.0 555.5 jit_solution(320897750737244086)
XLA Ops:
  7.2 1.8 slice_bitcast_fusion
  11.0 5.2 collective-permute-start.4
  16.9 3.8 collective-permute-start.1
  20.7 1.3 collective-permute-start
  24.0 1.9 slice.831
  27.0 13.0 %copy.11 = bf16[4,1,8,8,1024]{0,4,3,2,1:T(8,128)(2,1)} copy(bf16[4,1,8,8,1024]{4,3,2,1,0:T(8,128)(2,1)} %slice.831) | data formatting | bytes 1048576 | tf_op jit(solution)/shard_map/slice | solution.py:61
  40.1 8.7 %gather_fusion = bf16[256,4]{1,0:T(8,128)(2,1)S(1)} fusion(bf16[4,65536]{0,1:T(8,128)(2,1)} %bitcast.532, s32[1024]{0:T(1024)S(1)} %pad_clamp_fusion), kind=kCustom, calls=%fused_computation | custom fusion | bytes 5120 | tf_op jit(solution)/shard_map/jit(_take)/gather | solution.py:63
  48.8 283.8 %psum.7 = f32[4,256]{0,1:T(8,128)S(1)} all-reduce(f32[4,256]{0,1:T(8,128)S(1)} %multiply_bitcast_fusion), channel_id=1, replica_groups=mesh['pair'=2,'gx'=8,'gy'=8] {'gx','gy'}, use_global_device_ids=true, to_apply=%region_0.1 | all-reduce | flops 1024 | bytes 8192 | tf_op jit(solution)/shard_map/psum | solution.py:65
  337.7 2.3 scatter_custom_fusion
  340.7 2.3 scatter_custom_fusion.1
  343.8 2.3 scatter_custom_fusion.2
  346.8 2.9 scatter_custom_fusion.3
  350.7 1.3 collective-permute-start.16
  352.0 1.3 collective-permute-start.29
  354.5 4.5 collective-permute-start.28
  359.1 1.3 collective-permute-start.41
  361.5 4.5 collective-permute-start.40
  366.1 1.3 collective-permute-start.7
  367.6 3.0 collective-permute-start.6
  370.7 1.3 collective-permute-start.19
  372.2 3.0 collective-permute-start.18
  375.3 1.3 collective-permute-start.31
  377.8 3.8 collective-permute-start.3
  381.6 1.5 collective-permute-start.2
  383.1 1.6 maximum_convert_fusion
  385.9 4.4 collective-permute-start.30
  391.6 1.9 fusion.39
  393.9 2.8 collective-permute-start.9
  398.0 1.5 maximum_convert_fusion.1
  399.6 3.0 collective-permute-done.8
  402.6 2.8 collective-permute-start.11
  407.4 3.8 collective-permute-done.10
  412.0 2.8 collective-permute-start.13
  417.3 3.8 collective-permute-start.42
  421.9 3.2 collective-permute-start.15
  425.1 1.3 collective-permute-start.14
  427.1 2.2 collective-permute-done.14
  430.7 2.8 collective-permute-start.21
  435.5 3.9 collective-permute-done.20
  439.4 4.3 collective-permute-start.23
  445.8 1.9 collective-permute-done.22
  448.3 2.8 collective-permute-start.25
  451.2 1.3 collective-permute-start.24
  453.7 4.4 collective-permute-done.24
  458.2 3.2 collective-permute-start.27
  461.4 1.5 collective-permute-start.26
  464.2 1.4 collective-permute-done.26
  467.1 2.8 collective-permute-start.33
  471.6 4.2 collective-permute-done.32
  475.8 4.3 collective-permute-start.35
  480.2 1.3 collective-permute-start.34
  481.6 2.4 collective-permute-done.34
  484.8 2.8 collective-permute-start.37
  487.6 1.3 collective-permute-start.36
  490.1 4.4 collective-permute-done.36
  494.7 3.2 collective-permute-start.39
  499.4 3.6 collective-permute-done.38
  504.4 2.5 collective-permute-start.45
  508.6 4.2 collective-permute-done.44
  512.8 4.3 collective-permute-start.47
  517.1 1.3 collective-permute-start.46
  518.6 2.4 collective-permute-done.46
  522.2 1.5 fusion.41
  524.7 23.9 %reduce-scatter.2.cloned.1.call-done = f32[4,8,8,512]{3,2,1,0:T(8,128)} async-done(((f32[4,8,8,1024]{3,2,1,0:T(8,128)}), f32[4,8,8,512]{3,2,1,0:T(8,128)}) %reduce-scatter.2.cloned.1.call-update) | async-done | bytes 524304 | tf_op jit(solution)/shard_map/reduce_scatter | solution.py:112
  (138 shorter events, 49.3 us)
Async XLA Ops:
  7.2 9.0 %copy-start = (f32[1,4,8,8,1024]{4,3,2,1,0:T(8,128)S(1)}, f32[1,4,8,8,1024]{4,3,2,1,0:T(8,128)}, u32[]{:S(2)}) copy-start(f32[1,4,8,8,1024]{4,3,2,1,0:T(8,128)} %param.11) | copy-start | bytes 3145732
  7.2 18.7 %copy-start.6 = (f32[256,4]{0,1:T(4,128)S(1)}, f32[256,4]{0,1:T(4,128)}, u32[]{:S(2)}) copy-start(f32[256,4]{0,1:T(4,128)} %param.15) | copy-start | bytes 12292
  7.2 19.3 %copy-start.5 = (s32[256,3]{0,1:T(4,128)S(1)}, s32[256,3]{0,1:T(4,128)}, u32[]{:S(2)}) copy-start(s32[256,3]{0,1:T(4,128)} %param.14) | copy-start | bytes 9220
  7.2 19.8 %copy-start.7 = (s32[256,3]{0,1:T(4,128)S(1)}, s32[256,3]{0,1:T(4,128)}, u32[]{:S(2)}) copy-start(s32[256,3]{0,1:T(4,128)} %param.13) | copy-start | bytes 9220
  7.2 541.4 %reduce-scatter.2.cloned.1.call-start = ((), (), s32[]{:S(2)}) async-start(), calls=%async_computation.1 | async-start | bytes 1572864 | tf_op jit(solution)/shard_map/reduce_scatter | solution.py:112
  9.7 341.0 %collective-permute-start.5 = (bf16[4,1,8,1024]{3,2,1,0:T(8,128)(2,1)}, bf16[4,1,8,1024]{3,2,1,0:T(8,128)(2,1)}, u32[]{:S(2)}, u32[]{:S(2)}) collective-permute-start(bf16[4,1,8,1024]{3,2,1,0:T(8,128)(2,1)} %get-tuple-element.83), channel_id=1, source_target_pairs={{8,0},{16,8},{24,16},{32,24},{40,32},{48,40},{56,48},{9,1},{17,9},... | collective-permute-start | bytes 196616 | tf_op jit(solution)/shard_map/ppermute | solution.py:17
  11.0 341.0 %collective-permute-start.4 = (bf16[4,1,8,1024]{3,2,1,0:T(8,128)(2,1)}, bf16[4,1,8,1024]{3,2,1,0:T(8,128)(2,1)}, u32[]{:S(2)}, u32[]{:S(2)}) collective-permute-start(bf16[4,1,8,1024]{3,2,1,0:T(8,128)(2,1)} %get-tuple-element.82), channel_id=1, source_target_pairs={{0,8},{8,16},{16,24},{24,32},{32,40},{40,48},{48,56},{1,9},{9,17},... | collective-permute-start | bytes 196616 | tf_op jit(solution)/shard_map/ppermute | solution.py:16
  16.9 355.3 %collective-permute-start.1 = (f32[4,1,8,1024]{3,2,1,0:T(8,128)}, f32[4,1,8,1024]{3,2,1,0:T(8,128)S(1)}, u32[]{:S(2)}, u32[]{:S(2)}) collective-permute-start(f32[4,1,8,1024]{3,2,1,0:T(8,128)} %get-tuple-element.66), channel_id=1, source_target_pairs={{0,8},{8,16},{16,24},{24,32},{32,40},{40,48},{48,56},{1,9},{9,17},... | collective-permute-start | bytes 393224 | tf_op jit(solution)/shard_map/ppermute | solution.py:16
  20.7 354.5 %collective-permute-start = (f32[4,1,8,1024]{3,2,1,0:T(8,128)}, f32[4,1,8,1024]{3,2,1,0:T(8,128)}, u32[]{:S(2)}, u32[]{:S(2)}) collective-permute-start(f32[4,1,8,1024]{3,2,1,0:T(8,128)} %get-tuple-element.67), channel_id=1, source_target_pairs={{8,0},{16,8},{24,16},{32,24},{40,32},{48,40},{56,48},{9,1},{17,9},... | collective-permute-start | bytes 393224 | tf_op jit(solution)/shard_map/ppermute | solution.py:17
  22.7 331.8 %collective-permute-start.17 = (bf16[4,1,8,1024]{3,2,1,0:T(8,128)(2,1)}, bf16[4,1,8,1024]{3,2,1,0:T(8,128)(2,1)}, u32[]{:S(2)}, u32[]{:S(2)}) collective-permute-start(bf16[4,1,8,1024]{3,2,1,0:T(8,128)(2,1)} %get-tuple-element.81), channel_id=1, source_target_pairs={{8,0},{16,8},{24,16},{32,24},{40,32},{48,40},{56,48},{9,1},{17,9},... | collective-permute-start | bytes 196616 | tf_op jit(solution)/shard_map/ppermute | solution.py:17
  350.7 8.3 %collective-permute-start.16 = (bf16[4,1,8,1024]{3,2,1,0:T(8,128)(2,1)}, bf16[4,1,8,1024]{3,2,1,0:T(8,128)(2,1)S(1)}, u32[]{:S(2)}, u32[]{:S(2)}) collective-permute-start(bf16[4,1,8,1024]{3,2,1,0:T(8,128)(2,1)} %get-tuple-element.80), channel_id=1, source_target_pairs={{0,8},{8,16},{16,24},{24,32},{32,40},{40,48},{48,56},{1,9},{9,17},... | collective-permute-start | bytes 196616 | tf_op jit(solution)/shard_map/ppermute | solution.py:16
  352.0 9.5 %collective-permute-start.29 = (bf16[4,1,8,1024]{3,2,1,0:T(8,128)(2,1)}, bf16[4,1,8,1024]{3,2,1,0:T(8,128)(2,1)S(1)}, u32[]{:S(2)}, u32[]{:S(2)}) collective-permute-start(bf16[4,1,8,1024]{3,2,1,0:T(8,128)(2,1)} %get-tuple-element.79), channel_id=1, source_target_pairs={{8,0},{16,8},{24,16},{32,24},{40,32},{48,40},{56,48},{9,1},{17,9},... | collective-permute-start | bytes 196616 | tf_op jit(solution)/shard_map/ppermute | solution.py:17
  354.5 11.6 %collective-permute-start.28 = (bf16[4,1,8,1024]{3,2,1,0:T(8,128)(2,1)}, bf16[4,1,8,1024]{3,2,1,0:T(8,128)(2,1)S(1)}, u32[]{:S(2)}, u32[]{:S(2)}) collective-permute-start(bf16[4,1,8,1024]{3,2,1,0:T(8,128)(2,1)} %get-tuple-element.78), channel_id=1, source_target_pairs={{0,8},{8,16},{16,24},{24,32},{32,40},{40,48},{48,56},{1,9},{9,17},... | collective-permute-start | bytes 196616 | tf_op jit(solution)/shard_map/ppermute | solution.py:16
  359.1 8.5 %collective-permute-start.41 = (bf16[4,1,8,1024]{3,2,1,0:T(8,128)(2,1)}, bf16[4,1,8,1024]{3,2,1,0:T(8,128)(2,1)S(1)}, u32[]{:S(2)}, u32[]{:S(2)}) collective-permute-start(bf16[4,1,8,1024]{3,2,1,0:T(8,128)(2,1)} %get-tuple-element.77), channel_id=1, source_target_pairs={{8,0},{16,8},{24,16},{32,24},{40,32},{48,40},{56,48},{9,1},{17,9},... | collective-permute-start | bytes 196616 | tf_op jit(solution)/shard_map/ppermute | solution.py:17
  361.5 9.2 %collective-permute-start.40 = (bf16[4,1,8,1024]{3,2,1,0:T(8,128)(2,1)}, bf16[4,1,8,1024]{3,2,1,0:T(8,128)(2,1)S(1)}, u32[]{:S(2)}, u32[]{:S(2)}) collective-permute-start(bf16[4,1,8,1024]{3,2,1,0:T(8,128)(2,1)} %get-tuple-element.76), channel_id=1, source_target_pairs={{0,8},{8,16},{16,24},{24,32},{32,40},{40,48},{48,56},{1,9},{9,17},... | collective-permute-start | bytes 196616 | tf_op jit(solution)/shard_map/ppermute | solution.py:16
  366.1 11.7 %collective-permute-start.7 = (bf16[4,10,1,1024]{3,2,1,0:T(2,128)(2,1)S(1)}, bf16[4,10,1,1024]{3,2,1,0:T(2,128)(2,1)S(1)}, u32[]{:S(2)}, u32[]{:S(2)}) collective-permute-start(bf16[4,10,1,1024]{3,2,1,0:T(2,128)(2,1)S(1)} %get-tuple-element.75), channel_id=1, source_target_pairs={{1,0},{2,1},{3,2},{4,3},{5,4},{6,5},{7,6},{9,8},{10,9},{11,10},{12... | collective-permute-start | bytes 245768 | tf_op jit(solution)/shard_map/ppermute | solution.py:17
  367.6 13.9 %collective-permute-start.6 = (bf16[4,10,1,1024]{3,2,1,0:T(2,128)(2,1)S(1)}, bf16[4,10,1,1024]{3,2,1,0:T(2,128)(2,1)S(1)}, u32[]{:S(2)}, u32[]{:S(2)}) collective-permute-start(bf16[4,10,1,1024]{3,2,1,0:T(2,128)(2,1)S(1)} %get-tuple-element.74), channel_id=1, source_target_pairs={{0,1},{1,2},{2,3},{3,4},{4,5},{5,6},{6,7},{8,9},{9,10},{10,11},{11... | collective-permute-start | bytes 245768 | tf_op jit(solution)/shard_map/ppermute | solution.py:16
  370.7 23.2 %collective-permute-start.19 = (bf16[4,10,1,1024]{3,2,1,0:T(2,128)(2,1)S(1)}, bf16[4,10,1,1024]{3,2,1,0:T(2,128)(2,1)S(1)}, u32[]{:S(2)}, u32[]{:S(2)}) collective-permute-start(bf16[4,10,1,1024]{3,2,1,0:T(2,128)(2,1)S(1)} %get-tuple-element.73), channel_id=1, source_target_pairs={{1,0},{2,1},{3,2},{4,3},{5,4},{6,5},{7,6},{9,8},{10,9},{11,10},{12... | collective-permute-start | bytes 245768 | tf_op jit(solution)/shard_map/ppermute | solution.py:17
  372.2 24.5 %collective-permute-start.18 = (bf16[4,10,1,1024]{3,2,1,0:T(2,128)(2,1)S(1)}, bf16[4,10,1,1024]{3,2,1,0:T(2,128)(2,1)S(1)}, u32[]{:S(2)}, u32[]{:S(2)}) collective-permute-start(bf16[4,10,1,1024]{3,2,1,0:T(2,128)(2,1)S(1)} %get-tuple-element.72), channel_id=1, source_target_pairs={{0,1},{1,2},{2,3},{3,4},{4,5},{5,6},{6,7},{8,9},{9,10},{10,11},{11... | collective-permute-start | bytes 245768 | tf_op jit(solution)/shard_map/ppermute | solution.py:16
  375.3 49.8 %collective-permute-start.31 = (bf16[4,10,1,1024]{3,2,1,0:T(2,128)(2,1)S(1)}, bf16[4,10,1,1024]{3,2,1,0:T(2,128)(2,1)S(1)}, u32[]{:S(2)}, u32[]{:S(2)}) collective-permute-start(bf16[4,10,1,1024]{3,2,1,0:T(2,128)(2,1)S(1)} %get-tuple-element.71), channel_id=1, source_target_pairs={{1,0},{2,1},{3,2},{4,3},{5,4},{6,5},{7,6},{9,8},{10,9},{11,10},{12... | collective-permute-start | bytes 245768 | tf_op jit(solution)/shard_map/ppermute | solution.py:17
  377.8 8.1 %collective-permute-start.3 = (f32[4,10,1,1024]{3,2,1,0:T(1,128)S(1)}, f32[4,10,1,1024]{3,2,1,0:T(1,128)S(1)}, u32[]{:S(2)}, u32[]{:S(2)}) collective-permute-start(f32[4,10,1,1024]{3,2,1,0:T(1,128)S(1)} %get-tuple-element.47), channel_id=1, source_target_pairs={{0,1},{1,2},{2,3},{3,4},{4,5},{5,6},{6,7},{8,9},{9,10},{10,11},{11... | collective-permute-start | bytes 491528 | tf_op jit(solution)/shard_map/ppermute | solution.py:16
  381.6 8.7 %collective-permute-start.2 = (f32[4,10,1,1024]{3,2,1,0:T(1,128)S(1)}, f32[4,10,1,1024]{3,2,1,0:T(1,128)S(1)}, u32[]{:S(2)}, u32[]{:S(2)}) collective-permute-start(f32[4,10,1,1024]{3,2,1,0:T(1,128)S(1)} %get-tuple-element.46), channel_id=1, source_target_pairs={{1,0},{2,1},{3,2},{4,3},{5,4},{6,5},{7,6},{9,8},{10,9},{11,10},{12... | collective-permute-start | bytes 491528 | tf_op jit(solution)/shard_map/ppermute | solution.py:17
  385.9 7.7 %copy-start.1 = (f32[8,8,1024]{2,1,0:T(8,128)S(1)}, f32[8,8,1024]{2,1,0:T(8,128)}, u32[]{:S(2)}) copy-start(f32[8,8,1024]{2,1,0:T(8,128)} %param.8) | copy-start | bytes 786436
  385.9 7.7 %copy-start.4 = (f32[8,8,1024]{2,1,0:T(8,128)S(1)}, f32[8,8,1024]{2,1,0:T(8,128)}, u32[]{:S(2)}) copy-start(f32[8,8,1024]{2,1,0:T(8,128)} %reshape.127) | copy-start | bytes 786436
  385.9 40.5 %collective-permute-start.30 = (bf16[4,10,1,1024]{3,2,1,0:T(2,128)(2,1)S(1)}, bf16[4,10,1,1024]{3,2,1,0:T(2,128)(2,1)S(1)}, u32[]{:S(2)}, u32[]{:S(2)}) collective-permute-start(bf16[4,10,1,1024]{3,2,1,0:T(2,128)(2,1)S(1)} %get-tuple-element.70), channel_id=1, source_target_pairs={{0,1},{1,2},{2,3},{3,4},{4,5},{5,6},{6,7},{8,9},{9,10},{10,11},{11... | collective-permute-start | bytes 245768 | tf_op jit(solution)/shard_map/ppermute | solution.py:16
  390.3 54.7 %collective-permute-start.43 = (bf16[4,10,1,1024]{3,2,1,0:T(2,128)(2,1)S(1)}, bf16[4,10,1,1024]{3,2,1,0:T(2,128)(2,1)S(1)}, u32[]{:S(2)}, u32[]{:S(2)}) collective-permute-start(bf16[4,10,1,1024]{3,2,1,0:T(2,128)(2,1)S(1)} %get-tuple-element.69), channel_id=1, source_target_pairs={{1,0},{2,1},{3,2},{4,3},{5,4},{6,5},{7,6},{9,8},{10,9},{11,10},{12... | collective-permute-start | bytes 245768 | tf_op jit(solution)/shard_map/ppermute | solution.py:17
  393.9 5.7 %collective-permute-start.9 = (f32[1,8,1024]{2,1,0:T(8,128)S(1)}, f32[1,8,1024]{2,1,0:T(8,128)S(1)}, u32[]{:S(2)}, u32[]{:S(2)}) collective-permute-start(f32[1,8,1024]{2,1,0:T(8,128)S(1)} %get-tuple-element.110), channel_id=1, source_target_pairs={{0,8},{8,16},{16,24},{24,32},{32,40},{40,48},{48,56},{1,9},{9,17},... | collective-permute-start | bytes 98312 | tf_op jit(solution)/shard_map/ppermute | solution.py:16
  396.7 5.8 %collective-permute-start.8 = (f32[1,8,1024]{2,1,0:T(8,128)S(1)}, f32[1,8,1024]{2,1,0:T(8,128)S(1)}, u32[]{:S(2)}, u32[]{:S(2)}) collective-permute-start(f32[1,8,1024]{2,1,0:T(8,128)S(1)} %get-tuple-element.111), channel_id=1, source_target_pairs={{8,0},{16,8},{24,16},{32,24},{40,32},{48,40},{56,48},{9,1},{17,9},... | collective-permute-start | bytes 98312 | tf_op jit(solution)/shard_map/ppermute | solution.py:17
  402.6 4.8 collective-permute-start.11
  405.4 5.8 %collective-permute-start.10 = (f32[10,1,1024]{2,1,0:T(1,128)S(1)}, f32[10,1,1024]{2,1,0:T(1,128)S(1)}, u32[]{:S(2)}, u32[]{:S(2)}) collective-permute-start(f32[10,1,1024]{2,1,0:T(1,128)S(1)} %get-tuple-element.98), channel_id=1, source_target_pairs={{1,0},{2,1},{3,2},{4,3},{5,4},{6,5},{7,6},{9,8},{10,9},{11,10},{12... | collective-permute-start | bytes 122888 | tf_op jit(solution)/shard_map/ppermute | solution.py:17
  412.0 5.3 collective-permute-start.13
  414.8 6.9 %collective-permute-start.12 = (f32[4,1,8,1024]{3,2,1,0:T(8,128)S(1)}, f32[4,1,8,1024]{3,2,1,0:T(8,128)S(1)}, u32[]{:S(2)}, u32[]{:S(2)}) collective-permute-start(f32[4,1,8,1024]{3,2,1,0:T(8,128)S(1)} %get-tuple-element.62), channel_id=1, source_target_pairs={{8,0},{16,8},{24,16},{32,24},{40,32},{48,40},{56,48},{9,1},{17,9},... | collective-permute-start | bytes 393224 | tf_op jit(solution)/shard_map/ppermute | solution.py:17
  417.3 27.8 %collective-permute-start.42 = (bf16[4,10,1,1024]{3,2,1,0:T(2,128)(2,1)S(1)}, bf16[4,10,1,1024]{3,2,1,0:T(2,128)(2,1)S(1)}, u32[]{:S(2)}, u32[]{:S(2)}) collective-permute-start(bf16[4,10,1,1024]{3,2,1,0:T(2,128)(2,1)S(1)} %get-tuple-element.68), channel_id=1, source_target_pairs={{0,1},{1,2},{2,3},{3,4},{4,5},{5,6},{6,7},{8,9},{9,10},{10,11},{11... | collective-permute-start | bytes 245768 | tf_op jit(solution)/shard_map/ppermute | solution.py:16
  421.9 5.2 collective-permute-start.15
  425.1 4.2 collective-permute-start.14
  427.1 3.3 copy-start.3
  430.7 4.8 collective-permute-start.21
  433.5 5.8 %collective-permute-start.20 = (f32[1,8,1024]{2,1,0:T(8,128)S(1)}, f32[1,8,1024]{2,1,0:T(8,128)S(1)}, u32[]{:S(2)}, u32[]{:S(2)}) collective-permute-start(f32[1,8,1024]{2,1,0:T(8,128)S(1)} %get-tuple-element.108), channel_id=1, source_target_pairs={{8,0},{16,8},{24,16},{32,24},{40,32},{48,40},{56,48},{9,1},{17,9},... | collective-permute-start | bytes 98312 | tf_op jit(solution)/shard_map/ppermute | solution.py:17
  439.4 6.3 %collective-permute-start.23 = (f32[10,1,1024]{2,1,0:T(1,128)S(1)}, f32[10,1,1024]{2,1,0:T(1,128)S(1)}, u32[]{:S(2)}, u32[]{:S(2)}) collective-permute-start(f32[10,1,1024]{2,1,0:T(1,128)S(1)} %get-tuple-element.95), channel_id=1, source_target_pairs={{0,1},{1,2},{2,3},{3,4},{4,5},{5,6},{6,7},{8,9},{9,10},{10,11},{11... | collective-permute-start | bytes 122888 | tf_op jit(solution)/shard_map/ppermute | solution.py:16
  443.7 3.9 collective-permute-start.22
  448.3 5.3 collective-permute-start.25
  451.2 6.9 %collective-permute-start.24 = (f32[4,1,8,1024]{3,2,1,0:T(8,128)S(1)}, f32[4,1,8,1024]{3,2,1,0:T(8,128)S(1)}, u32[]{:S(2)}, u32[]{:S(2)}) collective-permute-start(f32[4,1,8,1024]{3,2,1,0:T(8,128)S(1)} %get-tuple-element.57), channel_id=1, source_target_pairs={{8,0},{16,8},{24,16},{32,24},{40,32},{48,40},{56,48},{9,1},{17,9},... | collective-permute-start | bytes 393224 | tf_op jit(solution)/shard_map/ppermute | solution.py:17
  458.2 6.0 %collective-permute-start.27 = (f32[4,10,1,1024]{3,2,1,0:T(1,128)S(1)}, f32[4,10,1,1024]{3,2,1,0:T(1,128)S(1)}, u32[]{:S(2)}, u32[]{:S(2)}) collective-permute-start(f32[4,10,1,1024]{3,2,1,0:T(1,128)S(1)} %get-tuple-element.39), channel_id=1, source_target_pairs={{0,1},{1,2},{2,3},{3,4},{4,5},{5,6},{6,7},{8,9},{9,10},{10,11},{11... | collective-permute-start | bytes 491528 | tf_op jit(solution)/shard_map/ppermute | solution.py:16
  461.4 4.2 collective-permute-start.26
  464.2 2.6 copy-start.2
  467.1 4.5 collective-permute-start.33
  470.0 5.8 %collective-permute-start.32 = (f32[1,8,1024]{2,1,0:T(8,128)S(1)}, f32[1,8,1024]{2,1,0:T(8,128)S(1)}, u32[]{:S(2)}, u32[]{:S(2)}) collective-permute-start(f32[1,8,1024]{2,1,0:T(8,128)S(1)} %get-tuple-element.105), channel_id=1, source_target_pairs={{8,0},{16,8},{24,16},{32,24},{40,32},{48,40},{56,48},{9,1},{17,9},... | collective-permute-start | bytes 98312 | tf_op jit(solution)/shard_map/ppermute | solution.py:17
  475.8 5.8 %collective-permute-start.35 = (f32[10,1,1024]{2,1,0:T(1,128)S(1)}, f32[10,1,1024]{2,1,0:T(1,128)S(1)}, u32[]{:S(2)}, u32[]{:S(2)}) collective-permute-start(f32[10,1,1024]{2,1,0:T(1,128)S(1)} %get-tuple-element.91), channel_id=1, source_target_pairs={{0,1},{1,2},{2,3},{3,4},{4,5},{5,6},{6,7},{8,9},{9,10},{10,11},{11... | collective-permute-start | bytes 122888 | tf_op jit(solution)/shard_map/ppermute | solution.py:16
  480.2 3.9 collective-permute-start.34
  484.8 5.3 collective-permute-start.37
  487.6 6.9 %collective-permute-start.36 = (f32[4,1,8,1024]{3,2,1,0:T(8,128)S(1)}, f32[4,1,8,1024]{3,2,1,0:T(8,128)S(1)}, u32[]{:S(2)}, u32[]{:S(2)}) collective-permute-start(f32[4,1,8,1024]{3,2,1,0:T(8,128)S(1)} %get-tuple-element.52), channel_id=1, source_target_pairs={{8,0},{16,8},{24,16},{32,24},{40,32},{48,40},{56,48},{9,1},{17,9},... | collective-permute-start | bytes 393224 | tf_op jit(solution)/shard_map/ppermute | solution.py:17
  494.7 4.7 collective-permute-start.39
  497.9 5.1 collective-permute-start.38
  504.4 4.2 collective-permute-start.45
  506.9 5.8 %collective-permute-start.44 = (f32[1,8,1024]{2,1,0:T(8,128)S(1)}, f32[1,8,1024]{2,1,0:T(8,128)S(1)}, u32[]{:S(2)}, u32[]{:S(2)}) collective-permute-start(f32[1,8,1024]{2,1,0:T(8,128)S(1)} %get-tuple-element.102), channel_id=1, source_target_pairs={{8,0},{16,8},{24,16},{32,24},{40,32},{48,40},{56,48},{9,1},{17,9},... | collective-permute-start | bytes 98312 | tf_op jit(solution)/shard_map/ppermute | solution.py:17
  512.8 5.8 %collective-permute-start.47 = (f32[10,1,1024]{2,1,0:T(1,128)S(1)}, f32[10,1,1024]{2,1,0:T(1,128)S(1)}, u32[]{:S(2)}, u32[]{:S(2)}) collective-permute-start(f32[10,1,1024]{2,1,0:T(1,128)S(1)} %get-tuple-element.87), channel_id=1, source_target_pairs={{0,1},{1,2},{2,3},{3,4},{4,5},{5,6},{6,7},{8,9},{9,10},{10,11},{11... | collective-permute-start | bytes 122888 | tf_op jit(solution)/shard_map/ppermute | solution.py:16
  517.1 3.9 collective-permute-start.46
Sparse Core Ops, SparseCore 0:
  523.8 24.7 reduce-scatter.1
where the time goes:
time: 559 us; the launch traced here: 555 us
  blocking collectives  284 us (51%)
  starting transfers between devices  114 us (20%)
  waiting for transfers between devices  68.4 us (12%)
  other arithmetic  40 us (7%)
  local copies, waits for them, and re-layouts  33.9 us (6%)
  between operations  15.8 us (3%)
    psum x1, blocking collectives, shards(): samples = lax.psum(local_samples, ('gx', 'gy'))  284 us
    ppermute x24, starting transfers between devices, extended(): before = lax.ppermute(last, axis, up)  82.2 us
    ppermute x24, waiting for transfers between devices, extended(): after = lax.ppermute(initial, axis, down)  42.3 us
    ppermute x24, starting transfers between devices, extended(): after = lax.ppermute(initial, axis, down)  31.4 us
    reduce_scatter x1, waiting for transfers between devices, shards(): lax.psum_scatter(kernel_local, 'pair', scatter_dimension=3, tiled=True)  23.9 us
    slice x2, local copies, waits for them, and re-layouts, shards(): pressure_snaps = forward_field[:, 0].reshape(steps_total, -1)  14.9 us
  transfers between devices with their start and end apart: 49, of which 18 were waited for; matrix products, arithmetic and copies ran while one was open for 12% of the time, Pallas kernels for 0%

commit v1 on v0

v1 whole, which is shorter than its diff:
```python
import jax
import jax.numpy as jnp
from jax import lax
from jax.sharding import PartitionSpec as P

step_length = 0.25


def neighbours(shard, axis, dim):
    size, length = (lax.axis_size(axis), shard.shape[dim])
    up = [(i, i + 1) for i in range(size - 1)]
    down = [(i + 1, i) for i in range(size - 1)]
    last = lax.slice_in_dim(shard, length - 1, length, axis=dim)
    first = lax.slice_in_dim(shard, 0, 1, axis=dim)
    before = lax.ppermute(last, axis, up)
    after = lax.ppermute(first, axis, down)
    return (before, after)


def halos(shard, dim_x, dim_y):
    return (neighbours(shard, "gx", dim_x), neighbours(shard, "gy", dim_y))


def central(field, rims):
    (west, east), (south, north) = rims
    dims = field.ndim
    x_hi = jnp.concatenate([lax.slice_in_dim(field, 1, field.shape[-3], axis=dims - 3), east], axis=dims - 3)
    x_lo = jnp.concatenate([west, lax.slice_in_dim(field, 0, field.shape[-3] - 1, axis=dims - 3)], axis=dims - 3)
    y_hi = jnp.concatenate([lax.slice_in_dim(field, 1, field.shape[-2], axis=dims - 2), north], axis=dims - 2)
    y_lo = jnp.concatenate([south, lax.slice_in_dim(field, 0, field.shape[-2] - 1, axis=dims - 2)], axis=dims - 2)
    east_diff = (x_hi - x_lo) * 0.5
    north_diff = (y_hi - y_lo) * 0.5
    vertical = jnp.pad(field, [(0, 0)] * (dims - 1) + [(1, 1)])
    up_diff = (vertical[..., 2:] - vertical[..., :-2]) * 0.5
    return (east_diff, north_diff, up_diff)


def local_cells(cells, width_x, width_y):
    local_x = cells[:, 0] - lax.axis_index("gx") * width_x
    local_y = cells[:, 1] - lax.axis_index("gy") * width_y
    inside = (local_x >= 0) & (local_x < width_x) & (local_y >= 0) & (local_y < width_y)
    return (
        jnp.clip(local_x, 0, width_x - 1),
        jnp.clip(local_y, 0, width_y - 1),
        cells[:, 2],
        inside.astype(jnp.float32),
    )


def shards(
    sound_speed_sq,
    wind_profile,
    forward_field,
    adjoint_state,
    pair_counts,
    source_cells,
    receiver_cells,
    residuals,
):
    steps_total = forward_field.shape[0]
    width_x, width_y, depth = sound_speed_sq.shape
    slots = residuals.shape[0]
    east_wind = wind_profile[0]
    north_wind = wind_profile[1]
    vertical_wind = wind_profile[2]
    live = (jnp.arange(slots, dtype=jnp.int32) < pair_counts[0]).astype(jnp.float32)
    sx, sy, sz, src_inside = local_cells(source_cells, width_x, width_y)
    rx, ry, rz, rcv_inside = local_cells(receiver_cells, width_x, width_y)
    local_samples = jnp.stack(
        [forward_field[t, 0][sx, sy, sz] for t in range(steps_total)]
    ).astype(jnp.float32) * src_inside[None, :]
    me = lax.axis_index("pair")
    slot = jnp.zeros((lax.axis_size("pair"),) + local_samples.shape, jnp.float32)
    samples = lax.psum(slot.at[me].set(local_samples), ("pair", "gx", "gy"))[me]
    forward_rims = halos(forward_field, 2, 3)
    rcv_flat = (rx * width_y + ry) * depth + rz
    state = adjoint_state[0]
    kernel_local = jnp.zeros((4, width_x, width_y, depth), jnp.float32)
    for step in range(steps_total):
        snap = steps_total - 1 - step
        amplitude = residuals[:, snap] * samples[snap] * live * rcv_inside
        injected = (
            jnp.zeros((width_x * width_y * depth,), jnp.float32)
            .at[rcv_flat]
            .add(amplitude)
            .reshape(width_x, width_y, depth)
        )
        east_diff, north_diff, up_diff = central(state, halos(state, 1, 2))
        pressure = state[0]
        velocity = state[1:]
        divergence = east_diff[1] + north_diff[2] + up_diff[3]
        p_new = (
            pressure
            + step_length
            * (
                sound_speed_sq * divergence
                + east_wind * east_diff[0]
                + north_wind * north_diff[0]
                + vertical_wind * up_diff[0]
            )
            + injected
        )
        p_east, p_north, p_up = central(p_new, halos(p_new, 0, 1))
        gradient = jnp.stack([p_east, p_north, p_up])
        a_new = velocity + step_length * (
            gradient
            + east_wind * east_diff[1:]
            + north_wind * north_diff[1:]
            + vertical_wind * up_diff[1:]
        )
        forward = forward_field[snap].astype(jnp.float32)
        rims = tuple(
            tuple(side[snap].astype(jnp.float32) for side in pair) for pair in forward_rims
        )
        f_east, f_north, f_up = central(forward, rims)
        pieces = [p_new * (f_east[1] + f_north[2] + f_up[3])]
        for along in (f_east, f_north, f_up):
            pieces.append(
                p_new * along[0] + a_new[0] * along[1] + a_new[1] * along[2] + a_new[2] * along[3]
            )
        increment = jnp.stack(pieces)
        kernel_local = kernel_local + increment
        state = jnp.concatenate([p_new[None], a_new], axis=0)
    kernels = lax.psum_scatter(kernel_local, "pair", scatter_dimension=3, tiled=True)
    return (kernels, state[None])


def solution(mesh):
    in_specs = (
        P("gx", "gy", None),
        P(),
        P(None, None, "gx", "gy", None),
        P("pair", None, "gx", "gy", None),
        P("pair"),
        P("pair", None),
        P("pair", None),
        P("pair", None),
    )
    out_specs = (P(None, "gx", "gy", "pair"), P("pair", None, "gx", "gy", None))
    return jax.shard_map(shards, mesh=mesh, in_specs=in_specs, out_specs=out_specs, check_vma=False)
```

time: 559 us -> 316 us (0.57)
  blocking collectives: 284 us -> 67.6 us
  waiting for transfers between devices: 68.4 us -> 43.3 us
  starting transfers between devices: 114 us -> 104 us
  local copies, waits for them, and re-layouts: 33.9 us -> 42.6 us
    psum x1, blocking collectives: 284 us -> 67.6 us  [shards(): samples = lax.psum(slot.at[me].set(local_samples), ('pair', 'gx', 'gy'))[me]]
    ppermute x48 -> x36, waiting for transfers between devices: 44.5 us -> 12 us  [the longest x18 11.1 us: neighbours(): before = lax.ppermute(last, axis, up)]
    unnamed x16 -> x73, local copies, waits for them, and re-layouts: 0.04 us -> 11.4 us
    ppermute x48 -> x36, starting transfers between devices: 114 us -> 104 us  [the longest x18 80.3 us: neighbours(): before = lax.ppermute(last, axis, up)]
    reduce_scatter x1, waiting for transfers between devices: 23.9 us -> 31.3 us  [shards(): lax.psum_scatter(kernel_local, 'pair', scatter_dimension=3, tiled=True)]
    gather x1 -> x4, local copies, waits for them, and re-layouts: 8.65 us -> 11.3 us  [shards(): forward_field[t, 0][sx, sy, sz]]
    slice x11 -> x17, local copies, waits for them, and re-layouts: 18.3 us -> 17.5 us  [the longest x11 6.16 us: neighbours(): last = lax.slice_in_dim(shard, length - 1, length, axis=dim)]
  transfers between devices with their start and end apart: 49 -> 37, of which waited for: 18 -> 11; matrix products, arithmetic and copies ran while one was open for 12% -> 19% of each run, Pallas kernels for 0% -> 0%
where the time goes in v1:
time: 316 us; the launch traced here: 313 us
  starting transfers between devices  104 us (33%)
  blocking collectives  67.6 us (21%)
  waiting for transfers between devices  43.3 us (14%)
  local copies, waits for them, and re-layouts  42.6 us (13%)
  other arithmetic  39.7 us (13%)
  between operations  16.1 us (5%)
    ppermute x18, starting transfers between devices, neighbours(): before = lax.ppermute(last, axis, up)  80.3 us
    psum x1, blocking collectives, shards(): samples = lax.psum(slot.at[me].set(local_samples), ('pair', 'gx', 'gy'))[me]  67.6 us
    reduce_scatter x1, waiting for transfers between devices, shards(): lax.psum_scatter(kernel_local, 'pair', scatter_dimension=3, tiled=True)  31.3 us
    ppermute x18, starting transfers between devices, neighbours(): after = lax.ppermute(first, axis, down)  23.7 us
    unnamed x73, local copies, waits for them, and re-layouts  11.4 us
    gather x4, local copies, waits for them, and re-layouts, shards(): forward_field[t, 0][sx, sy, sz]  11.3 us
    ppermute x18, waiting for transfers between devices, neighbours(): before = lax.ppermute(last, axis, up)  11.1 us
    scatter-add x4, other arithmetic, shards(): injected = jnp.zeros((width_x * width_y * depth,), jnp.float32).at[rcv_fl...  8.57 us
  transfers between devices with their start and end apart: 37, of which 11 were waited for; matrix products, arithmetic and copies ran while one was open for 19% of the time, Pallas kernels for 0%

profile of v1, /device:TPU:0, one launch (start us, length us, event | category | flops | bytes accessed | tf_op | source)
XLA Modules:
  0.0 313.5 jit_solution(12173777314110619622)
XLA Ops:
  7.2 2.1 slice_bitcast_fusion.32
  9.3 1.4 collective-permute-start.4
  10.7 5.3 %collective-permute-start.5 = (bf16[4,4,1,8,1024]{4,3,1,2,0:T(8,128)(2,1)}, bf16[4,4,1,8,1024]{4,3,1,2,0:T(8,128)(2,1)}, u32[]{:S(2)}, u32[]{:S(2)}) collective-permute-start(bf16[4,4,1,8,1024]{4,3,1,2,0:T(8,128)(2,1)} %get-tuple-element.30), channel_id=1, source_target_pairs={{0,8},{8,16},{16,24},{24,32},{32,40},{40,48},{48,56},{1,9},{9,17},... | collective-permute-start | bytes 786440 | tf_op jit(solution)/shard_map/ppermute | solution.py:15
  16.0 4.4 %fusion.266 = (bf16[4,4,8,1,1024]{4,3,2,1,0:T(2,128)(2,1)}, bf16[4,4,8,1,1024]{4,3,2,1,0:T(2,128)(2,1)}) fusion(bf16[4,4,8,8,1024]{4,3,2,1,0:T(8,128)(2,1)} %param.12), kind=kLoop, calls=%fused_computation.506 | loop fusion | bytes 1048576 | tf_op jit(solution)/shard_map/slice | solution.py:13
  23.8 4.3 %collective-permute-start.3 = (f32[4,8,1,1024]{3,2,1,0:T(1,128)}, f32[4,8,1,1024]{3,2,1,0:T(1,128)}, u32[]{:S(2)}, u32[]{:S(2)}) collective-permute-start(f32[4,8,1,1024]{3,2,1,0:T(1,128)} %get-tuple-element.82), channel_id=1, source_target_pairs={{0,1},{1,2},{2,3},{3,4},{4,5},{5,6},{6,7},{8,9},{9,10},{10,11},{11... | collective-permute-start | bytes 393224 | tf_op jit(solution)/shard_map/ppermute | solution.py:15
  28.6 2.5 fusion.1
  31.1 2.0 fusion.271
  33.0 2.2 fusion.272
  35.3 1.8 slice_bitcast_fusion.53
  37.1 1.6 fusion.276
  39.4 1.5 fusion.274
  40.9 1.6 fusion.7
  42.5 1.6 fusion.11
  44.1 2.0 fusion.267
  46.1 2.2 fusion.268
  48.3 2.9 gather_fusion.3
  51.2 2.8 gather_fusion.2
  54.0 2.8 gather_fusion.1
  56.9 2.8 gather_fusion
  61.2 67.6 %psum.7 = f32[2,4,256]{2,1,0:T(4,128)S(1)} all-reduce(f32[2,4,256]{2,1,0:T(4,128)S(1)} %select_dynamic-update-slice_fusion), channel_id=1, replica_groups=mesh['pair'=2,'gx'=8,'gy'=8] {'pair','gx','gy'}, use_global_device_ids=true, to_apply=%region_1.2 | all-reduce | flops 2048 | bytes 16384 | tf_op jit(solution)/shard_map/psum | solution.py:74
  129.5 2.3 scatter_custom_fusion
  131.9 2.1 scatter_custom_fusion.1
  134.0 2.1 scatter_custom_fusion.2
  136.2 2.1 scatter_custom_fusion.3
  139.0 1.3 collective-permute-start
  140.3 4.6 %collective-permute-start.1 = (f32[4,1,8,1024]{3,2,1,0:T(8,128)S(1)}, f32[4,1,8,1024]{3,2,1,0:T(8,128)S(1)}, u32[]{:S(2)}, u32[]{:S(2)}) collective-permute-start(f32[4,1,8,1024]{3,2,1,0:T(8,128)S(1)} %copy-done.30), channel_id=1, source_target_pairs={{0,8},{8,16},{16,24},{24,32},{32,40},{40,48},{48,56},{1,9},{9,17},... | collective-permute-start | bytes 393224 | tf_op jit(solution)/shard_map/ppermute | solution.py:15
  144.9 1.6 fusion.23
  146.5 1.3 collective-permute-start.7
  150.5 1.8 fusion.231
  154.9 1.4 collective-permute-start.10
  156.3 4.9 %collective-permute-start.11 = (f32[8,1,1024]{2,1,0:T(1,128)S(1)}, f32[8,1,1024]{2,1,0:T(1,128)S(1)}, u32[]{:S(2)}, u32[]{:S(2)}) collective-permute-start(f32[8,1,1024]{2,1,0:T(1,128)S(1)} %get-tuple-element.134), channel_id=1, source_target_pairs={{0,1},{1,2},{2,3},{3,4},{4,5},{5,6},{6,7},{8,9},{9,10},{10,11},{11... | collective-permute-start | bytes 98312 | tf_op jit(solution)/shard_map/ppermute | solution.py:15
  169.5 1.3 collective-permute-start.8
  170.8 4.9 %collective-permute-start.9 = (f32[1,8,1024]{2,1,0:T(8,128)S(1)}, f32[1,8,1024]{2,1,0:T(8,128)S(1)}, u32[]{:S(2)}, u32[]{:S(2)}) collective-permute-start(f32[1,8,1024]{2,1,0:T(8,128)S(1)} %get-tuple-element.130), channel_id=1, source_target_pairs={{0,8},{8,16},{16,24},{24,32},{32,40},{40,48},{48,56},{1,9},{9,17},... | collective-permute-start | bytes 98312 | tf_op jit(solution)/shard_map/ppermute | solution.py:15
  175.9 1.4 collective-permute-done.9
  178.9 1.5 collective-permute-start.14
  180.4 4.2 %collective-permute-start.15 = (f32[4,8,1,1024]{3,2,1,0:T(1,128)S(1)}, f32[4,8,1,1024]{3,2,1,0:T(1,128)S(1)}, u32[]{:S(2)}, u32[]{:S(2)}) collective-permute-start(f32[4,8,1,1024]{3,2,1,0:T(1,128)S(1)} %get-tuple-element.68), channel_id=1, source_target_pairs={{0,1},{1,2},{2,3},{3,4},{4,5},{5,6},{6,7},{8,9},{9,10},{10,11},{11... | collective-permute-start | bytes 393224 | tf_op jit(solution)/shard_map/ppermute | solution.py:15
  184.6 1.3 collective-permute-start.12
  185.9 5.2 %collective-permute-start.13 = (f32[4,1,8,1024]{3,2,1,0:T(8,128)S(1)}, f32[4,1,8,1024]{3,2,1,0:T(8,128)S(1)}, u32[]{:S(2)}, u32[]{:S(2)}) collective-permute-start(f32[4,1,8,1024]{3,2,1,0:T(8,128)S(1)} %get-tuple-element.64), channel_id=1, source_target_pairs={{0,8},{8,16},{16,24},{24,32},{32,40},{40,48},{48,56},{1,9},{9,17},... | collective-permute-start | bytes 393224 | tf_op jit(solution)/shard_map/ppermute | solution.py:15
  192.4 1.8 collective-permute-done.13
  195.9 1.3 collective-permute-start.18
  197.2 3.4 %collective-permute-start.19 = (f32[8,1,1024]{2,1,0:T(1,128)S(1)}, f32[8,1,1024]{2,1,0:T(1,128)S(1)}, u32[]{:S(2)}, u32[]{:S(2)}) collective-permute-start(f32[8,1,1024]{2,1,0:T(1,128)S(1)} %get-tuple-element.126), channel_id=1, source_target_pairs={{0,1},{1,2},{2,3},{3,4},{4,5},{5,6},{6,7},{8,9},{9,10},{10,11},{11... | collective-permute-start | bytes 98312 | tf_op jit(solution)/shard_map/ppermute | solution.py:15
  200.8 1.3 collective-permute-start.16
  202.1 5.5 %collective-permute-start.17 = (f32[1,8,1024]{2,1,0:T(8,128)S(1)}, f32[1,8,1024]{2,1,0:T(8,128)S(1)}, u32[]{:S(2)}, u32[]{:S(2)}) collective-permute-start(f32[1,8,1024]{2,1,0:T(8,128)S(1)} %get-tuple-element.122), channel_id=1, source_target_pairs={{0,8},{8,16},{16,24},{24,32},{32,40},{40,48},{48,56},{1,9},{9,17},... | collective-permute-start | bytes 98312 | tf_op jit(solution)/shard_map/ppermute | solution.py:15
  207.7 1.4 collective-permute-done.17
  210.8 1.3 collective-permute-start.22
  212.1 3.6 %collective-permute-start.23 = (f32[4,8,1,1024]{3,2,1,0:T(1,128)S(1)}, f32[4,8,1,1024]{3,2,1,0:T(1,128)S(1)}, u32[]{:S(2)}, u32[]{:S(2)}) collective-permute-start(f32[4,8,1,1024]{3,2,1,0:T(1,128)S(1)} %get-tuple-element.54), channel_id=1, source_target_pairs={{0,1},{1,2},{2,3},{3,4},{4,5},{5,6},{6,7},{8,9},{9,10},{10,11},{11... | collective-permute-start | bytes 393224 | tf_op jit(solution)/shard_map/ppermute | solution.py:15
  215.7 1.3 collective-permute-start.20
  217.0 5.9 %collective-permute-start.21 = (f32[4,1,8,1024]{3,2,1,0:T(8,128)S(1)}, f32[4,1,8,1024]{3,2,1,0:T(8,128)S(1)}, u32[]{:S(2)}, u32[]{:S(2)}) collective-permute-start(f32[4,1,8,1024]{3,2,1,0:T(8,128)S(1)} %get-tuple-element.50), channel_id=1, source_target_pairs={{0,8},{8,16},{16,24},{24,32},{32,40},{40,48},{48,56},{1,9},{9,17},... | collective-permute-start | bytes 393224 | tf_op jit(solution)/shard_map/ppermute | solution.py:15
  224.3 1.8 collective-permute-done.21
  227.7 1.3 collective-permute-start.26
  229.0 3.4 %collective-permute-start.27 = (f32[8,1,1024]{2,1,0:T(1,128)S(1)}, f32[8,1,1024]{2,1,0:T(1,128)S(1)}, u32[]{:S(2)}, u32[]{:S(2)}) collective-permute-start(f32[8,1,1024]{2,1,0:T(1,128)S(1)} %get-tuple-element.118), channel_id=1, source_target_pairs={{0,1},{1,2},{2,3},{3,4},{4,5},{5,6},{6,7},{8,9},{9,10},{10,11},{11... | collective-permute-start | bytes 98312 | tf_op jit(solution)/shard_map/ppermute | solution.py:15
  232.6 1.3 collective-permute-start.24
  233.9 5.5 %collective-permute-start.25 = (f32[1,8,1024]{2,1,0:T(8,128)S(1)}, f32[1,8,1024]{2,1,0:T(8,128)S(1)}, u32[]{:S(2)}, u32[]{:S(2)}) collective-permute-start(f32[1,8,1024]{2,1,0:T(8,128)S(1)} %get-tuple-element.114), channel_id=1, source_target_pairs={{0,8},{8,16},{16,24},{24,32},{32,40},{40,48},{48,56},{1,9},{9,17},... | collective-permute-start | bytes 98312 | tf_op jit(solution)/shard_map/ppermute | solution.py:15
  239.5 1.4 collective-permute-done.25
  242.6 1.3 collective-permute-start.30
  243.9 3.7 %collective-permute-start.31 = (f32[4,8,1,1024]{3,2,1,0:T(1,128)S(1)}, f32[4,8,1,1024]{3,2,1,0:T(1,128)S(1)}, u32[]{:S(2)}, u32[]{:S(2)}) collective-permute-start(f32[4,8,1,1024]{3,2,1,0:T(1,128)S(1)} %get-tuple-element.40), channel_id=1, source_target_pairs={{0,1},{1,2},{2,3},{3,4},{4,5},{5,6},{6,7},{8,9},{9,10},{10,11},{11... | collective-permute-start | bytes 393224 | tf_op jit(solution)/shard_map/ppermute | solution.py:15
  248.9 5.9 %collective-permute-start.29 = (f32[4,1,8,1024]{3,2,1,0:T(8,128)S(1)}, f32[4,1,8,1024]{3,2,1,0:T(8,128)S(1)}, u32[]{:S(2)}, u32[]{:S(2)}) collective-permute-start(f32[4,1,8,1024]{3,2,1,0:T(8,128)S(1)} %get-tuple-element.36), channel_id=1, source_target_pairs={{0,8},{8,16},{16,24},{24,32},{32,40},{40,48},{48,56},{1,9},{9,17},... | collective-permute-start | bytes 393224 | tf_op jit(solution)/shard_map/ppermute | solution.py:15
  256.2 1.8 collective-permute-done.29
  258.7 1.3 collective-permute-start.34
  260.0 3.4 %collective-permute-start.35 = (f32[8,1,1024]{2,1,0:T(1,128)S(1)}, f32[8,1,1024]{2,1,0:T(1,128)S(1)}, u32[]{:S(2)}, u32[]{:S(2)}) collective-permute-start(f32[8,1,1024]{2,1,0:T(1,128)S(1)} %get-tuple-element.102), channel_id=1, source_target_pairs={{0,1},{1,2},{2,3},{3,4},{4,5},{5,6},{6,7},{8,9},{9,10},{10,11},{11... | collective-permute-start | bytes 98312 | tf_op jit(solution)/shard_map/ppermute | solution.py:15
  264.8 5.5 %collective-permute-start.33 = (f32[1,8,1024]{2,1,0:T(8,128)S(1)}, f32[1,8,1024]{2,1,0:T(8,128)S(1)}, u32[]{:S(2)}, u32[]{:S(2)}) collective-permute-start(f32[1,8,1024]{2,1,0:T(8,128)S(1)} %get-tuple-element.98), channel_id=1, source_target_pairs={{0,8},{8,16},{16,24},{24,32},{32,40},{40,48},{48,56},{1,9},{9,17},... | collective-permute-start | bytes 98312 | tf_op jit(solution)/shard_map/ppermute | solution.py:15
  270.5 1.4 collective-permute-done.33
  272.8 1.4 fusion.27
  275.3 31.3 %reduce-scatter.2.cloned.1.call-done = f32[4,8,8,512]{3,2,1,0:T(8,128)} async-done(((f32[4,8,8,1024]{3,2,1,0:T(8,128)}), f32[4,8,8,512]{3,2,1,0:T(8,128)}) %reduce-scatter.2.cloned.1.call-update) | async-done | bytes 524304 | tf_op jit(solution)/shard_map/reduce_scatter | solution.py:124
  (209 shorter events, 38.4 us)
Async XLA Ops:
  7.2 299.5 %reduce-scatter.2.cloned.1.call-start = ((), (), s32[]{:S(2)}) async-start(), calls=%async_computation.1 | async-start | bytes 1572864 | tf_op jit(solution)/shard_map/reduce_scatter | solution.py:124
  7.2 20.9 %copy-start.3 = (bf16[4,4,8,8,1024]{4,3,2,1,0:T(8,128)(2,1)S(1)}, bf16[4,4,8,8,1024]{4,3,2,1,0:T(8,128)(2,1)}, u32[]{:S(2)}) copy-start(bf16[4,4,8,8,1024]{4,3,2,1,0:T(8,128)(2,1)} %param.12) | copy-start | bytes 6291460
  9.3 12.4 %copy-start = (f32[1,4,8,8,1024]{4,3,2,1,0:T(8,128)S(1)}, f32[1,4,8,8,1024]{4,3,2,1,0:T(8,128)}, u32[]{:S(2)}) copy-start(f32[1,4,8,8,1024]{4,3,2,1,0:T(8,128)} %param.13) | copy-start | bytes 3145732
  9.3 138.8 %collective-permute-start.4 = (bf16[4,4,1,8,1024]{4,3,1,2,0:T(8,128)(2,1)}, bf16[4,4,1,8,1024]{4,3,1,2,0:T(8,128)(2,1)}, u32[]{:S(2)}, u32[]{:S(2)}) collective-permute-start(bf16[4,4,1,8,1024]{4,3,1,2,0:T(8,128)(2,1)} %get-tuple-element.31), channel_id=1, source_target_pairs={{8,0},{16,8},{24,16},{32,24},{40,32},{48,40},{56,48},{9,1},{17,9},... | collective-permute-start | bytes 786440 | tf_op jit(solution)/shard_map/ppermute | solution.py:16
  10.7 138.5 %collective-permute-start.5 = (bf16[4,4,1,8,1024]{4,3,1,2,0:T(8,128)(2,1)}, bf16[4,4,1,8,1024]{4,3,1,2,0:T(8,128)(2,1)}, u32[]{:S(2)}, u32[]{:S(2)}) collective-permute-start(bf16[4,4,1,8,1024]{4,3,1,2,0:T(8,128)(2,1)} %get-tuple-element.30), channel_id=1, source_target_pairs={{0,8},{8,16},{16,24},{24,32},{32,40},{40,48},{48,56},{1,9},{9,17},... | collective-permute-start | bytes 786440 | tf_op jit(solution)/shard_map/ppermute | solution.py:15
  20.4 130.1 %collective-permute-start.6 = (bf16[4,4,8,1,1024]{4,3,2,1,0:T(2,128)(2,1)}, bf16[4,4,8,1,1024]{4,3,2,1,0:T(2,128)(2,1)}, u32[]{:S(2)}, u32[]{:S(2)}) collective-permute-start(bf16[4,4,8,1,1024]{4,3,2,1,0:T(2,128)(2,1)} %get-tuple-element.33), channel_id=1, source_target_pairs={{1,0},{2,1},{3,2},{4,3},{5,4},{6,5},{7,6},{9,8},{10,9},{11,10},{12... | collective-permute-start | bytes 786440 | tf_op jit(solution)/shard_map/ppermute | solution.py:16
  22.5 116.4 %collective-permute-start.2 = (f32[4,8,1,1024]{3,2,1,0:T(1,128)}, f32[4,8,1,1024]{3,2,1,0:T(1,128)}, u32[]{:S(2)}, u32[]{:S(2)}) collective-permute-start(f32[4,8,1,1024]{3,2,1,0:T(1,128)} %get-tuple-element.83), channel_id=1, source_target_pairs={{1,0},{2,1},{3,2},{4,3},{5,4},{6,5},{7,6},{9,8},{10,9},{11,10},{12... | collective-permute-start | bytes 393224 | tf_op jit(solution)/shard_map/ppermute | solution.py:16
  23.8 116.4 %collective-permute-start.3 = (f32[4,8,1,1024]{3,2,1,0:T(1,128)}, f32[4,8,1,1024]{3,2,1,0:T(1,128)}, u32[]{:S(2)}, u32[]{:S(2)}) collective-permute-start(f32[4,8,1,1024]{3,2,1,0:T(1,128)} %get-tuple-element.82), channel_id=1, source_target_pairs={{0,1},{1,2},{2,3},{3,4},{4,5},{5,6},{6,7},{8,9},{9,10},{10,11},{11... | collective-permute-start | bytes 393224 | tf_op jit(solution)/shard_map/ppermute | solution.py:15
  28.6 4.5 %copy-start.1 = (f32[4,8,8,1024]{3,2,1,0:T(8,128)}, f32[4,8,8,1024]{3,2,1,0:T(8,128)S(1)}, u32[]{:S(2)}) copy-start(f32[4,8,8,1024]{3,2,1,0:T(8,128)S(1)} %get-tuple-element.23) | copy-start | bytes 3145732
  33.0 2.2 copy-start.32
  33.0 2.2 copy-start.33
  39.4 1.5 copy-start.2
  46.1 2.2 copy-start.34
  48.3 11.4 %copy-start.35 = (s32[3]{0:T(128)S(1)}, s32[3]{0:T(128)}, u32[]{:S(2)}) copy-start(s32[3]{0:T(128)} %constant.65.clone.1) | copy-start | bytes 40
  54.0 77.8 %copy-start.31 = (f32[3,1024]{1,0:T(4,128)S(1)}, f32[3,1024]{1,0:T(4,128)}, u32[]{:S(2)}) copy-start(f32[3,1024]{1,0:T(4,128)} %param.11) | copy-start | bytes 36868
  138.3 2.0 copy-start.30
  138.3 6.5 %copy-start.9 = (f32[4,8,7,1024]{3,2,1,0:T(8,128)S(1)}, f32[4,8,7,1024]{3,2,1,0:T(8,128)}, u32[]{:S(2)}) copy-start(f32[4,8,7,1024]{3,2,1,0:T(8,128)} %get-tuple-element.84) | copy-start | bytes 2752516
  138.4 6.5 %copy-start.10 = (f32[4,8,7,1024]{3,2,1,0:T(8,128)S(1)}, f32[4,8,7,1024]{3,2,1,0:T(8,128)}, u32[]{:S(2)}) copy-start(f32[4,8,7,1024]{3,2,1,0:T(8,128)} %get-tuple-element.85) | copy-start | bytes 2752516
  139.0 7.5 %collective-permute-start = (f32[4,1,8,1024]{3,2,1,0:T(8,128)}, f32[4,1,8,1024]{3,2,1,0:T(8,128)S(1)}, u32[]{:S(2)}, u32[]{:S(2)}) collective-permute-start(f32[4,1,8,1024]{3,2,1,0:T(8,128)} %get-tuple-element.79), channel_id=1, source_target_pairs={{8,0},{16,8},{24,16},{32,24},{40,32},{48,40},{56,48},{9,1},{17,9},... | collective-permute-start | bytes 393224 | tf_op jit(solution)/shard_map/ppermute | solution.py:16
  140.3 7.6 %collective-permute-start.1 = (f32[4,1,8,1024]{3,2,1,0:T(8,128)S(1)}, f32[4,1,8,1024]{3,2,1,0:T(8,128)S(1)}, u32[]{:S(2)}, u32[]{:S(2)}) collective-permute-start(f32[4,1,8,1024]{3,2,1,0:T(8,128)S(1)} %copy-done.30), channel_id=1, source_target_pairs={{0,8},{8,16},{16,24},{24,32},{32,40},{40,48},{48,56},{1,9},{9,17},... | collective-permute-start | bytes 393224 | tf_op jit(solution)/shard_map/ppermute | solution.py:15
  144.9 1.6 copy-start.29
  144.9 3.0 copy-start.27
  144.9 3.0 copy-start.28
  146.5 5.7 %collective-permute-start.7 = (bf16[4,4,8,1,1024]{4,3,2,1,0:T(2,128)(2,1)S(1)}, bf16[4,4,8,1,1024]{4,3,2,1,0:T(2,128)(2,1)S(1)}, u32[]{:S(2)}, u32[]{:S(2)}) collective-permute-start(bf16[4,4,8,1,1024]{4,3,2,1,0:T(2,128)(2,1)S(1)} %copy-done.29), channel_id=1, source_target_pairs={{0,1},{1,2},{2,3},{3,4},{4,5},{5,6},{6,7},{8,9},{9,10},{10,11},{11... | collective-permute-start | bytes 786440 | tf_op jit(solution)/shard_map/ppermute | solution.py:15
  147.9 2.3 copy-start.26
  148.1 2.1 copy-start.25
  150.5 2.4 copy-start.15
  150.5 2.4 copy-start.16
  152.9 1.5 copy-start.7
  152.9 1.6 copy-start.8
  154.7 6.5 %copy-start.19 = (f32[4,7,8,1024]{3,2,1,0:T(8,128)S(1)}, f32[4,7,8,1024]{3,2,1,0:T(8,128)}, u32[]{:S(2)}) copy-start(f32[4,7,8,1024]{3,2,1,0:T(8,128)} %get-tuple-element.72) | copy-start | bytes 2752516
  154.7 6.5 %copy-start.20 = (f32[4,7,8,1024]{3,2,1,0:T(8,128)S(1)}, f32[4,7,8,1024]{3,2,1,0:T(8,128)}, u32[]{:S(2)}) copy-start(f32[4,7,8,1024]{3,2,1,0:T(8,128)} %get-tuple-element.73) | copy-start | bytes 2752516
  154.9 20.8 %collective-permute-start.10 = (f32[8,1,1024]{2,1,0:T(1,128)S(1)}, f32[8,1,1024]{2,1,0:T(1,128)S(1)}, u32[]{:S(2)}, u32[]{:S(2)}) collective-permute-start(f32[8,1,1024]{2,1,0:T(1,128)S(1)} %get-tuple-element.135), channel_id=1, source_target_pairs={{1,0},{2,1},{3,2},{4,3},{5,4},{6,5},{7,6},{9,8},{10,9},{11,10},{12... | collective-permute-start | bytes 98312 | tf_op jit(solution)/shard_map/ppermute | solution.py:16
  156.3 19.4 %collective-permute-start.11 = (f32[8,1,1024]{2,1,0:T(1,128)S(1)}, f32[8,1,1024]{2,1,0:T(1,128)S(1)}, u32[]{:S(2)}, u32[]{:S(2)}) collective-permute-start(f32[8,1,1024]{2,1,0:T(1,128)S(1)} %get-tuple-element.134), channel_id=1, source_target_pairs={{0,1},{1,2},{2,3},{3,4},{4,5},{5,6},{6,7},{8,9},{9,10},{10,11},{11... | collective-permute-start | bytes 98312 | tf_op jit(solution)/shard_map/ppermute | solution.py:15
  161.3 1.5 copy-start.12
  164.3 1.5 copy-start.18
  165.8 1.5 copy-start.22
  167.3 1.5 copy-start.14
  169.5 6.4 %collective-permute-start.8 = (f32[1,8,1024]{2,1,0:T(8,128)S(1)}, f32[1,8,1024]{2,1,0:T(8,128)S(1)}, u32[]{:S(2)}, u32[]{:S(2)}) collective-permute-start(f32[1,8,1024]{2,1,0:T(8,128)S(1)} %get-tuple-element.131), channel_id=1, source_target_pairs={{8,0},{16,8},{24,16},{32,24},{40,32},{48,40},{56,48},{9,1},{17,9},... | collective-permute-start | bytes 98312 | tf_op jit(solution)/shard_map/ppermute | solution.py:16
  170.8 6.5 %collective-permute-start.9 = (f32[1,8,1024]{2,1,0:T(8,128)S(1)}, f32[1,8,1024]{2,1,0:T(8,128)S(1)}, u32[]{:S(2)}, u32[]{:S(2)}) collective-permute-start(f32[1,8,1024]{2,1,0:T(8,128)S(1)} %get-tuple-element.130), channel_id=1, source_target_pairs={{0,8},{8,16},{16,24},{24,32},{32,40},{40,48},{48,56},{1,9},{9,17},... | collective-permute-start | bytes 98312 | tf_op jit(solution)/shard_map/ppermute | solution.py:15
  178.9 12.8 %collective-permute-start.14 = (f32[4,8,1,1024]{3,2,1,0:T(1,128)S(1)}, f32[4,8,1,1024]{3,2,1,0:T(1,128)S(1)}, u32[]{:S(2)}, u32[]{:S(2)}) collective-permute-start(f32[4,8,1,1024]{3,2,1,0:T(1,128)S(1)} %get-tuple-element.69), channel_id=1, source_target_pairs={{1,0},{2,1},{3,2},{4,3},{5,4},{6,5},{7,6},{9,8},{10,9},{11,10},{12... | collective-permute-start | bytes 393224 | tf_op jit(solution)/shard_map/ppermute | solution.py:16
  180.4 11.3 %collective-permute-start.15 = (f32[4,8,1,1024]{3,2,1,0:T(1,128)S(1)}, f32[4,8,1,1024]{3,2,1,0:T(1,128)S(1)}, u32[]{:S(2)}, u32[]{:S(2)}) collective-permute-start(f32[4,8,1,1024]{3,2,1,0:T(1,128)S(1)} %get-tuple-element.68), channel_id=1, source_target_pairs={{0,1},{1,2},{2,3},{3,4},{4,5},{5,6},{6,7},{8,9},{9,10},{10,11},{11... | collective-permute-start | bytes 393224 | tf_op jit(solution)/shard_map/ppermute | solution.py:15
  184.6 7.8 %collective-permute-start.12 = (f32[4,1,8,1024]{3,2,1,0:T(8,128)S(1)}, f32[4,1,8,1024]{3,2,1,0:T(8,128)S(1)}, u32[]{:S(2)}, u32[]{:S(2)}) collective-permute-start(f32[4,1,8,1024]{3,2,1,0:T(8,128)S(1)} %get-tuple-element.65), channel_id=1, source_target_pairs={{8,0},{16,8},{24,16},{32,24},{40,32},{48,40},{56,48},{9,1},{17,9},... | collective-permute-start | bytes 393224 | tf_op jit(solution)/shard_map/ppermute | solution.py:16
  185.9 8.3 %collective-permute-start.13 = (f32[4,1,8,1024]{3,2,1,0:T(8,128)S(1)}, f32[4,1,8,1024]{3,2,1,0:T(8,128)S(1)}, u32[]{:S(2)}, u32[]{:S(2)}) collective-permute-start(f32[4,1,8,1024]{3,2,1,0:T(8,128)S(1)} %get-tuple-element.64), channel_id=1, source_target_pairs={{0,8},{8,16},{16,24},{24,32},{32,40},{40,48},{48,56},{1,9},{9,17},... | collective-permute-start | bytes 393224 | tf_op jit(solution)/shard_map/ppermute | solution.py:15
  195.9 11.7 %collective-permute-start.18 = (f32[8,1,1024]{2,1,0:T(1,128)S(1)}, f32[8,1,1024]{2,1,0:T(1,128)S(1)}, u32[]{:S(2)}, u32[]{:S(2)}) collective-permute-start(f32[8,1,1024]{2,1,0:T(1,128)S(1)} %get-tuple-element.127), channel_id=1, source_target_pairs={{1,0},{2,1},{3,2},{4,3},{5,4},{6,5},{7,6},{9,8},{10,9},{11,10},{12... | collective-permute-start | bytes 98312 | tf_op jit(solution)/shard_map/ppermute | solution.py:16
  197.2 10.4 %collective-permute-start.19 = (f32[8,1,1024]{2,1,0:T(1,128)S(1)}, f32[8,1,1024]{2,1,0:T(1,128)S(1)}, u32[]{:S(2)}, u32[]{:S(2)}) collective-permute-start(f32[8,1,1024]{2,1,0:T(1,128)S(1)} %get-tuple-element.126), channel_id=1, source_target_pairs={{0,1},{1,2},{2,3},{3,4},{4,5},{5,6},{6,7},{8,9},{9,10},{10,11},{11... | collective-permute-start | bytes 98312 | tf_op jit(solution)/shard_map/ppermute | solution.py:15
  200.8 6.9 %collective-permute-start.16 = (f32[1,8,1024]{2,1,0:T(8,128)S(1)}, f32[1,8,1024]{2,1,0:T(8,128)S(1)}, u32[]{:S(2)}, u32[]{:S(2)}) collective-permute-start(f32[1,8,1024]{2,1,0:T(8,128)S(1)} %get-tuple-element.123), channel_id=1, source_target_pairs={{8,0},{16,8},{24,16},{32,24},{40,32},{48,40},{56,48},{9,1},{17,9},... | collective-permute-start | bytes 98312 | tf_op jit(solution)/shard_map/ppermute | solution.py:16
  202.1 7.0 %collective-permute-start.17 = (f32[1,8,1024]{2,1,0:T(8,128)S(1)}, f32[1,8,1024]{2,1,0:T(8,128)S(1)}, u32[]{:S(2)}, u32[]{:S(2)}) collective-permute-start(f32[1,8,1024]{2,1,0:T(8,128)S(1)} %get-tuple-element.122), channel_id=1, source_target_pairs={{0,8},{8,16},{16,24},{24,32},{32,40},{40,48},{48,56},{1,9},{9,17},... | collective-permute-start | bytes 98312 | tf_op jit(solution)/shard_map/ppermute | solution.py:15
  210.8 12.7 %collective-permute-start.22 = (f32[4,8,1,1024]{3,2,1,0:T(1,128)S(1)}, f32[4,8,1,1024]{3,2,1,0:T(1,128)S(1)}, u32[]{:S(2)}, u32[]{:S(2)}) collective-permute-start(f32[4,8,1,1024]{3,2,1,0:T(1,128)S(1)} %get-tuple-element.55), channel_id=1, source_target_pairs={{1,0},{2,1},{3,2},{4,3},{5,4},{6,5},{7,6},{9,8},{10,9},{11,10},{12... | collective-permute-start | bytes 393224 | tf_op jit(solution)/shard_map/ppermute | solution.py:16
  212.1 11.4 %collective-permute-start.23 = (f32[4,8,1,1024]{3,2,1,0:T(1,128)S(1)}, f32[4,8,1,1024]{3,2,1,0:T(1,128)S(1)}, u32[]{:S(2)}, u32[]{:S(2)}) collective-permute-start(f32[4,8,1,1024]{3,2,1,0:T(1,128)S(1)} %get-tuple-element.54), channel_id=1, source_target_pairs={{0,1},{1,2},{2,3},{3,4},{4,5},{5,6},{6,7},{8,9},{9,10},{10,11},{11... | collective-permute-start | bytes 393224 | tf_op jit(solution)/shard_map/ppermute | solution.py:15
  215.7 8.6 %collective-permute-start.20 = (f32[4,1,8,1024]{3,2,1,0:T(8,128)S(1)}, f32[4,1,8,1024]{3,2,1,0:T(8,128)S(1)}, u32[]{:S(2)}, u32[]{:S(2)}) collective-permute-start(f32[4,1,8,1024]{3,2,1,0:T(8,128)S(1)} %get-tuple-element.51), channel_id=1, source_target_pairs={{8,0},{16,8},{24,16},{32,24},{40,32},{48,40},{56,48},{9,1},{17,9},... | collective-permute-start | bytes 393224 | tf_op jit(solution)/shard_map/ppermute | solution.py:16
  217.0 9.1 %collective-permute-start.21 = (f32[4,1,8,1024]{3,2,1,0:T(8,128)S(1)}, f32[4,1,8,1024]{3,2,1,0:T(8,128)S(1)}, u32[]{:S(2)}, u32[]{:S(2)}) collective-permute-start(f32[4,1,8,1024]{3,2,1,0:T(8,128)S(1)} %get-tuple-element.50), channel_id=1, source_target_pairs={{0,8},{8,16},{16,24},{24,32},{32,40},{40,48},{48,56},{1,9},{9,17},... | collective-permute-start | bytes 393224 | tf_op jit(solution)/shard_map/ppermute | solution.py:15
  227.7 11.7 %collective-permute-start.26 = (f32[8,1,1024]{2,1,0:T(1,128)S(1)}, f32[8,1,1024]{2,1,0:T(1,128)S(1)}, u32[]{:S(2)}, u32[]{:S(2)}) collective-permute-start(f32[8,1,1024]{2,1,0:T(1,128)S(1)} %get-tuple-element.119), channel_id=1, source_target_pairs={{1,0},{2,1},{3,2},{4,3},{5,4},{6,5},{7,6},{9,8},{10,9},{11,10},{12... | collective-permute-start | bytes 98312 | tf_op jit(solution)/shard_map/ppermute | solution.py:16
  229.0 10.4 %collective-permute-start.27 = (f32[8,1,1024]{2,1,0:T(1,128)S(1)}, f32[8,1,1024]{2,1,0:T(1,128)S(1)}, u32[]{:S(2)}, u32[]{:S(2)}) collective-permute-start(f32[8,1,1024]{2,1,0:T(1,128)S(1)} %get-tuple-element.118), channel_id=1, source_target_pairs={{0,1},{1,2},{2,3},{3,4},{4,5},{5,6},{6,7},{8,9},{9,10},{10,11},{11... | collective-permute-start | bytes 98312 | tf_op jit(solution)/shard_map/ppermute | solution.py:15
  232.6 6.9 %collective-permute-start.24 = (f32[1,8,1024]{2,1,0:T(8,128)S(1)}, f32[1,8,1024]{2,1,0:T(8,128)S(1)}, u32[]{:S(2)}, u32[]{:S(2)}) collective-permute-start(f32[1,8,1024]{2,1,0:T(8,128)S(1)} %get-tuple-element.115), channel_id=1, source_target_pairs={{8,0},{16,8},{24,16},{32,24},{40,32},{48,40},{56,48},{9,1},{17,9},... | collective-permute-start | bytes 98312 | tf_op jit(solution)/shard_map/ppermute | solution.py:16
  233.9 7.0 %collective-permute-start.25 = (f32[1,8,1024]{2,1,0:T(8,128)S(1)}, f32[1,8,1024]{2,1,0:T(8,128)S(1)}, u32[]{:S(2)}, u32[]{:S(2)}) collective-permute-start(f32[1,8,1024]{2,1,0:T(8,128)S(1)} %get-tuple-element.114), channel_id=1, source_target_pairs={{0,8},{8,16},{16,24},{24,32},{32,40},{40,48},{48,56},{1,9},{9,17},... | collective-permute-start | bytes 98312 | tf_op jit(solution)/shard_map/ppermute | solution.py:15
  242.6 12.9 %collective-permute-start.30 = (f32[4,8,1,1024]{3,2,1,0:T(1,128)S(1)}, f32[4,8,1,1024]{3,2,1,0:T(1,128)S(1)}, u32[]{:S(2)}, u32[]{:S(2)}) collective-permute-start(f32[4,8,1,1024]{3,2,1,0:T(1,128)S(1)} %get-tuple-element.41), channel_id=1, source_target_pairs={{1,0},{2,1},{3,2},{4,3},{5,4},{6,5},{7,6},{9,8},{10,9},{11,10},{12... | collective-permute-start | bytes 393224 | tf_op jit(solution)/shard_map/ppermute | solution.py:16
  243.9 11.6 %collective-permute-start.31 = (f32[4,8,1,1024]{3,2,1,0:T(1,128)S(1)}, f32[4,8,1,1024]{3,2,1,0:T(1,128)S(1)}, u32[]{:S(2)}, u32[]{:S(2)}) collective-permute-start(f32[4,8,1,1024]{3,2,1,0:T(1,128)S(1)} %get-tuple-element.40), channel_id=1, source_target_pairs={{0,1},{1,2},{2,3},{3,4},{4,5},{5,6},{6,7},{8,9},{9,10},{10,11},{11... | collective-permute-start | bytes 393224 | tf_op jit(solution)/shard_map/ppermute | solution.py:15
  247.6 8.6 %collective-permute-start.28 = (f32[4,1,8,1024]{3,2,1,0:T(8,128)S(1)}, f32[4,1,8,1024]{3,2,1,0:T(8,128)S(1)}, u32[]{:S(2)}, u32[]{:S(2)}) collective-permute-start(f32[4,1,8,1024]{3,2,1,0:T(8,128)S(1)} %get-tuple-element.37), channel_id=1, source_target_pairs={{8,0},{16,8},{24,16},{32,24},{40,32},{48,40},{56,48},{9,1},{17,9},... | collective-permute-start | bytes 393224 | tf_op jit(solution)/shard_map/ppermute | solution.py:16
  248.9 9.1 %collective-permute-start.29 = (f32[4,1,8,1024]{3,2,1,0:T(8,128)S(1)}, f32[4,1,8,1024]{3,2,1,0:T(8,128)S(1)}, u32[]{:S(2)}, u32[]{:S(2)}) collective-permute-start(f32[4,1,8,1024]{3,2,1,0:T(8,128)S(1)} %get-tuple-element.36), channel_id=1, source_target_pairs={{0,8},{8,16},{16,24},{24,32},{32,40},{40,48},{48,56},{1,9},{9,17},... | collective-permute-start | bytes 393224 | tf_op jit(solution)/shard_map/ppermute | solution.py:15
  258.7 11.7 %collective-permute-start.34 = (f32[8,1,1024]{2,1,0:T(1,128)S(1)}, f32[8,1,1024]{2,1,0:T(1,128)S(1)}, u32[]{:S(2)}, u32[]{:S(2)}) collective-permute-start(f32[8,1,1024]{2,1,0:T(1,128)S(1)} %get-tuple-element.103), channel_id=1, source_target_pairs={{1,0},{2,1},{3,2},{4,3},{5,4},{6,5},{7,6},{9,8},{10,9},{11,10},{12... | collective-permute-start | bytes 98312 | tf_op jit(solution)/shard_map/ppermute | solution.py:16
  260.0 10.4 %collective-permute-start.35 = (f32[8,1,1024]{2,1,0:T(1,128)S(1)}, f32[8,1,1024]{2,1,0:T(1,128)S(1)}, u32[]{:S(2)}, u32[]{:S(2)}) collective-permute-start(f32[8,1,1024]{2,1,0:T(1,128)S(1)} %get-tuple-element.102), channel_id=1, source_target_pairs={{0,1},{1,2},{2,3},{3,4},{4,5},{5,6},{6,7},{8,9},{9,10},{10,11},{11... | collective-permute-start | bytes 98312 | tf_op jit(solution)/shard_map/ppermute | solution.py:15
  263.5 6.9 %collective-permute-start.32 = (f32[1,8,1024]{2,1,0:T(8,128)S(1)}, f32[1,8,1024]{2,1,0:T(8,128)S(1)}, u32[]{:S(2)}, u32[]{:S(2)}) collective-permute-start(f32[1,8,1024]{2,1,0:T(8,128)S(1)} %get-tuple-element.99), channel_id=1, source_target_pairs={{8,0},{16,8},{24,16},{32,24},{40,32},{48,40},{56,48},{9,1},{17,9},... | collective-permute-start | bytes 98312 | tf_op jit(solution)/shard_map/ppermute | solution.py:16
  264.8 7.0 %collective-permute-start.33 = (f32[1,8,1024]{2,1,0:T(8,128)S(1)}, f32[1,8,1024]{2,1,0:T(8,128)S(1)}, u32[]{:S(2)}, u32[]{:S(2)}) collective-permute-start(f32[1,8,1024]{2,1,0:T(8,128)S(1)} %get-tuple-element.98), channel_id=1, source_target_pairs={{0,8},{8,16},{16,24},{24,32},{32,40},{40,48},{48,56},{1,9},{9,17},... | collective-permute-start | bytes 98312 | tf_op jit(solution)/shard_map/ppermute | solution.py:15
  (9 other events, 11.2 us)
Sparse Core Ops, SparseCore 0:
  274.4 32.2 reduce-scatter.1

commit v2 on v1

v2 whole, which is shorter than its diff:
```python
import functools

import jax
import jax.numpy as jnp
from jax import lax
from jax.experimental import pallas as pl
from jax.experimental.pallas import tpu as pltpu
from jax.sharding import PartitionSpec as P

step_length = 0.25
MESH = pl.DeviceIdType.MESH


def neighbours(shard, axis, dim):
    size, length = (lax.axis_size(axis), shard.shape[dim])
    up = [(i, i + 1) for i in range(size - 1)]
    down = [(i + 1, i) for i in range(size - 1)]
    last = lax.slice_in_dim(shard, length - 1, length, axis=dim)
    first = lax.slice_in_dim(shard, 0, 1, axis=dim)
    before = lax.ppermute(last, axis, up)
    after = lax.ppermute(first, axis, down)
    return (before, after)


def local_cells(cells, width_x, width_y):
    local_x = cells[:, 0] - lax.axis_index("gx") * width_x
    local_y = cells[:, 1] - lax.axis_index("gy") * width_y
    inside = (local_x >= 0) & (local_x < width_x) & (local_y >= 0) & (local_y < width_y)
    return (
        jnp.clip(local_x, 0, width_x - 1),
        jnp.clip(local_y, 0, width_y - 1),
        cells[:, 2],
        inside.astype(jnp.float32),
    )


def stencil_kernel(
    nx, ny, steps,
    state_in, sound, wind, fpad, fyr, inj,
    state_out, acc_out,
    pads, pbuf, ysend, yrecv, ypsend, yprecv, ss, rs, ps, pr,
):
    _, width_x, width_y, depth = state_in.shape
    me_p = lax.axis_index("pair")
    gx = lax.axis_index("gx")
    gy = lax.axis_index("gy")
    has_lo_x = gx > 0
    has_hi_x = gx < nx - 1
    has_lo_y = gy > 0
    has_hi_y = gy < ny - 1
    dev_lo_x = (me_p, gx - 1, gy)
    dev_hi_x = (me_p, gx + 1, gy)
    dev_lo_y = (me_p, gx, gy - 1)
    dev_hi_y = (me_p, gx, gy + 1)

    zero_slab = jnp.zeros((width_y, depth), jnp.float32)
    for par in range(2):
        for c in range(4):
            pads[par, c, 0] = zero_slab
            pads[par, c, width_x + 1] = zero_slab
            for side in range(2):
                yrecv[par, side, c] = jnp.zeros((width_x, 1, depth), jnp.float32)
    pbuf[0] = zero_slab
    pbuf[width_x + 1] = zero_slab
    for side in range(2):
        yprecv[side] = jnp.zeros((width_x, 1, depth), jnp.float32)

    barrier = pltpu.get_barrier_semaphore()
    for cond, dev in ((has_lo_x, dev_lo_x), (has_hi_x, dev_hi_x), (has_lo_y, dev_lo_y), (has_hi_y, dev_hi_y)):
        @pl.when(cond)
        def _():
            pl.semaphore_signal(barrier, 1, device_id=dev, device_id_type=MESH)
    peers = (
        (gx + nx - 1) // nx + (2 * nx - 2 - gx) // nx
        + (gy + ny - 1) // ny + (2 * ny - 2 - gy) // ny
    )
    pl.semaphore_wait(barrier, peers)

    iy = lax.broadcasted_iota(jnp.int32, (width_y, depth), 0)
    iz = lax.broadcasted_iota(jnp.int32, (width_y, depth), 1)
    we = wind[0:1, :]
    wn = wind[1:2, :]
    wv = wind[2:3, :]

    def dy(v, lo, hi):
        up = jnp.where(iy == width_y - 1, hi, pltpu.roll(v, width_y - 1, 0))
        down = jnp.where(iy == 0, lo, pltpu.roll(v, 1, 0))
        return (up - down) * 0.5

    def dz(v):
        up = jnp.where(iz == depth - 1, 0.0, pltpu.roll(v, depth - 1, 1))
        down = jnp.where(iz == 0, 0.0, pltpu.roll(v, 1, 1))
        return (up - down) * 0.5

    def exchange(src_lo_x, src_hi_x, dst_lo_x, dst_hi_x, src_y_hi, src_y_lo, dst_y_lo, dst_y_hi, send, recv):
        outs = (
            (has_hi_x, src_hi_x, dst_lo_x, 0, dev_hi_x),
            (has_lo_x, src_lo_x, dst_hi_x, 1, dev_lo_x),
            (has_hi_y, src_y_hi, dst_y_lo, 2, dev_hi_y),
            (has_lo_y, src_y_lo, dst_y_hi, 3, dev_lo_y),
        )
        copies = []
        for cond, src, dst, slot, dev in outs:
            copy = pltpu.make_async_remote_copy(
                src_ref=src, dst_ref=dst, send_sem=send.at[slot], recv_sem=recv.at[slot],
                device_id=dev, device_id_type=MESH,
            )
            copies.append((cond, copy))

            @pl.when(cond)
            def _():
                copy.start()
        incoming = (has_lo_x, has_hi_x, has_lo_y, has_hi_y)
        for (cond, copy), arrives in zip(copies, incoming):
            @pl.when(cond)
            def _():
                copy.wait_send()

            @pl.when(arrives)
            def _():
                copy.wait_recv()

    def fill_state(par, x, c, v):
        pads[par, c, x + 1] = v
        ysend[par, 0, c, x] = v[width_y - 1:width_y, :]
        ysend[par, 1, c, x] = v[0:1, :]

    def copy_in(x, carry):
        for c in range(4):
            fill_state(0, x, c, state_in[c, x])
        return carry

    lax.fori_loop(0, width_x, copy_in, 0)

    for step in range(steps):
        par = step % 2
        nxt = 1 - par
        snap = steps - 1 - step
        last = step == steps - 1
        exchange(
            pads.at[par, :, pl.ds(1, 1)], pads.at[par, :, pl.ds(width_x, 1)],
            pads.at[par, :, pl.ds(0, 1)], pads.at[par, :, pl.ds(width_x + 1, 1)],
            ysend.at[par, 0], ysend.at[par, 1], yrecv.at[par, 0], yrecv.at[par, 1],
            ss.at[par], rs.at[par],
        )

        def pressure_slab(x, carry, par=par, snap=snap):
            xp = x + 1
            old = pads.at[par]
            p = old[0, xp]
            dxp = (old[0, xp + 1] - old[0, x]) * 0.5
            dxa = (old[1, xp + 1] - old[1, x]) * 0.5
            dyp = dy(p, yrecv[par, 0, 0, x], yrecv[par, 1, 0, x])
            dya = dy(old[2, xp], yrecv[par, 0, 2, x], yrecv[par, 1, 2, x])
            dzp = dz(p)
            dza = dz(old[3, xp])
            divergence = dxa + dya + dza
            p_new = (
                p
                + step_length * (sound[x] * divergence + we * dxp + wn * dyp + wv * dzp)
                + inj[snap, x]
            )
            pbuf[xp] = p_new
            ypsend[0, x] = p_new[width_y - 1:width_y, :]
            ypsend[1, x] = p_new[0:1, :]
            return carry

        lax.fori_loop(0, width_x, pressure_slab, 0)
        exchange(
            pbuf.at[pl.ds(1, 1)], pbuf.at[pl.ds(width_x, 1)],
            pbuf.at[pl.ds(0, 1)], pbuf.at[pl.ds(width_x + 1, 1)],
            ypsend.at[0], ypsend.at[1], yprecv.at[0], yprecv.at[1],
            ps, pr,
        )

        def velocity_slab(x, carry, par=par, nxt=nxt, snap=snap, last=last, step=step):
            xp = x + 1
            old = pads.at[par]
            p_new = pbuf[xp]
            grad = (
                (pbuf[xp + 1] - pbuf[x]) * 0.5,
                dy(p_new, yprecv[0, x], yprecv[1, x]),
                dz(p_new),
            )
            a_new = []
            for i in range(3):
                a = old[1 + i, xp]
                dxa = (old[1 + i, xp + 1] - old[1 + i, x]) * 0.5
                dya = dy(a, yrecv[par, 0, 1 + i, x], yrecv[par, 1, 1 + i, x])
                dza = dz(a)
                a_new.append(a + step_length * (grad[i] + we * dxa + wn * dya + wv * dza))
            fe, fn, fu = [], [], []
            for c in range(4):
                f = fpad[snap, c, xp].astype(jnp.float32)
                fe.append((fpad[snap, c, xp + 1].astype(jnp.float32) - fpad[snap, c, x].astype(jnp.float32)) * 0.5)
                fn.append(dy(f, fyr[snap, 0, c, x].astype(jnp.float32), fyr[snap, 1, c, x].astype(jnp.float32)))
                fu.append(dz(f))
            pieces = [p_new * (fe[1] + fn[2] + fu[3])]
            for along in (fe, fn, fu):
                pieces.append(p_new * along[0] + a_new[0] * along[1] + a_new[1] * along[2] + a_new[2] * along[3])
            for c in range(4):
                if step == 0:
                    acc_out[c, x] = pieces[c]
                else:
                    acc_out[c, x] = acc_out[c, x] + pieces[c]
            new_state = [p_new] + a_new
            for c in range(4):
                if last:
                    state_out[c, x] = new_state[c]
                else:
                    fill_state(nxt, x, c, new_state[c])
            return carry

        lax.fori_loop(0, width_x, velocity_slab, 0)


def shards(
    sound_speed_sq,
    wind_profile,
    forward_field,
    adjoint_state,
    pair_counts,
    source_cells,
    receiver_cells,
    residuals,
):
    steps_total = forward_field.shape[0]
    width_x, width_y, depth = sound_speed_sq.shape
    slots = residuals.shape[0]
    live = (jnp.arange(slots, dtype=jnp.int32) < pair_counts[0]).astype(jnp.float32)
    sx, sy, sz, src_inside = local_cells(source_cells, width_x, width_y)
    rx, ry, rz, rcv_inside = local_cells(receiver_cells, width_x, width_y)
    local_samples = jnp.stack(
        [forward_field[t, 0][sx, sy, sz] for t in range(steps_total)]
    ).astype(jnp.float32) * src_inside[None, :]
    me = lax.axis_index("pair")
    slot = jnp.zeros((lax.axis_size("pair"),) + local_samples.shape, jnp.float32)
    samples = lax.psum(slot.at[me].set(local_samples), ("pair", "gx", "gy"))[me]
    amplitude = jnp.transpose(residuals) * samples * (live * rcv_inside)[None, :]
    rcv_flat = (rx * width_y + ry) * depth + rz
    step_index = jnp.broadcast_to(jnp.arange(steps_total)[:, None], amplitude.shape)
    injected = (
        jnp.zeros((steps_total, width_x * width_y * depth), jnp.float32)
        .at[step_index, jnp.broadcast_to(rcv_flat[None, :], amplitude.shape)]
        .add(amplitude)
        .reshape(steps_total, width_x, width_y, depth)
    )
    lo_x, hi_x = neighbours(forward_field, "gx", 2)
    fpad = jnp.concatenate([lo_x, forward_field, hi_x], axis=2)
    up = [(i, i + 1) for i in range(lax.axis_size("gy") - 1)]
    down = [(i + 1, i) for i in range(lax.axis_size("gy") - 1)]
    lo_y = lax.ppermute(forward_field[:, :, :, width_y - 1:width_y, :], "gy", up)
    hi_y = lax.ppermute(forward_field[:, :, :, 0:1, :], "gy", down)
    fyr = jnp.stack([lo_y, hi_y], axis=1)

    vmem = pl.BlockSpec(memory_space=pltpu.VMEM)
    kernel = functools.partial(
        stencil_kernel, lax.axis_size("gx"), lax.axis_size("gy"), steps_total
    )
    state_new, kernel_local = pl.pallas_call(
        kernel,
        out_shape=(
            jax.ShapeDtypeStruct((4, width_x, width_y, depth), jnp.float32),
            jax.ShapeDtypeStruct((4, width_x, width_y, depth), jnp.float32),
        ),
        in_specs=[vmem] * 6,
        out_specs=(vmem, vmem),
        scratch_shapes=[
            pltpu.VMEM((2, 4, width_x + 2, width_y, depth), jnp.float32),
            pltpu.VMEM((width_x + 2, width_y, depth), jnp.float32),
            pltpu.VMEM((2, 2, 4, width_x, 1, depth), jnp.float32),
            pltpu.VMEM((2, 2, 4, width_x, 1, depth), jnp.float32),
            pltpu.VMEM((2, width_x, 1, depth), jnp.float32),
            pltpu.VMEM((2, width_x, 1, depth), jnp.float32),
            pltpu.SemaphoreType.DMA((2, 4)),
            pltpu.SemaphoreType.DMA((2, 4)),
            pltpu.SemaphoreType.DMA((4,)),
            pltpu.SemaphoreType.DMA((4,)),
        ],
        compiler_params=pltpu.CompilerParams(
            collective_id=0, has_side_effects=True, vmem_limit_bytes=48 * 1024 * 1024
        ),
    )(adjoint_state[0], sound_speed_sq, wind_profile, fpad, fyr, injected)
    kernels = lax.psum_scatter(kernel_local, "pair", scatter_dimension=3, tiled=True)
    return (kernels, state_new[None])


def solution(mesh):
    in_specs = (
        P("gx", "gy", None),
        P(),
        P(None, None, "gx", "gy", None),
        P("pair", None, "gx", "gy", None),
        P("pair"),
        P("pair", None),
        P("pair", None),
        P("pair", None),
    )
    out_specs = (P(None, "gx", "gy", "pair"), P("pair", None, "gx", "gy", None))
    return jax.shard_map(shards, mesh=mesh, in_specs=in_specs, out_specs=out_specs, check_vma=False)
```

time: 316 us -> 212 us (0.67)
  starting transfers between devices: 104 us -> 9.97 us
  Pallas kernels: 0 us -> 58 us
  other arithmetic: 39.7 us -> 13.4 us
  waiting for transfers between devices: 43.3 us -> 21.3 us
  local copies, waits for them, and re-layouts: 42.6 us -> 23.5 us
    ppermute x18 -> x1, starting transfers between devices: 80.3 us -> 3.61 us  [neighbours(): before = lax.ppermute(last, axis, up)]
    pallas_call x0 -> x1, Pallas kernels: none -> 58 us  [shards(): pl.pallas_call(kernel, out_shape=(jax.ShapeDtypeStruct((4, width_x, width...]
    ppermute x18 -> x1, starting transfers between devices: 23.7 us -> 1.29 us  [neighbours(): after = lax.ppermute(first, axis, down)]
    mul x32 -> x1, other arithmetic: 15 us -> 0.01 us  [shards(): live * rcv_inside]
    ppermute x18 -> x1, waiting for transfers between devices: 11.1 us -> 0.01 us  [neighbours(): before = lax.ppermute(last, axis, up)]
    reduce_scatter x1, waiting for transfers between devices: 31.3 us -> 21.3 us  [shards(): lax.psum_scatter(kernel_local, 'pair', scatter_dimension=3, tiled=True)]
    unnamed x73 -> x25, local copies, waits for them, and re-layouts: 11.4 us -> 2.59 us
    scatter-add x4 -> x0, other arithmetic: 8.57 us -> none  [shards(): injected = jnp.zeros((width_x * width_y * depth,), jnp.float32).at[rcv_fl...]
  transfers between devices with their start and end apart: 37 -> 5, of which waited for: 11 -> 1; matrix products, arithmetic and copies ran while one was open for 19% -> 15% of each run, Pallas kernels for 0% -> 0%
where the time goes in v2:
time: 212 us; the launch traced here: 210 us
  blocking collectives  69.3 us (33%)
  Pallas kernels  58 us (27%)
  local copies, waits for them, and re-layouts  23.5 us (11%)
  waiting for transfers between devices  21.3 us (10%)
  between operations  15 us (7%)
  other arithmetic  13.4 us (6%)
  starting transfers between devices  9.97 us (5%)
    psum x1, blocking collectives, shards(): samples = lax.psum(slot.at[me].set(local_samples), ('pair', 'gx', 'gy'))[me]  69.3 us
    pallas_call x1, Pallas kernels, shards(): pl.pallas_call(kernel, out_shape=(jax.ShapeDtypeStruct((4, width_x, width...  58 us
    reduce_scatter x1, waiting for transfers between devices, shards(): lax.psum_scatter(kernel_local, 'pair', scatter_dimension=3, tiled=True)  21.3 us
    gather x4, local copies, waits for them, and re-layouts, shards(): forward_field[t, 0][sx, sy, sz]  11.2 us
    unnamed x5, other arithmetic  7.45 us
  transfers between devices with their start and end apart: 5, of which 1 were waited for; matrix products, arithmetic and copies ran while one was open for 15% of the time, Pallas kernels for 0%

profile of v2, /device:TPU:0, one launch (start us, length us, event | category | flops | bytes accessed | tf_op | source)
XLA Modules:
  0.0 210.5 jit_solution(832111292534236213)
XLA Ops:
  7.2 0.0 copy-start.3
  7.2 0.0 copy-start.4
  7.2 0.0 copy-start.5
  7.2 0.0 reduce-scatter.2.cloned.1.call-start
  7.2 2.0 fusion.14
  9.2 0.0 copy-start.8
  9.2 0.0 copy-start.7
  9.2 3.6 %collective-permute-start = (bf16[4,4,1,8,1024]{4,3,2,1,0:T(8,128)(2,1)}, bf16[4,4,1,8,1024]{4,3,2,1,0:T(8,128)(2,1)S(1)}, u32[]{:S(2)}, u32[]{:S(2)}) collective-permute-start(bf16[4,4,1,8,1024]{4,3,2,1,0:T(8,128)(2,1)} %get-tuple-element.24), channel_id=1, source_target_pairs={{0,8},{8,16},{16,24},{24,32},{32,40},{40,48},{48,56},{1,9},{9,17},... | collective-permute-start | bytes 786440 | tf_op jit(solution)/shard_map/ppermute | solution.py:20
  12.8 1.3 collective-permute-start.1
  14.1 3.4 %fusion.13 = (bf16[4,4,8,1,1024]{4,3,2,1,0:T(2,128)(2,1)S(1)}, bf16[4,4,8,1,1024]{4,3,2,1,0:T(2,128)(2,1)S(1)}) fusion(bf16[4,4,8,8,1024]{4,3,2,1,0:T(8,128)(2,1)} %param.12), kind=kLoop, calls=%fused_computation.45 | loop fusion | bytes 1048576 | tf_op jit(solution)/shard_map/slice | solution.py:252
  17.5 0.0 copy-start.9
  17.5 0.0 copy-start.6
  17.6 0.8 copy.21
  18.3 1.3 collective-permute-start.3
  19.6 0.8 copy.20
  20.4 3.7 %collective-permute-start.2 = (bf16[4,4,8,1,1024]{4,2,1,0,3:T(8,128)(2,1)}, bf16[4,4,8,1,1024]{4,2,1,0,3:T(8,128)(2,1)}, u32[]{:S(2)}, u32[]{:S(2)}) collective-permute-start(bf16[4,4,8,1,1024]{4,2,1,0,3:T(8,128)(2,1)} %copy.20), channel_id=1, source_target_pairs={{0,1},{1,2},{2,3},{3,4},{4,5},{5,6},{6,7},{8,9},{9,10},{10,11},{11... | collective-permute-start | bytes 786440 | tf_op jit(solution)/shard_map/ppermute | solution.py:252
  24.2 0.0 copy-done.4
  24.2 0.0 copy-done.5
  24.3 0.0 copy-done.3
  25.0 0.0 copy-done.8
  25.0 0.1 and_reduce_fusion
  25.1 0.0 copy-done.7
  25.1 0.1 multiply_reduce_fusion
  25.2 2.8 %gather_fusion = bf16[256]{0:T(256)(128)(2,1)S(1)} fusion(bf16[8,8,1024]{2,1,0:T(8,128)(2,1)S(1)} %get-tuple-element.18, s32[256]{0:T(256)S(1)} %bitcast.34), kind=kCustom, calls=%fused_computation | custom fusion | bytes 4096 | tf_op jit(solution)/shard_map/gather | solution.py:234
  28.0 2.8 %gather_fusion.1 = bf16[256]{0:T(256)(128)(2,1)S(1)} fusion(bf16[8,8,1024]{2,1,0:T(8,128)(2,1)S(1)} %get-tuple-element.19, s32[256]{0:T(256)S(1)} %bitcast.35), kind=kCustom, calls=%fused_computation.1 | custom fusion | bytes 4096 | tf_op jit(solution)/shard_map/gather | solution.py:234
  30.8 2.8 %gather_fusion.3 = bf16[256]{0:T(256)(128)(2,1)S(1)} fusion(bf16[8,8,1024]{2,1,0:T(8,128)(2,1)S(1)} %get-tuple-element.20, s32[256]{0:T(256)S(1)} %bitcast.36), kind=kCustom, calls=%fused_computation.3 | custom fusion | bytes 4096 | tf_op jit(solution)/shard_map/gather | solution.py:234
  33.6 2.8 %gather_fusion.2 = bf16[256]{0:T(256)(128)(2,1)S(1)} fusion(bf16[8,8,1024]{2,1,0:T(8,128)(2,1)S(1)} %get-tuple-element.21, s32[256]{0:T(256)S(1)} %bitcast.37), kind=kCustom, calls=%fused_computation.2 | custom fusion | bytes 4096 | tf_op jit(solution)/shard_map/gather | solution.py:234
  36.5 0.0 copy-done.9
  36.5 0.7 and_reduce_fusion.2
  37.2 0.6 select_dynamic-update-slice_fusion
  37.8 69.3 %psum.7 = f32[2,4,256]{2,1,0:T(4,128)S(1)} all-reduce(f32[2,4,256]{2,1,0:T(4,128)S(1)} %select_dynamic-update-slice_fusion), channel_id=1, replica_groups=mesh['pair'=2,'gx'=8,'gy'=8] {'pair','gx','gy'}, use_global_device_ids=true, to_apply=%region_1.2 | all-reduce | flops 2048 | bytes 16384 | tf_op jit(solution)/shard_map/psum | solution.py:238
  107.0 0.0 copy-done.6
  107.1 7.3 %scatter_custom_fusion = f32[262144]{0:T(1024)} fusion(s32[1024]{0:T(1024)S(1)} %bitcast.41, f32[1024]{0:T(1024)S(1)} %bitcast.42, f32[]{:T(128)} %constant.42.clone.1), kind=kCustom, calls=%fused_computation.7 | custom fusion | flops 1024 | bytes 1048580
  114.3 1.4 reshape.261.inj
  115.7 0.0 collective-permute-done.3
  115.7 1.4 copy.19
  117.2 0.0 collective-permute-done.2
  117.2 1.4 copy.18
  118.7 1.7 pad_maximum_fusion.1.fyr
  120.4 0.0 copy-start
  120.4 0.0 copy-start.1
  120.4 0.0 copy-start.2
  120.4 0.0 collective-permute-done
  120.4 0.0 collective-permute-done.1
  120.4 2.9 %pad_maximum_fusion.fpad = bf16[4,4,10,8,1024]{4,3,2,1,0:T(8,128)(2,1)} fusion(bf16[4,4,1,8,1024]{4,3,2,1,0:T(8,128)(2,1)} %collective-permute-done.1, bf16[4,4,8,8,1024]{4,3,2,1,0:T(8,128)(2,1)S(1)} %copy-done.3, bf16[4,4,1,8,1024]{4,3,2,1,0:T(8,128)(2,1)S(1)} %collective-permute-done), kind=kLoop, calls=%fused_computation.5 | loop fusion | flops 2621440 | bytes 5242880 | tf_op jit(solution)/shard_map/concatenate | solution.py:249
  123.3 0.0 copy-done
  123.3 0.0 copy-done.1
  123.3 0.0 copy-done.2
  123.3 58.0 %shard_map.95 = (f32[4,8,8,1024]{3,2,1,0:T(8,128)S(1)}, f32[4,8,8,1024]{3,2,1,0:T(8,128)}) custom-call(f32[4,8,8,1024]{3,2,1,0:T(8,128)S(1)} %bitcast.33, f32[8,8,1024]{2,1,0:T(8,128)S(1)} %copy-done.1, f32[3,1024]{1,0:T(4,128)S(1)} %copy-done.2, bf16[4,4,10,8,1024]{4,3,2,1,0:T(8,128)(2,1)} %pad_maximum_fusion.fpad, ...), custom_call_target="tpu_custom_call" | custom-call | tf_op jit(solution)/shard_map/pallas_call | solution.py:260
  181.3 0.0 reduce-scatter.2.cloned.1.call-update
  181.4 21.3 %reduce-scatter.2.cloned.1.call-done = f32[4,8,8,512]{3,2,1,0:T(8,128)} async-done(((f32[4,8,8,1024]{3,2,1,0:T(8,128)}), f32[4,8,8,512]{3,2,1,0:T(8,128)}) %reduce-scatter.2.cloned.1.call-update) | async-done | bytes 524304 | tf_op jit(solution)/shard_map/reduce_scatter | solution.py:284
  202.6 1.0 copy.27
  (18 shorter events, 0.2 us)
Async XLA Ops:
  7.2 17.1 %copy-start.3 = (bf16[4,4,8,8,1024]{4,3,2,1,0:T(8,128)(2,1)S(1)}, bf16[4,4,8,8,1024]{4,3,2,1,0:T(8,128)(2,1)}, u32[]{:S(2)}) copy-start(bf16[4,4,8,8,1024]{4,3,2,1,0:T(8,128)(2,1)} %param.12) | copy-start | bytes 6291460
  7.2 17.0 %copy-start.4 = (s32[256,3]{0,1:T(4,128)S(1)}, s32[256,3]{0,1:T(4,128)}, u32[]{:S(2)}) copy-start(s32[256,3]{0,1:T(4,128)} %param.16) | copy-start | bytes 9220
  7.2 17.0 %copy-start.5 = (s32[256,3]{0,1:T(4,128)S(1)}, s32[256,3]{0,1:T(4,128)}, u32[]{:S(2)}) copy-start(s32[256,3]{0,1:T(4,128)} %param.15) | copy-start | bytes 9220
  7.2 195.4 %reduce-scatter.2.cloned.1.call-start = ((), (), s32[]{:S(2)}) async-start(), calls=%async_computation.1 | async-start | bytes 1572864 | tf_op jit(solution)/shard_map/reduce_scatter | solution.py:284
  9.2 15.8 %copy-start.8 = (s32[2]{0:T(128)S(1)}, s32[2]{0:T(128)}, u32[]{:S(2)}) copy-start(s32[2]{0:T(128)} %constant.61) | copy-start | bytes 28
  9.2 15.9 %copy-start.7 = (s32[2]{0:T(128)S(1)}, s32[2]{0:T(128)}, u32[]{:S(2)}) copy-start(s32[2]{0:T(128)} %constant.58) | copy-start | bytes 28
  9.2 111.2 %collective-permute-start = (bf16[4,4,1,8,1024]{4,3,2,1,0:T(8,128)(2,1)}, bf16[4,4,1,8,1024]{4,3,2,1,0:T(8,128)(2,1)S(1)}, u32[]{:S(2)}, u32[]{:S(2)}) collective-permute-start(bf16[4,4,1,8,1024]{4,3,2,1,0:T(8,128)(2,1)} %get-tuple-element.24), channel_id=1, source_target_pairs={{0,8},{8,16},{16,24},{24,32},{32,40},{40,48},{48,56},{1,9},{9,17},... | collective-permute-start | bytes 786440 | tf_op jit(solution)/shard_map/ppermute | solution.py:20
  12.8 107.6 %collective-permute-start.1 = (bf16[4,4,1,8,1024]{4,3,2,1,0:T(8,128)(2,1)}, bf16[4,4,1,8,1024]{4,3,2,1,0:T(8,128)(2,1)}, u32[]{:S(2)}, u32[]{:S(2)}) collective-permute-start(bf16[4,4,1,8,1024]{4,3,2,1,0:T(8,128)(2,1)} %get-tuple-element.25), channel_id=1, source_target_pairs={{8,0},{16,8},{24,16},{32,24},{40,32},{48,40},{56,48},{9,1},{17,9},... | collective-permute-start | bytes 786440 | tf_op jit(solution)/shard_map/ppermute | solution.py:21
  17.5 18.9 %copy-start.9 = (s32[3]{0:T(128)S(1)}, s32[3]{0:T(128)}, u32[]{:S(2)}) copy-start(s32[3]{0:T(128)} %constant.54.clone.1) | copy-start | bytes 40
  17.5 89.5 %copy-start.6 = (f32[256,4]{0,1:T(4,128)S(1)}, f32[256,4]{0,1:T(4,128)}, u32[]{:S(2)}) copy-start(f32[256,4]{0,1:T(4,128)} %param.17) | copy-start | bytes 12292
  18.3 97.4 %collective-permute-start.3 = (bf16[4,4,8,1,1024]{4,2,1,0,3:T(8,128)(2,1)}, bf16[4,4,8,1,1024]{4,2,1,0,3:T(8,128)(2,1)}, u32[]{:S(2)}, u32[]{:S(2)}) collective-permute-start(bf16[4,4,8,1,1024]{4,2,1,0,3:T(8,128)(2,1)} %copy.21), channel_id=1, source_target_pairs={{1,0},{2,1},{3,2},{4,3},{5,4},{6,5},{7,6},{9,8},{10,9},{11,10},{12... | collective-permute-start | bytes 786440 | tf_op jit(solution)/shard_map/ppermute | solution.py:253
  20.4 96.8 %collective-permute-start.2 = (bf16[4,4,8,1,1024]{4,2,1,0,3:T(8,128)(2,1)}, bf16[4,4,8,1,1024]{4,2,1,0,3:T(8,128)(2,1)}, u32[]{:S(2)}, u32[]{:S(2)}) collective-permute-start(bf16[4,4,8,1,1024]{4,2,1,0,3:T(8,128)(2,1)} %copy.20), channel_id=1, source_target_pairs={{0,1},{1,2},{2,3},{3,4},{4,5},{5,6},{6,7},{8,9},{9,10},{10,11},{11... | collective-permute-start | bytes 786440 | tf_op jit(solution)/shard_map/ppermute | solution.py:252
  120.4 2.9 %copy-start = (f32[1,4,8,8,1024]{4,3,2,1,0:T(8,128)S(1)}, f32[1,4,8,8,1024]{4,3,2,1,0:T(8,128)}, u32[]{:S(2)}) copy-start(f32[1,4,8,8,1024]{4,3,2,1,0:T(8,128)} %param.13) | copy-start | bytes 3145732
  120.4 2.9 %copy-start.1 = (f32[8,8,1024]{2,1,0:T(8,128)S(1)}, f32[8,8,1024]{2,1,0:T(8,128)}, u32[]{:S(2)}) copy-start(f32[8,8,1024]{2,1,0:T(8,128)} %sound.1) | copy-start | bytes 786436
  120.4 2.9 %copy-start.2 = (f32[3,1024]{1,0:T(4,128)S(1)}, f32[3,1024]{1,0:T(4,128)}, u32[]{:S(2)}) copy-start(f32[3,1024]{1,0:T(4,128)} %wind.1) | copy-start | bytes 36868
Sparse Core Ops, SparseCore 0:
  181.5 21.1 reduce-scatter.1

commit v3 on v2

--- a/solution.py
+++ b/solution.py
@@ -214,6 +214,61 @@
         lax.fori_loop(0, width_x, velocity_slab, 0)
 
 
+def samples_kernel(nx, ny, local_ref, out_ref, sent, got, send_sem, recv_sem):
+    me_p = lax.axis_index("pair")
+    gx = lax.axis_index("gx")
+    gy = lax.axis_index("gy")
+    rounds = []
+    k = 1
+    while k < nx:
+        rounds.append((me_p, gx + k - 2 * k * ((gx // k) % 2), gy))
+        k *= 2
+    k = 1
+    while k < ny:
+        rounds.append((me_p, gx, gy + k - 2 * k * ((gy // k) % 2)))
+        k *= 2
+    barrier = pltpu.get_barrier_semaphore()
+    for dev in rounds:
+        pl.semaphore_signal(barrier, 1, device_id=dev, device_id_type=MESH)
+    pl.semaphore_wait(barrier, len(rounds))
+    total = local_ref[...]
+    for r, dev in enumerate(rounds):
+        src = local_ref
+        if r > 0:
+            sent[r] = total
+            src = sent.at[r]
+        copy = pltpu.make_async_remote_copy(
+            src_ref=src, dst_ref=got.at[r], send_sem=send_sem.at[r], recv_sem=recv_sem.at[r],
+            device_id=dev, device_id_type=MESH,
+        )
+        copy.start()
+        copy.wait_send()
+        copy.wait_recv()
+        total = total + got[r]
+    out_ref[...] = total
+
+
+def gathered_samples(local_samples):
+    nx, ny = lax.axis_size("gx"), lax.axis_size("gy")
+    rounds = (nx.bit_length() - 1) + (ny.bit_length() - 1)
+    if (nx & (nx - 1)) or (ny & (ny - 1)) or rounds == 0:
+        return lax.psum(local_samples, ("gx", "gy"))
+    vmem = pl.BlockSpec(memory_space=pltpu.VMEM)
+    return pl.pallas_call(
+        functools.partial(samples_kernel, nx, ny),
+        out_shape=jax.ShapeDtypeStruct(local_samples.shape, jnp.float32),
+        in_specs=[vmem],
+        out_specs=vmem,
+        scratch_shapes=[
+            pltpu.VMEM((rounds,) + local_samples.shape, jnp.float32),
+            pltpu.VMEM((rounds,) + local_samples.shape, jnp.float32),
+            pltpu.SemaphoreType.DMA((rounds,)),
+            pltpu.SemaphoreType.DMA((rounds,)),
+        ],
+        compiler_params=pltpu.CompilerParams(collective_id=1, has_side_effects=True),
+    )(local_samples)
+
+
 def shards(
     sound_speed_sq,
     wind_profile,
@@ -233,9 +288,7 @@
     local_samples = jnp.stack(
         [forward_field[t, 0][sx, sy, sz] for t in range(steps_total)]
     ).astype(jnp.float32) * src_inside[None, :]
-    me = lax.axis_index("pair")
-    slot = jnp.zeros((lax.axis_size("pair"),) + local_samples.shape, jnp.float32)
-    samples = lax.psum(slot.at[me].set(local_samples), ("pair", "gx", "gy"))[me]
+    samples = gathered_samples(local_samples)
     amplitude = jnp.transpose(residuals) * samples * (live * rcv_inside)[None, :]
     rcv_flat = (rx * width_y + ry) * depth + rz
     step_index = jnp.broadcast_to(jnp.arange(steps_total)[:, None], amplitude.shape)

time: 212 us -> 165 us (0.78)
  blocking collectives: 69.3 us -> 0 us
  Pallas kernels: 58 us -> 79.5 us
    psum x1 -> x0, blocking collectives: 69.3 us -> none  [shards(): samples = lax.psum(slot.at[me].set(local_samples), ('pair', 'gx', 'gy'))[me]]
    pallas_call x0 -> x1, Pallas kernels: none -> 24.2 us  [gathered_samples(): pl.pallas_call(functools.partial(samples_kernel, nx, ny), out_shape=jax.S...]
    pallas_call x1, Pallas kernels: 58 us -> 55.3 us  [shards(): pl.pallas_call(kernel, out_shape=(jax.ShapeDtypeStruct((4, width_x, width...]
  transfers between devices with their start and end apart: 5 -> 5, of which waited for: 1 -> 1; matrix products, arithmetic and copies ran while one was open for 15% -> 19% of each run, Pallas kernels for 0% -> 15%
where the time goes in v3:
time: 165 us; the launch traced here: 163 us
  Pallas kernels  79.5 us (48%)
  local copies, waits for them, and re-layouts  23.5 us (14%)
  waiting for transfers between devices  22.2 us (13%)
  between operations  15 us (9%)
  other arithmetic  13.5 us (8%)
  starting transfers between devices  9.82 us (6%)
    pallas_call x1, Pallas kernels, shards(): pl.pallas_call(kernel, out_shape=(jax.ShapeDtypeStruct((4, width_x, width...  55.3 us
    pallas_call x1, Pallas kernels, gathered_samples(): pl.pallas_call(functools.partial(samples_kernel, nx, ny), out_shape=jax.S...  24.2 us
    reduce_scatter x1, waiting for transfers between devices, shards(): lax.psum_scatter(kernel_local, 'pair', scatter_dimension=3, tiled=True)  22.1 us
    gather x4, local copies, waits for them, and re-layouts, shards(): forward_field[t, 0][sx, sy, sz]  11.2 us
    unnamed x5, other arithmetic  8.22 us
    ppermute x1, starting transfers between devices, shards(): lax.ppermute(forward_field[:, :, :, width_y - 1:width_y, :], 'gy', up)  3.73 us
    ppermute x1, starting transfers between devices, neighbours(): before = lax.ppermute(last, axis, up)  3.48 us
    slice x1, local copies, waits for them, and re-layouts, shards(): forward_field[:, :, :, width_y - 1:width_y, :]  3.39 us
  transfers between devices with their start and end apart: 5, of which 1 were waited for; matrix products, arithmetic and copies ran while one was open for 19% of the time, Pallas kernels for 15%

profile of v3, /device:TPU:0, one launch (start us, length us, event | category | flops | bytes accessed | tf_op | source)
XLA Modules:
  0.0 163.4 jit_solution(8648233489819264885)
XLA Ops:
  7.2 0.0 copy-start.3
  7.2 0.0 copy-start.5
  7.2 0.0 copy-start.4
  7.2 0.0 reduce-scatter.2.cloned.1.call-start
  7.2 2.0 %fusion.14 = (bf16[4,4,1,8,1024]{4,3,2,1,0:T(8,128)(2,1)}, bf16[4,4,1,8,1024]{4,3,2,1,0:T(8,128)(2,1)}) fusion(bf16[4,4,8,8,1024]{4,3,2,1,0:T(8,128)(2,1)} %param.10), kind=kLoop, calls=%fused_computation.45 | loop fusion | bytes 1048576 | tf_op jit(solution)/shard_map/slice | solution.py:18
  9.2 3.5 %collective-permute-start = (bf16[4,4,1,8,1024]{4,3,2,1,0:T(8,128)(2,1)}, bf16[4,4,1,8,1024]{4,3,2,1,0:T(8,128)(2,1)S(1)}, u32[]{:S(2)}, u32[]{:S(2)}) collective-permute-start(bf16[4,4,1,8,1024]{4,3,2,1,0:T(8,128)(2,1)} %get-tuple-element.12), channel_id=1, source_target_pairs={{0,8},{8,16},{16,24},{24,32},{32,40},{40,48},{48,56},{1,9},{9,17},... | collective-permute-start | bytes 786440 | tf_op jit(solution)/shard_map/ppermute | solution.py:20
  12.7 1.3 collective-permute-start.1
  14.0 3.4 %fusion.13 = (bf16[4,4,8,1,1024]{4,3,2,1,0:T(2,128)(2,1)S(1)}, bf16[4,4,8,1,1024]{4,3,2,1,0:T(2,128)(2,1)S(1)}) fusion(bf16[4,4,8,8,1024]{4,3,2,1,0:T(8,128)(2,1)} %param.10), kind=kLoop, calls=%fused_computation.44 | loop fusion | bytes 1048576 | tf_op jit(solution)/shard_map/slice | solution.py:305
  17.4 0.0 copy-start.8
  17.4 0.0 copy-start.6
  17.4 0.0 copy-start.7
  17.4 0.8 copy.21
  18.2 1.3 collective-permute-start.3
  19.5 0.8 copy.20
  20.3 3.7 %collective-permute-start.2 = (bf16[4,4,8,1,1024]{4,2,1,0,3:T(8,128)(2,1)}, bf16[4,4,8,1,1024]{4,2,1,0,3:T(8,128)(2,1)}, u32[]{:S(2)}, u32[]{:S(2)}) collective-permute-start(bf16[4,4,8,1,1024]{4,2,1,0,3:T(8,128)(2,1)} %copy.20), channel_id=1, source_target_pairs={{0,1},{1,2},{2,3},{3,4},{4,5},{5,6},{6,7},{8,9},{9,10},{10,11},{11... | collective-permute-start | bytes 786440 | tf_op jit(solution)/shard_map/ppermute | solution.py:305
  24.0 0.0 copy-done.5
  24.0 0.0 copy-done.4
  24.1 0.0 copy-done.3
  24.8 2.8 %gather_fusion = bf16[256]{0:T(256)(128)(2,1)S(1)} fusion(bf16[8,8,1024]{2,1,0:T(8,128)(2,1)S(1)} %get-tuple-element.6, s32[256]{0:T(256)S(1)} %bitcast.31), kind=kCustom, calls=%fused_computation | custom fusion | bytes 4096 | tf_op jit(solution)/shard_map/gather | solution.py:289
  27.6 2.8 %gather_fusion.1 = bf16[256]{0:T(256)(128)(2,1)S(1)} fusion(bf16[8,8,1024]{2,1,0:T(8,128)(2,1)S(1)} %get-tuple-element.7, s32[256]{0:T(256)S(1)} %bitcast.32), kind=kCustom, calls=%fused_computation.1 | custom fusion | bytes 4096 | tf_op jit(solution)/shard_map/gather | solution.py:289
  30.5 2.8 %gather_fusion.3 = bf16[256]{0:T(256)(128)(2,1)S(1)} fusion(bf16[8,8,1024]{2,1,0:T(8,128)(2,1)S(1)} %get-tuple-element.8, s32[256]{0:T(256)S(1)} %bitcast.33), kind=kCustom, calls=%fused_computation.3 | custom fusion | bytes 4096 | tf_op jit(solution)/shard_map/gather | solution.py:289
  33.3 2.8 %gather_fusion.2 = bf16[256]{0:T(256)(128)(2,1)S(1)} fusion(bf16[8,8,1024]{2,1,0:T(8,128)(2,1)S(1)} %get-tuple-element.9, s32[256]{0:T(256)S(1)} %bitcast.34), kind=kCustom, calls=%fused_computation.2 | custom fusion | bytes 4096 | tf_op jit(solution)/shard_map/gather | solution.py:289
  36.1 0.6 convert_multiply_fusion.local_ref
  36.7 24.2 %shard_map.95 = f32[4,256]{1,0:T(4,128)} custom-call(f32[4,256]{1,0:T(4,128)} %convert_multiply_fusion.local_ref), custom_call_target="tpu_custom_call" | custom-call | tf_op jit(solution)/shard_map/pallas_call | solution.py:257
  60.9 0.0 copy-done.8
  60.9 0.1 and_reduce_fusion
  61.0 0.0 copy-done.6
  61.0 0.7 fusion.3
  61.7 0.0 copy-done.7
  61.7 0.1 multiply_reduce_fusion
  61.8 7.4 %scatter_custom_fusion = f32[262144]{0:T(1024)} fusion(s32[1024]{0:T(1024)S(1)} %bitcast.38, f32[1024]{0:T(1024)S(1)} %bitcast.39, f32[]{:T(128)} %constant.8.clone.1), kind=kCustom, calls=%fused_computation.7 | custom fusion | flops 1024 | bytes 1048580
  69.2 1.4 reshape.167.inj
  70.6 0.0 collective-permute-done.3
  70.6 1.4 copy.19
  72.0 0.0 collective-permute-done.2
  72.0 1.4 copy.18
  73.5 1.7 %pad_maximum_fusion.1.fyr = bf16[4,2,4,8,1,1024]{5,4,3,2,1,0:T(2,128)(2,1)S(1)} fusion(bf16[4,1,4,8,1,1024]{5,4,3,2,1,0:T(2,128)(2,1)S(1)} %copy.19, bf16[4,1,4,8,1,1024]{5,4,3,2,1,0:T(2,128)(2,1)S(1)} %copy.18), kind=kLoop, calls=%fused_computation.6 | loop fusion | flops 262144 | bytes 1048576 | tf_op jit(solution)/shard_map/stack | solution.py:307
  75.2 0.0 copy-start
  75.2 0.0 copy-start.1
  75.2 0.0 copy-start.2
  75.2 0.0 collective-permute-done
  75.2 0.0 collective-permute-done.1
  75.2 2.9 %pad_maximum_fusion.fpad = bf16[4,4,10,8,1024]{4,3,2,1,0:T(8,128)(2,1)} fusion(bf16[4,4,1,8,1024]{4,3,2,1,0:T(8,128)(2,1)} %collective-permute-done.1, bf16[4,4,8,8,1024]{4,3,2,1,0:T(8,128)(2,1)S(1)} %copy-done.3, bf16[4,4,1,8,1024]{4,3,2,1,0:T(8,128)(2,1)S(1)} %collective-permute-done), kind=kLoop, calls=%fused_computation.5 | loop fusion | flops 2621440 | bytes 5242880 | tf_op jit(solution)/shard_map/concatenate | solution.py:302
  78.1 0.0 copy-done
  78.1 0.0 copy-done.1
  78.1 0.0 copy-done.2
  78.1 55.3 %shard_map.96 = (f32[4,8,8,1024]{3,2,1,0:T(8,128)S(1)}, f32[4,8,8,1024]{3,2,1,0:T(8,128)}) custom-call(f32[4,8,8,1024]{3,2,1,0:T(8,128)S(1)} %bitcast.30, f32[8,8,1024]{2,1,0:T(8,128)S(1)} %copy-done.1, f32[3,1024]{1,0:T(4,128)S(1)} %copy-done.2, bf16[4,4,10,8,1024]{4,3,2,1,0:T(8,128)(2,1)} %pad_maximum_fusion.fpad, ...), custom_call_target="tpu_custom_call" | custom-call | tf_op jit(solution)/shard_map/pallas_call | solution.py:313
  133.5 0.0 reduce-scatter.2.cloned.1.call-update
  133.5 22.1 %reduce-scatter.2.cloned.1.call-done = f32[4,8,8,512]{3,2,1,0:T(8,128)} async-done(((f32[4,8,8,1024]{3,2,1,0:T(8,128)}), f32[4,8,8,512]{3,2,1,0:T(8,128)}) %reduce-scatter.2.cloned.1.call-update) | async-done | bytes 524304 | tf_op jit(solution)/shard_map/reduce_scatter | solution.py:337
  155.6 1.0 copy.26
  (15 shorter events, 0.1 us)
Async XLA Ops:
  7.2 16.9 %copy-start.3 = (bf16[4,4,8,8,1024]{4,3,2,1,0:T(8,128)(2,1)S(1)}, bf16[4,4,8,8,1024]{4,3,2,1,0:T(8,128)(2,1)}, u32[]{:S(2)}) copy-start(bf16[4,4,8,8,1024]{4,3,2,1,0:T(8,128)(2,1)} %param.10) | copy-start | bytes 6291460
  7.2 16.9 %copy-start.5 = (s32[256,3]{0,1:T(4,128)S(1)}, s32[256,3]{0,1:T(4,128)}, u32[]{:S(2)}) copy-start(s32[256,3]{0,1:T(4,128)} %param.14) | copy-start | bytes 9220
  7.2 16.8 %copy-start.4 = (s32[256,3]{0,1:T(4,128)S(1)}, s32[256,3]{0,1:T(4,128)}, u32[]{:S(2)}) copy-start(s32[256,3]{0,1:T(4,128)} %param.13) | copy-start | bytes 9220
  7.2 148.4 %reduce-scatter.2.cloned.1.call-start = ((), (), s32[]{:S(2)}) async-start(), calls=%async_computation.1 | async-start | bytes 1572864 | tf_op jit(solution)/shard_map/reduce_scatter | solution.py:337
  9.2 66.0 %collective-permute-start = (bf16[4,4,1,8,1024]{4,3,2,1,0:T(8,128)(2,1)}, bf16[4,4,1,8,1024]{4,3,2,1,0:T(8,128)(2,1)S(1)}, u32[]{:S(2)}, u32[]{:S(2)}) collective-permute-start(bf16[4,4,1,8,1024]{4,3,2,1,0:T(8,128)(2,1)} %get-tuple-element.12), channel_id=1, source_target_pairs={{0,8},{8,16},{16,24},{24,32},{32,40},{40,48},{48,56},{1,9},{9,17},... | collective-permute-start | bytes 786440 | tf_op jit(solution)/shard_map/ppermute | solution.py:20
  12.7 62.5 %collective-permute-start.1 = (bf16[4,4,1,8,1024]{4,3,2,1,0:T(8,128)(2,1)}, bf16[4,4,1,8,1024]{4,3,2,1,0:T(8,128)(2,1)}, u32[]{:S(2)}, u32[]{:S(2)}) collective-permute-start(bf16[4,4,1,8,1024]{4,3,2,1,0:T(8,128)(2,1)} %get-tuple-element.13), channel_id=1, source_target_pairs={{8,0},{16,8},{24,16},{32,24},{40,32},{48,40},{56,48},{9,1},{17,9},... | collective-permute-start | bytes 786440 | tf_op jit(solution)/shard_map/ppermute | solution.py:21
  17.4 43.5 %copy-start.8 = (s32[2]{0:T(128)S(1)}, s32[2]{0:T(128)}, u32[]{:S(2)}) copy-start(s32[2]{0:T(128)} %constant.30) | copy-start | bytes 28
  17.4 43.6 %copy-start.6 = (f32[256,4]{0,1:T(4,128)S(1)}, f32[256,4]{0,1:T(4,128)}, u32[]{:S(2)}) copy-start(f32[256,4]{0,1:T(4,128)} %param.15) | copy-start | bytes 12292
  17.4 44.3 %copy-start.7 = (s32[2]{0:T(128)S(1)}, s32[2]{0:T(128)}, u32[]{:S(2)}) copy-start(s32[2]{0:T(128)} %constant.27) | copy-start | bytes 28
  18.2 52.3 %collective-permute-start.3 = (bf16[4,4,8,1,1024]{4,2,1,0,3:T(8,128)(2,1)}, bf16[4,4,8,1,1024]{4,2,1,0,3:T(8,128)(2,1)}, u32[]{:S(2)}, u32[]{:S(2)}) collective-permute-start(bf16[4,4,8,1,1024]{4,2,1,0,3:T(8,128)(2,1)} %copy.21), channel_id=1, source_target_pairs={{1,0},{2,1},{3,2},{4,3},{5,4},{6,5},{7,6},{9,8},{10,9},{11,10},{12... | collective-permute-start | bytes 786440 | tf_op jit(solution)/shard_map/ppermute | solution.py:306
  20.3 51.7 %collective-permute-start.2 = (bf16[4,4,8,1,1024]{4,2,1,0,3:T(8,128)(2,1)}, bf16[4,4,8,1,1024]{4,2,1,0,3:T(8,128)(2,1)}, u32[]{:S(2)}, u32[]{:S(2)}) collective-permute-start(bf16[4,4,8,1,1024]{4,2,1,0,3:T(8,128)(2,1)} %copy.20), channel_id=1, source_target_pairs={{0,1},{1,2},{2,3},{3,4},{4,5},{5,6},{6,7},{8,9},{9,10},{10,11},{11... | collective-permute-start | bytes 786440 | tf_op jit(solution)/shard_map/ppermute | solution.py:305
  75.2 2.9 %copy-start = (f32[1,4,8,8,1024]{4,3,2,1,0:T(8,128)S(1)}, f32[1,4,8,8,1024]{4,3,2,1,0:T(8,128)}, u32[]{:S(2)}) copy-start(f32[1,4,8,8,1024]{4,3,2,1,0:T(8,128)} %param.11) | copy-start | bytes 3145732
  75.2 2.9 %copy-start.1 = (f32[8,8,1024]{2,1,0:T(8,128)S(1)}, f32[8,8,1024]{2,1,0:T(8,128)}, u32[]{:S(2)}) copy-start(f32[8,8,1024]{2,1,0:T(8,128)} %sound.1) | copy-start | bytes 786436
  75.2 2.9 %copy-start.2 = (f32[3,1024]{1,0:T(4,128)S(1)}, f32[3,1024]{1,0:T(4,128)}, u32[]{:S(2)}) copy-start(f32[3,1024]{1,0:T(4,128)} %wind.1) | copy-start | bytes 36868
Sparse Core Ops, SparseCore 0:
  133.6 21.9 reduce-scatter.1

commit v4 on v3

--- a/solution.py
+++ b/solution.py
@@ -37,8 +37,8 @@
 def stencil_kernel(
     nx, ny, steps,
     state_in, sound, wind, fpad, fyr, inj,
-    state_out, acc_out,
-    pads, pbuf, ysend, yrecv, ypsend, yprecv, ss, rs, ps, pr,
+    state_out, kernel_out,
+    pads, pbuf, ysend, yrecv, ypsend, yprecv, acc_out, ksend, krecv, ss, rs, ps, pr, ks, kr,
 ):
     _, width_x, width_y, depth = state_in.shape
     me_p = lax.axis_index("pair")
@@ -52,6 +52,8 @@
     dev_hi_x = (me_p, gx + 1, gy)
     dev_lo_y = (me_p, gx, gy - 1)
     dev_hi_y = (me_p, gx, gy + 1)
+    dev_pair = (1 - me_p, gx, gy)
+    half = depth // 2
 
     zero_slab = jnp.zeros((width_y, depth), jnp.float32)
     for par in range(2):
@@ -66,11 +68,12 @@
         yprecv[side] = jnp.zeros((width_x, 1, depth), jnp.float32)
 
     barrier = pltpu.get_barrier_semaphore()
+    pl.semaphore_signal(barrier, 1, device_id=dev_pair, device_id_type=MESH)
     for cond, dev in ((has_lo_x, dev_lo_x), (has_hi_x, dev_hi_x), (has_lo_y, dev_lo_y), (has_hi_y, dev_hi_y)):
         @pl.when(cond)
         def _():
             pl.semaphore_signal(barrier, 1, device_id=dev, device_id_type=MESH)
-    peers = (
+    peers = 1 + (
         (gx + nx - 1) // nx + (2 * nx - 2 - gx) // nx
         + (gy + ny - 1) // ny + (2 * ny - 2 - gy) // ny
     )
@@ -199,10 +202,18 @@
             for along in (fe, fn, fu):
                 pieces.append(p_new * along[0] + a_new[0] * along[1] + a_new[1] * along[2] + a_new[2] * along[3])
             for c in range(4):
-                if step == 0:
-                    acc_out[c, x] = pieces[c]
-                else:
-                    acc_out[c, x] = acc_out[c, x] + pieces[c]
+                total = pieces[c] if step == 0 else acc_out[c, x] + pieces[c]
+                if not last:
+                    acc_out[c, x] = total
+                    continue
+                low, high = total[:, :half], total[:, half:]
+                kernel_out[c, x] = jnp.where(me_p == 0, low, high)
+                ksend[x, c] = jnp.where(me_p == 0, high, low)
+            if last:
+                pltpu.make_async_remote_copy(
+                    src_ref=ksend.at[x], dst_ref=krecv.at[x], send_sem=ks.at[x], recv_sem=kr.at[x],
+                    device_id=dev_pair, device_id_type=MESH,
+                ).start()
             new_state = [p_new] + a_new
             for c in range(4):
                 if last:
@@ -212,6 +223,21 @@
             return carry
 
         lax.fori_loop(0, width_x, velocity_slab, 0)
+
+    for x in range(width_x):
+        copy = pltpu.make_async_remote_copy(
+            src_ref=ksend.at[x], dst_ref=krecv.at[x], send_sem=ks.at[x], recv_sem=kr.at[x],
+            device_id=dev_pair, device_id_type=MESH,
+        )
+        copy.wait_send()
+        copy.wait_recv()
+
+    def add_partner(x, carry):
+        for c in range(4):
+            kernel_out[c, x] = kernel_out[c, x] + krecv[x, c]
+        return carry
+
+    lax.fori_loop(0, width_x, add_partner, 0)
 
 
 def samples_kernel(nx, ny, local_ref, out_ref, sent, got, send_sem, recv_sem):
@@ -310,11 +336,11 @@
     kernel = functools.partial(
         stencil_kernel, lax.axis_size("gx"), lax.axis_size("gy"), steps_total
     )
-    state_new, kernel_local = pl.pallas_call(
+    state_new, kernels = pl.pallas_call(
         kernel,
         out_shape=(
             jax.ShapeDtypeStruct((4, width_x, width_y, depth), jnp.float32),
-            jax.ShapeDtypeStruct((4, width_x, width_y, depth), jnp.float32),
+            jax.ShapeDtypeStruct((4, width_x, width_y, depth // 2), jnp.float32),
         ),
         in_specs=[vmem] * 6,
         out_specs=(vmem, vmem),
@@ -325,16 +351,20 @@
             pltpu.VMEM((2, 2, 4, width_x, 1, depth), jnp.float32),
             pltpu.VMEM((2, width_x, 1, depth), jnp.float32),
             pltpu.VMEM((2, width_x, 1, depth), jnp.float32),
+            pltpu.VMEM((4, width_x, width_y, depth), jnp.float32),
+            pltpu.VMEM((width_x, 4, width_y, depth // 2), jnp.float32),
+            pltpu.VMEM((width_x, 4, width_y, depth // 2), jnp.float32),
             pltpu.SemaphoreType.DMA((2, 4)),
             pltpu.SemaphoreType.DMA((2, 4)),
             pltpu.SemaphoreType.DMA((4,)),
             pltpu.SemaphoreType.DMA((4,)),
+            pltpu.SemaphoreType.DMA((width_x,)),
+            pltpu.SemaphoreType.DMA((width_x,)),
         ],
         compiler_params=pltpu.CompilerParams(
             collective_id=0, has_side_effects=True, vmem_limit_bytes=48 * 1024 * 1024
         ),
     )(adjoint_state[0], sound_speed_sq, wind_profile, fpad, fyr, injected)
-    kernels = lax.psum_scatter(kernel_local, "pair", scatter_dimension=3, tiled=True)
     return (kernels, state_new[None])
 
 

time: 165 us -> 141 us (0.85)
  waiting for transfers between devices: 22.2 us -> 0.01 us
  between operations: 15 us -> 1.59 us
  Pallas kernels: 79.5 us -> 91.4 us
    reduce_scatter x1 -> x0, waiting for transfers between devices: 22.1 us -> none  [shards(): lax.psum_scatter(kernel_local, 'pair', scatter_dimension=3, tiled=True)]
    pallas_call x1, Pallas kernels: 55.3 us -> 67.2 us  [shards(): pl.pallas_call(kernel, out_shape=(jax.ShapeDtypeStruct((4, width_x, width...]
    unnamed x23 -> x24, local copies, waits for them, and re-layouts: 2.59 us -> 3.39 us
  transfers between devices with their start and end apart: 5 -> 4, of which waited for: 1 -> 0; matrix products, arithmetic and copies ran while one was open for 19% -> 22% of each run, Pallas kernels for 15% -> 17%
where the time goes in v4:
time: 141 us; the launch traced here: 140 us
  Pallas kernels  91.4 us (65%)
  local copies, waits for them, and re-layouts  24.3 us (17%)
  other arithmetic  13.3 us (9%)
  starting transfers between devices  9.78 us (7%)
  between operations  1.59 us (1%)
    pallas_call x1, Pallas kernels, shards(): pl.pallas_call(kernel, out_shape=(jax.ShapeDtypeStruct((4, width_x, width...  67.2 us
    pallas_call x1, Pallas kernels, gathered_samples(): pl.pallas_call(functools.partial(samples_kernel, nx, ny), out_shape=jax.S...  24.2 us
    gather x4, local copies, waits for them, and re-layouts, shards(): forward_field[t, 0][sx, sy, sz]  11.2 us
    unnamed x5, other arithmetic  8.03 us
    ppermute x1, starting transfers between devices, shards(): lax.ppermute(forward_field[:, :, :, width_y - 1:width_y, :], 'gy', up)  3.73 us
    ppermute x1, starting transfers between devices, neighbours(): before = lax.ppermute(last, axis, up)  3.48 us
    slice x1, local copies, waits for them, and re-layouts, shards(): forward_field[:, :, :, width_y - 1:width_y, :]  3.39 us
    unnamed x24, local copies, waits for them, and re-layouts  3.39 us
  transfers between devices with their start and end apart: 4, of which 0 were waited for; matrix products, arithmetic and copies ran while one was open for 22% of the time, Pallas kernels for 17%

profile of v4, /device:TPU:0, one launch (start us, length us, event | category | flops | bytes accessed | tf_op | source)
XLA Modules:
  0.0 140.3 jit_solution(11903238476009767672)
XLA Ops:
  0.6 0.0 copy-start.3
  0.6 0.0 copy-start.5
  0.7 0.0 copy-start.4
  0.7 2.0 %fusion.14 = (bf16[4,4,1,8,1024]{4,3,2,1,0:T(8,128)(2,1)}, bf16[4,4,1,8,1024]{4,3,2,1,0:T(8,128)(2,1)}) fusion(bf16[4,4,8,8,1024]{4,3,2,1,0:T(8,128)(2,1)} %param.10), kind=kLoop, calls=%fused_computation.45 | loop fusion | bytes 1048576 | tf_op jit(solution)/shard_map/slice | solution.py:18
  2.7 3.5 %collective-permute-start = (bf16[4,4,1,8,1024]{4,3,2,1,0:T(8,128)(2,1)}, bf16[4,4,1,8,1024]{4,3,2,1,0:T(8,128)(2,1)S(1)}, u32[]{:S(2)}, u32[]{:S(2)}) collective-permute-start(bf16[4,4,1,8,1024]{4,3,2,1,0:T(8,128)(2,1)} %get-tuple-element.12), channel_id=1, source_target_pairs={{0,8},{8,16},{16,24},{24,32},{32,40},{40,48},{48,56},{1,9},{9,17},... | collective-permute-start | bytes 786440 | tf_op jit(solution)/shard_map/ppermute | solution.py:20
  6.1 1.3 collective-permute-start.1
  7.4 3.4 %fusion.13 = (bf16[4,4,8,1,1024]{4,3,2,1,0:T(2,128)(2,1)S(1)}, bf16[4,4,8,1,1024]{4,3,2,1,0:T(2,128)(2,1)S(1)}) fusion(bf16[4,4,8,8,1024]{4,3,2,1,0:T(8,128)(2,1)} %param.10), kind=kLoop, calls=%fused_computation.44 | loop fusion | bytes 1048576 | tf_op jit(solution)/shard_map/slice | solution.py:331
  10.8 0.0 copy-start.8
  10.9 0.0 copy-start.6
  10.9 0.0 copy-start.7
  10.9 0.8 copy.21
  11.7 1.3 collective-permute-start.3
  12.9 0.8 copy.20
  13.7 3.7 %collective-permute-start.2 = (bf16[4,4,8,1,1024]{4,2,1,0,3:T(8,128)(2,1)}, bf16[4,4,8,1,1024]{4,2,1,0,3:T(8,128)(2,1)}, u32[]{:S(2)}, u32[]{:S(2)}) collective-permute-start(bf16[4,4,8,1,1024]{4,2,1,0,3:T(8,128)(2,1)} %copy.20), channel_id=1, source_target_pairs={{0,1},{1,2},{2,3},{3,4},{4,5},{5,6},{6,7},{8,9},{9,10},{10,11},{11... | collective-permute-start | bytes 786440 | tf_op jit(solution)/shard_map/ppermute | solution.py:331
  17.5 0.0 copy-done.5
  17.5 0.0 copy-done.4
  17.5 0.0 copy-done.3
  18.2 2.8 %gather_fusion = bf16[256]{0:T(256)(128)(2,1)S(1)} fusion(bf16[8,8,1024]{2,1,0:T(8,128)(2,1)S(1)} %get-tuple-element.6, s32[256]{0:T(256)S(1)} %bitcast.31), kind=kCustom, calls=%fused_computation | custom fusion | bytes 4096 | tf_op jit(solution)/shard_map/gather | solution.py:315
  21.1 2.8 %gather_fusion.1 = bf16[256]{0:T(256)(128)(2,1)S(1)} fusion(bf16[8,8,1024]{2,1,0:T(8,128)(2,1)S(1)} %get-tuple-element.7, s32[256]{0:T(256)S(1)} %bitcast.32), kind=kCustom, calls=%fused_computation.1 | custom fusion | bytes 4096 | tf_op jit(solution)/shard_map/gather | solution.py:315
  23.9 2.8 %gather_fusion.3 = bf16[256]{0:T(256)(128)(2,1)S(1)} fusion(bf16[8,8,1024]{2,1,0:T(8,128)(2,1)S(1)} %get-tuple-element.8, s32[256]{0:T(256)S(1)} %bitcast.33), kind=kCustom, calls=%fused_computation.3 | custom fusion | bytes 4096 | tf_op jit(solution)/shard_map/gather | solution.py:315
  26.7 2.8 %gather_fusion.2 = bf16[256]{0:T(256)(128)(2,1)S(1)} fusion(bf16[8,8,1024]{2,1,0:T(8,128)(2,1)S(1)} %get-tuple-element.9, s32[256]{0:T(256)S(1)} %bitcast.34), kind=kCustom, calls=%fused_computation.2 | custom fusion | bytes 4096 | tf_op jit(solution)/shard_map/gather | solution.py:315
  29.5 0.6 convert_multiply_fusion.local_ref
  30.1 24.2 %shard_map.95 = f32[4,256]{1,0:T(4,128)} custom-call(f32[4,256]{1,0:T(4,128)} %convert_multiply_fusion.local_ref), custom_call_target="tpu_custom_call" | custom-call | tf_op jit(solution)/shard_map/pallas_call | solution.py:283
  54.4 0.0 copy-done.8
  54.4 0.1 and_reduce_fusion
  54.5 0.0 copy-done.6
  54.5 0.7 fusion.3
  55.1 0.0 copy-done.7
  55.1 0.1 multiply_reduce_fusion
  55.2 7.2 %scatter_custom_fusion = f32[262144]{0:T(1024)} fusion(s32[1024]{0:T(1024)S(1)} %bitcast.38, f32[1024]{0:T(1024)S(1)} %bitcast.39, f32[]{:T(128)} %constant.8.clone.1), kind=kCustom, calls=%fused_computation.7 | custom fusion | flops 1024 | bytes 1048580
  62.4 1.4 reshape.167.inj
  63.8 0.0 collective-permute-done.3
  63.8 1.4 %copy.19 = bf16[4,1,4,8,1,1024]{5,4,3,2,1,0:T(2,128)(2,1)S(1)} copy(bf16[4,1,4,8,1,1024]{5,3,2,0,4,1:T(8,128)(2,1)} %bitcast.2) | data formatting | bytes 524288 | tf_op jit(solution)/shard_map/stack | solution.py:333
  65.3 0.0 collective-permute-done.2
  65.3 1.4 %copy.18 = bf16[4,1,4,8,1,1024]{5,4,3,2,1,0:T(2,128)(2,1)S(1)} copy(bf16[4,1,4,8,1,1024]{5,3,2,0,4,1:T(8,128)(2,1)} %bitcast.1) | data formatting | bytes 524288 | tf_op jit(solution)/shard_map/stack | solution.py:333
  66.7 1.7 %pad_maximum_fusion.1.fyr = bf16[4,2,4,8,1,1024]{5,4,3,2,1,0:T(2,128)(2,1)S(1)} fusion(bf16[4,1,4,8,1,1024]{5,4,3,2,1,0:T(2,128)(2,1)S(1)} %copy.19, bf16[4,1,4,8,1,1024]{5,4,3,2,1,0:T(2,128)(2,1)S(1)} %copy.18), kind=kLoop, calls=%fused_computation.6 | loop fusion | flops 262144 | bytes 1048576 | tf_op jit(solution)/shard_map/stack | solution.py:333
  68.4 0.0 copy-start
  68.4 0.0 copy-start.1
  68.5 0.0 copy-start.2
  68.5 0.0 collective-permute-done
  68.5 0.0 collective-permute-done.1
  68.5 2.9 %pad_maximum_fusion.fpad = bf16[4,4,10,8,1024]{4,3,2,1,0:T(8,128)(2,1)} fusion(bf16[4,4,1,8,1024]{4,3,2,1,0:T(8,128)(2,1)} %collective-permute-done.1, bf16[4,4,8,8,1024]{4,3,2,1,0:T(8,128)(2,1)S(1)} %copy-done.3, bf16[4,4,1,8,1024]{4,3,2,1,0:T(8,128)(2,1)S(1)} %collective-permute-done), kind=kLoop, calls=%fused_computation.5 | loop fusion | flops 2621440 | bytes 5242880 | tf_op jit(solution)/shard_map/concatenate | solution.py:328
  71.4 0.0 copy-done
  71.4 0.0 copy-done.1
  71.4 0.0 copy-done.2
  71.4 67.2 %shard_map.96 = (f32[4,8,8,1024]{3,2,1,0:T(8,128)S(1)}, f32[4,8,8,512]{3,2,1,0:T(8,128)S(1)}) custom-call(f32[4,8,8,1024]{3,2,1,0:T(8,128)S(1)} %bitcast.30, f32[8,8,1024]{2,1,0:T(8,128)S(1)} %copy-done.1, f32[3,1024]{1,0:T(4,128)S(1)} %copy-done.2, bf16[4,4,10,8,1024]{4,3,2,1,0:T(8,128)(2,1)} %pad_maximum_fusion.fpad, ...), custom_call_target="tpu_custom_call" | custom-call | tf_op jit(solution)/shard_map/pallas_call | solution.py:339
  138.6 0.8 copy.27
  139.3 1.0 copy.28
  (15 shorter events, 0.1 us)
Async XLA Ops:
  0.6 16.9 %copy-start.3 = (bf16[4,4,8,8,1024]{4,3,2,1,0:T(8,128)(2,1)S(1)}, bf16[4,4,8,8,1024]{4,3,2,1,0:T(8,128)(2,1)}, u32[]{:S(2)}) copy-start(bf16[4,4,8,8,1024]{4,3,2,1,0:T(8,128)(2,1)} %param.10) | copy-start | bytes 6291460
  0.6 16.8 %copy-start.5 = (s32[256,3]{0,1:T(4,128)S(1)}, s32[256,3]{0,1:T(4,128)}, u32[]{:S(2)}) copy-start(s32[256,3]{0,1:T(4,128)} %param.14) | copy-start | bytes 9220
  0.7 16.8 %copy-start.4 = (s32[256,3]{0,1:T(4,128)S(1)}, s32[256,3]{0,1:T(4,128)}, u32[]{:S(2)}) copy-start(s32[256,3]{0,1:T(4,128)} %param.13) | copy-start | bytes 9220
  2.7 65.8 %collective-permute-start = (bf16[4,4,1,8,1024]{4,3,2,1,0:T(8,128)(2,1)}, bf16[4,4,1,8,1024]{4,3,2,1,0:T(8,128)(2,1)S(1)}, u32[]{:S(2)}, u32[]{:S(2)}) collective-permute-start(bf16[4,4,1,8,1024]{4,3,2,1,0:T(8,128)(2,1)} %get-tuple-element.12), channel_id=1, source_target_pairs={{0,8},{8,16},{16,24},{24,32},{32,40},{40,48},{48,56},{1,9},{9,17},... | collective-permute-start | bytes 786440 | tf_op jit(solution)/shard_map/ppermute | solution.py:20
  6.1 62.3 %collective-permute-start.1 = (bf16[4,4,1,8,1024]{4,3,2,1,0:T(8,128)(2,1)}, bf16[4,4,1,8,1024]{4,3,2,1,0:T(8,128)(2,1)}, u32[]{:S(2)}, u32[]{:S(2)}) collective-permute-start(bf16[4,4,1,8,1024]{4,3,2,1,0:T(8,128)(2,1)} %get-tuple-element.13), channel_id=1, source_target_pairs={{8,0},{16,8},{24,16},{32,24},{40,32},{48,40},{56,48},{9,1},{17,9},... | collective-permute-start | bytes 786440 | tf_op jit(solution)/shard_map/ppermute | solution.py:21
  10.8 43.5 %copy-start.8 = (s32[2]{0:T(128)S(1)}, s32[2]{0:T(128)}, u32[]{:S(2)}) copy-start(s32[2]{0:T(128)} %constant.30) | copy-start | bytes 28
  10.9 43.6 %copy-start.6 = (f32[256,4]{0,1:T(4,128)S(1)}, f32[256,4]{0,1:T(4,128)}, u32[]{:S(2)}) copy-start(f32[256,4]{0,1:T(4,128)} %param.15) | copy-start | bytes 12292
  10.9 44.3 %copy-start.7 = (s32[2]{0:T(128)S(1)}, s32[2]{0:T(128)}, u32[]{:S(2)}) copy-start(s32[2]{0:T(128)} %constant.27) | copy-start | bytes 28
  11.7 52.1 %collective-permute-start.3 = (bf16[4,4,8,1,1024]{4,2,1,0,3:T(8,128)(2,1)}, bf16[4,4,8,1,1024]{4,2,1,0,3:T(8,128)(2,1)}, u32[]{:S(2)}, u32[]{:S(2)}) collective-permute-start(bf16[4,4,8,1,1024]{4,2,1,0,3:T(8,128)(2,1)} %copy.21), channel_id=1, source_target_pairs={{1,0},{2,1},{3,2},{4,3},{5,4},{6,5},{7,6},{9,8},{10,9},{11,10},{12... | collective-permute-start | bytes 786440 | tf_op jit(solution)/shard_map/ppermute | solution.py:332
  13.7 51.5 %collective-permute-start.2 = (bf16[4,4,8,1,1024]{4,2,1,0,3:T(8,128)(2,1)}, bf16[4,4,8,1,1024]{4,2,1,0,3:T(8,128)(2,1)}, u32[]{:S(2)}, u32[]{:S(2)}) collective-permute-start(bf16[4,4,8,1,1024]{4,2,1,0,3:T(8,128)(2,1)} %copy.20), channel_id=1, source_target_pairs={{0,1},{1,2},{2,3},{3,4},{4,5},{5,6},{6,7},{8,9},{9,10},{10,11},{11... | collective-permute-start | bytes 786440 | tf_op jit(solution)/shard_map/ppermute | solution.py:331
  68.4 2.9 %copy-start = (f32[1,4,8,8,1024]{4,3,2,1,0:T(8,128)S(1)}, f32[1,4,8,8,1024]{4,3,2,1,0:T(8,128)}, u32[]{:S(2)}) copy-start(f32[1,4,8,8,1024]{4,3,2,1,0:T(8,128)} %param.11) | copy-start | bytes 3145732
  68.4 2.9 %copy-start.1 = (f32[8,8,1024]{2,1,0:T(8,128)S(1)}, f32[8,8,1024]{2,1,0:T(8,128)}, u32[]{:S(2)}) copy-start(f32[8,8,1024]{2,1,0:T(8,128)} %sound.1) | copy-start | bytes 786436
  68.5 2.9 %copy-start.2 = (f32[3,1024]{1,0:T(4,128)S(1)}, f32[3,1024]{1,0:T(4,128)}, u32[]{:S(2)}) copy-start(f32[3,1024]{1,0:T(4,128)} %wind.1) | copy-start | bytes 36868

commit v5 on v4

--- a/solution.py
+++ b/solution.py
@@ -309,20 +309,29 @@
     width_x, width_y, depth = sound_speed_sq.shape
     slots = residuals.shape[0]
     live = (jnp.arange(slots, dtype=jnp.int32) < pair_counts[0]).astype(jnp.float32)
-    sx, sy, sz, src_inside = local_cells(source_cells, width_x, width_y)
-    rx, ry, rz, rcv_inside = local_cells(receiver_cells, width_x, width_y)
-    local_samples = jnp.stack(
-        [forward_field[t, 0][sx, sy, sz] for t in range(steps_total)]
-    ).astype(jnp.float32) * src_inside[None, :]
+    gx_first = lax.axis_index("gx") * width_x
+    gy_first = lax.axis_index("gy") * width_y
+    x_range = jnp.arange(width_x, dtype=jnp.int32)
+    y_range = jnp.arange(width_y, dtype=jnp.int32)
+    z_range = jnp.arange(depth, dtype=jnp.int32)
+
+    def tile_mask(cells):
+        on_x = (cells[:, 0][None, :] - gx_first) == x_range[:, None]
+        on_y = (cells[:, 1][None, :] - gy_first) == y_range[:, None]
+        return (on_x[:, None, :] & on_y[None, :, :]).astype(jnp.float32)
+
+    source_z = (source_cells[:, 2][None, :] == z_range[:, None]).astype(jnp.bfloat16)
+    along_z = jnp.einsum(
+        "txyz,zn->txyn", forward_field[:, 0], source_z, preferred_element_type=jnp.float32
+    )
+    local_samples = jnp.sum(along_z * tile_mask(source_cells)[None], axis=(1, 2))
     samples = gathered_samples(local_samples)
-    amplitude = jnp.transpose(residuals) * samples * (live * rcv_inside)[None, :]
-    rcv_flat = (rx * width_y + ry) * depth + rz
-    step_index = jnp.broadcast_to(jnp.arange(steps_total)[:, None], amplitude.shape)
-    injected = (
-        jnp.zeros((steps_total, width_x * width_y * depth), jnp.float32)
-        .at[step_index, jnp.broadcast_to(rcv_flat[None, :], amplitude.shape)]
-        .add(amplitude)
-        .reshape(steps_total, width_x, width_y, depth)
+    amplitude = jnp.transpose(residuals) * samples * live[None, :]
+    spread = amplitude[:, None, None, :] * tile_mask(receiver_cells)[None]
+    receiver_z = (receiver_cells[:, 2][:, None] == z_range[None, :]).astype(jnp.float32)
+    injected = jnp.einsum(
+        "txyn,nz->txyz", spread, receiver_z, precision=lax.Precision.HIGHEST,
+        preferred_element_type=jnp.float32,
     )
     lo_x, hi_x = neighbours(forward_field, "gx", 2)
     fpad = jnp.concatenate([lo_x, forward_field, hi_x], axis=2)

time: 141 us -> 119 us (0.84)
  local copies, waits for them, and re-layouts: 24.3 us -> 9.29 us
  other arithmetic: 13.3 us -> 4.28 us
  matrix products: 0 us -> 1.76 us
    gather x4 -> x0, local copies, waits for them, and re-layouts: 11.2 us -> none  [shards(): forward_field[t, 0][sx, sy, sz]]
    unnamed x5 -> x0, other arithmetic: 8.03 us -> none
    dot_general x0 -> x2, matrix products: none -> 1.76 us  [the longest x1 0.99 us: shards(): jnp.einsum('txyz,zn->txyn', forward_field[:, 0], source_z, preferred_elem...]
    unnamed x24 -> x18, local copies, waits for them, and re-layouts: 3.39 us -> 1.98 us
  transfers between devices with their start and end apart: 4 -> 4, of which waited for: 0 -> 0; matrix products, arithmetic and copies ran while one was open for 22% -> 8% of each run, Pallas kernels for 17% -> 20%
where the time goes in v5:
time: 119 us; the launch traced here: 118 us
  Pallas kernels  91.5 us (77%)
  starting transfers between devices  9.81 us (8%)
  local copies, waits for them, and re-layouts  9.29 us (8%)
  other arithmetic  4.28 us (4%)
  matrix products  1.76 us (1%)
  between operations  1.55 us (1%)
    pallas_call x1, Pallas kernels, shards(): pl.pallas_call(kernel, out_shape=(jax.ShapeDtypeStruct((4, width_x, width...  68 us
    pallas_call x1, Pallas kernels, gathered_samples(): pl.pallas_call(functools.partial(samples_kernel, nx, ny), out_shape=jax.S...  23.5 us
    ppermute x1, starting transfers between devices, shards(): lax.ppermute(forward_field[:, :, :, width_y - 1:width_y, :], 'gy', up)  3.74 us
    ppermute x1, starting transfers between devices, neighbours(): before = lax.ppermute(last, axis, up)  3.48 us
    slice x1, local copies, waits for them, and re-layouts, shards(): forward_field[:, :, :, width_y - 1:width_y, :]  3.39 us
  transfers between devices with their start and end apart: 4, of which 0 were waited for; matrix products, arithmetic and copies ran while one was open for 8% of the time, Pallas kernels for 20%

profile of v5, /device:TPU:0, one launch (start us, length us, event | category | flops | bytes accessed | tf_op | source)
XLA Modules:
  0.0 118.2 jit_solution(6155525442336783382)
XLA Ops:
  0.6 0.0 copy-start.3
  0.6 0.0 copy-start.5
  0.7 0.0 copy-start.6
  0.7 2.0 %fusion.16 = (bf16[4,4,1,8,1024]{4,3,2,1,0:T(8,128)(2,1)}, bf16[4,4,1,8,1024]{4,3,2,1,0:T(8,128)(2,1)}) fusion(bf16[4,4,8,8,1024]{4,3,2,1,0:T(8,128)(2,1)} %param.10), kind=kLoop, calls=%fused_computation.31 | loop fusion | bytes 1048576 | tf_op jit(solution)/shard_map/slice | solution.py:18
  2.7 3.5 %collective-permute-start = (bf16[4,4,1,8,1024]{4,3,2,1,0:T(8,128)(2,1)}, bf16[4,4,1,8,1024]{4,3,2,1,0:T(8,128)(2,1)S(1)}, u32[]{:S(2)}, u32[]{:S(2)}) collective-permute-start(bf16[4,4,1,8,1024]{4,3,2,1,0:T(8,128)(2,1)} %get-tuple-element.8), channel_id=1, source_target_pairs={{0,8},{8,16},{16,24},{24,32},{32,40},{40,48},{48,56},{1,9},{9,17},... | collective-permute-start | bytes 786440 | tf_op jit(solution)/shard_map/ppermute | solution.py:20
  6.2 1.3 %collective-permute-start.1 = (bf16[4,4,1,8,1024]{4,3,2,1,0:T(8,128)(2,1)}, bf16[4,4,1,8,1024]{4,3,2,1,0:T(8,128)(2,1)S(1)}, u32[]{:S(2)}, u32[]{:S(2)}) collective-permute-start(bf16[4,4,1,8,1024]{4,3,2,1,0:T(8,128)(2,1)} %get-tuple-element.9), channel_id=1, source_target_pairs={{8,0},{16,8},{24,16},{32,24},{40,32},{48,40},{56,48},{9,1},{17,9},... | collective-permute-start | bytes 786440 | tf_op jit(solution)/shard_map/ppermute | solution.py:21
  7.5 3.4 %fusion.15 = (bf16[4,4,8,1,1024]{4,3,2,1,0:T(2,128)(2,1)S(1)}, bf16[4,4,8,1,1024]{4,3,2,1,0:T(2,128)(2,1)S(1)}) fusion(bf16[4,4,8,8,1024]{4,3,2,1,0:T(8,128)(2,1)} %param.10), kind=kLoop, calls=%fused_computation.30 | loop fusion | bytes 1048576 | tf_op jit(solution)/shard_map/slice | solution.py:340
  10.8 0.1 copy.24
  10.9 1.3 %collective-permute-start.3 = (bf16[4,4,8,1,1024]{4,2,1,0,3:T(8,128)(2,1)S(1)}, bf16[4,4,8,1,1024]{4,2,1,0,3:T(8,128)(2,1)S(1)}, u32[]{:S(2)}, u32[]{:S(2)}) collective-permute-start(bf16[4,4,8,1,1024]{4,2,1,0,3:T(8,128)(2,1)S(1)} %copy.24), channel_id=1, source_target_pairs={{1,0},{2,1},{3,2},{4,3},{5,4},{6,5},{7,6},{9,8},{10,9},{11,10},{12... | collective-permute-start | bytes 786440 | tf_op jit(solution)/shard_map/ppermute | solution.py:341
  12.2 0.1 copy.23
  12.3 3.7 %collective-permute-start.2 = (bf16[4,4,8,1,1024]{4,2,1,0,3:T(8,128)(2,1)S(1)}, bf16[4,4,8,1,1024]{4,2,1,0,3:T(8,128)(2,1)}, u32[]{:S(2)}, u32[]{:S(2)}) collective-permute-start(bf16[4,4,8,1,1024]{4,2,1,0,3:T(8,128)(2,1)S(1)} %copy.23), channel_id=1, source_target_pairs={{0,1},{1,2},{2,3},{3,4},{4,5},{5,6},{6,7},{8,9},{9,10},{10,11},{11... | collective-permute-start | bytes 786440 | tf_op jit(solution)/shard_map/ppermute | solution.py:340
  16.7 0.0 copy-done.5
  16.7 0.0 copy-done.6
  16.8 0.0 copy-done.3
  16.9 0.0 copy-start.4
  16.9 1.0 fusion.1.local_ref
  17.9 23.5 %shard_map.95 = f32[4,256]{1,0:T(4,128)} custom-call(f32[4,256]{1,0:T(4,128)} %fusion.1.local_ref), custom_call_target="tpu_custom_call" | custom-call | tf_op jit(solution)/shard_map/pallas_call | solution.py:283
  41.4 0.0 copy-done.4
  41.4 0.7 fusion.14
  42.1 0.8 fusion.5.inj
  42.8 0.0 collective-permute-done.3
  42.8 0.5 copy.19
  43.3 0.0 collective-permute-done.2
  43.3 1.4 %copy.18 = bf16[4,1,4,8,1,1024]{5,4,3,2,1,0:T(2,128)(2,1)S(1)} copy(bf16[4,1,4,8,1,1024]{5,3,2,0,4,1:T(8,128)(2,1)} %bitcast.1) | data formatting | bytes 524288 | tf_op jit(solution)/shard_map/stack | solution.py:342
  44.8 1.7 %pad_maximum_fusion.1.fyr = bf16[4,2,4,8,1,1024]{5,4,3,2,1,0:T(2,128)(2,1)S(1)} fusion(bf16[4,1,4,8,1,1024]{5,4,3,2,1,0:T(2,128)(2,1)S(1)} %copy.19, bf16[4,1,4,8,1,1024]{5,4,3,2,1,0:T(2,128)(2,1)S(1)} %copy.18), kind=kLoop, calls=%fused_computation.4 | loop fusion | flops 262144 | bytes 1048576 | tf_op jit(solution)/shard_map/stack | solution.py:342
  46.5 0.0 copy-start
  46.5 0.0 copy-start.1
  46.5 0.0 copy-start.2
  46.5 0.0 collective-permute-done
  46.5 0.0 collective-permute-done.1
  46.5 1.8 %pad_maximum_fusion.fpad = bf16[4,4,10,8,1024]{4,3,2,1,0:T(8,128)(2,1)} fusion(bf16[4,4,1,8,1024]{4,3,2,1,0:T(8,128)(2,1)S(1)} %collective-permute-done.1, bf16[4,4,8,8,1024]{4,3,2,1,0:T(8,128)(2,1)S(1)} %copy-done.3, bf16[4,4,1,8,1024]{4,3,2,1,0:T(8,128)(2,1)S(1)} %collective-permute-done), kind=kLoop, calls=%fused_computation | loop fusion | flops 2621440 | bytes 5242880 | tf_op jit(solution)/shard_map/concatenate | solution.py:337
  48.4 0.0 copy-done
  48.4 0.0 copy-done.1
  48.4 0.0 copy-done.2
  48.4 68.0 %shard_map.96 = (f32[4,8,8,1024]{3,2,1,0:T(8,128)S(1)}, f32[4,8,8,512]{3,2,1,0:T(8,128)S(1)}) custom-call(f32[4,8,8,1024]{3,2,1,0:T(8,128)S(1)} %bitcast.38, f32[8,8,1024]{2,1,0:T(8,128)S(1)} %copy-done.1, f32[3,1024]{1,0:T(4,128)S(1)} %copy-done.2, bf16[4,4,10,8,1024]{4,3,2,1,0:T(8,128)(2,1)} %pad_maximum_fusion.fpad, ...), custom_call_target="tpu_custom_call" | custom-call | tf_op jit(solution)/shard_map/pallas_call | solution.py:348
  116.4 0.8 copy.29
  117.2 1.0 copy.30
  (8 shorter events, 0.1 us)
Async XLA Ops:
  0.6 16.2 %copy-start.3 = (bf16[4,4,8,8,1024]{4,3,2,1,0:T(8,128)(2,1)S(1)}, bf16[4,4,8,8,1024]{4,3,2,1,0:T(8,128)(2,1)}, u32[]{:S(2)}) copy-start(bf16[4,4,8,8,1024]{4,3,2,1,0:T(8,128)(2,1)} %param.10) | copy-start | bytes 6291460
  0.6 16.1 %copy-start.5 = (s32[256,3]{0,1:T(4,128)S(1)}, s32[256,3]{0,1:T(4,128)}, u32[]{:S(2)}) copy-start(s32[256,3]{0,1:T(4,128)} %param.14) | copy-start | bytes 9220
  0.7 16.1 %copy-start.6 = (s32[256,3]{0,1:T(4,128)S(1)}, s32[256,3]{0,1:T(4,128)}, u32[]{:S(2)}) copy-start(s32[256,3]{0,1:T(4,128)} %param.13) | copy-start | bytes 9220
  2.7 43.9 %collective-permute-start = (bf16[4,4,1,8,1024]{4,3,2,1,0:T(8,128)(2,1)}, bf16[4,4,1,8,1024]{4,3,2,1,0:T(8,128)(2,1)S(1)}, u32[]{:S(2)}, u32[]{:S(2)}) collective-permute-start(bf16[4,4,1,8,1024]{4,3,2,1,0:T(8,128)(2,1)} %get-tuple-element.8), channel_id=1, source_target_pairs={{0,8},{8,16},{16,24},{24,32},{32,40},{40,48},{48,56},{1,9},{9,17},... | collective-permute-start | bytes 786440 | tf_op jit(solution)/shard_map/ppermute | solution.py:20
  6.2 40.4 %collective-permute-start.1 = (bf16[4,4,1,8,1024]{4,3,2,1,0:T(8,128)(2,1)}, bf16[4,4,1,8,1024]{4,3,2,1,0:T(8,128)(2,1)S(1)}, u32[]{:S(2)}, u32[]{:S(2)}) collective-permute-start(bf16[4,4,1,8,1024]{4,3,2,1,0:T(8,128)(2,1)} %get-tuple-element.9), channel_id=1, source_target_pairs={{8,0},{16,8},{24,16},{32,24},{40,32},{48,40},{56,48},{9,1},{17,9},... | collective-permute-start | bytes 786440 | tf_op jit(solution)/shard_map/ppermute | solution.py:21
  10.9 31.9 %collective-permute-start.3 = (bf16[4,4,8,1,1024]{4,2,1,0,3:T(8,128)(2,1)S(1)}, bf16[4,4,8,1,1024]{4,2,1,0,3:T(8,128)(2,1)S(1)}, u32[]{:S(2)}, u32[]{:S(2)}) collective-permute-start(bf16[4,4,8,1,1024]{4,2,1,0,3:T(8,128)(2,1)S(1)} %copy.24), channel_id=1, source_target_pairs={{1,0},{2,1},{3,2},{4,3},{5,4},{6,5},{7,6},{9,8},{10,9},{11,10},{12... | collective-permute-start | bytes 786440 | tf_op jit(solution)/shard_map/ppermute | solution.py:341
  12.3 31.0 %collective-permute-start.2 = (bf16[4,4,8,1,1024]{4,2,1,0,3:T(8,128)(2,1)S(1)}, bf16[4,4,8,1,1024]{4,2,1,0,3:T(8,128)(2,1)}, u32[]{:S(2)}, u32[]{:S(2)}) collective-permute-start(bf16[4,4,8,1,1024]{4,2,1,0,3:T(8,128)(2,1)S(1)} %copy.23), channel_id=1, source_target_pairs={{0,1},{1,2},{2,3},{3,4},{4,5},{5,6},{6,7},{8,9},{9,10},{10,11},{11... | collective-permute-start | bytes 786440 | tf_op jit(solution)/shard_map/ppermute | solution.py:340
  16.9 24.5 %copy-start.4 = (f32[256,4]{0,1:T(4,128)S(1)}, f32[256,4]{0,1:T(4,128)}, u32[]{:S(2)}) copy-start(f32[256,4]{0,1:T(4,128)} %param.15) | copy-start | bytes 12292
  46.5 1.9 %copy-start = (f32[1,4,8,8,1024]{4,3,2,1,0:T(8,128)S(1)}, f32[1,4,8,8,1024]{4,3,2,1,0:T(8,128)}, u32[]{:S(2)}) copy-start(f32[1,4,8,8,1024]{4,3,2,1,0:T(8,128)} %param.11) | copy-start | bytes 3145732
  46.5 1.9 %copy-start.1 = (f32[8,8,1024]{2,1,0:T(8,128)S(1)}, f32[8,8,1024]{2,1,0:T(8,128)}, u32[]{:S(2)}) copy-start(f32[8,8,1024]{2,1,0:T(8,128)} %sound.1) | copy-start | bytes 786436
  46.5 1.9 %copy-start.2 = (f32[3,1024]{1,0:T(4,128)S(1)}, f32[3,1024]{1,0:T(4,128)}, u32[]{:S(2)}) copy-start(f32[3,1024]{1,0:T(4,128)} %wind.1) | copy-start | bytes 36868

commit v6 on v5

--- a/solution.py
+++ b/solution.py
@@ -240,44 +240,40 @@
     lax.fori_loop(0, width_x, add_partner, 0)
 
 
-def samples_kernel(nx, ny, local_ref, out_ref, sent, got, send_sem, recv_sem):
+def samples_kernel(nx, ny, local_ref, out_ref, sent, got_x, got_y, send_sem, recv_sem):
     me_p = lax.axis_index("pair")
     gx = lax.axis_index("gx")
     gy = lax.axis_index("gy")
-    rounds = []
-    k = 1
-    while k < nx:
-        rounds.append((me_p, gx + k - 2 * k * ((gx // k) % 2), gy))
-        k *= 2
-    k = 1
-    while k < ny:
-        rounds.append((me_p, gx, gy + k - 2 * k * ((gy // k) % 2)))
-        k *= 2
+    peers_x = [(me_p, (gx + d) % nx, gy) for d in range(1, nx)]
+    peers_y = [(me_p, gx, (gy + d) % ny) for d in range(1, ny)]
     barrier = pltpu.get_barrier_semaphore()
-    for dev in rounds:
+    for dev in peers_x + peers_y:
         pl.semaphore_signal(barrier, 1, device_id=dev, device_id_type=MESH)
-    pl.semaphore_wait(barrier, len(rounds))
+    pl.semaphore_wait(barrier, len(peers_x) + len(peers_y))
+    rounds = ((local_ref, got_x, peers_x, 0), (sent, got_y, peers_y, nx - 1))
     total = local_ref[...]
-    for r, dev in enumerate(rounds):
-        src = local_ref
-        if r > 0:
-            sent[r] = total
-            src = sent.at[r]
-        copy = pltpu.make_async_remote_copy(
-            src_ref=src, dst_ref=got.at[r], send_sem=send_sem.at[r], recv_sem=recv_sem.at[r],
-            device_id=dev, device_id_type=MESH,
-        )
-        copy.start()
-        copy.wait_send()
-        copy.wait_recv()
-        total = total + got[r]
+    for src, got, peers, base in rounds:
+        copies = []
+        for i, dev in enumerate(peers):
+            copy = pltpu.make_async_remote_copy(
+                src_ref=src, dst_ref=got.at[i], send_sem=send_sem.at[base + i],
+                recv_sem=recv_sem.at[base + i], device_id=dev, device_id_type=MESH,
+            )
+            copy.start()
+            copies.append(copy)
+        for copy in copies:
+            copy.wait_send()
+            copy.wait_recv()
+        for i in range(len(peers)):
+            total = total + got[i]
+        if base == 0:
+            sent[...] = total
     out_ref[...] = total
 
 
 def gathered_samples(local_samples):
     nx, ny = lax.axis_size("gx"), lax.axis_size("gy")
-    rounds = (nx.bit_length() - 1) + (ny.bit_length() - 1)
-    if (nx & (nx - 1)) or (ny & (ny - 1)) or rounds == 0:
+    if nx < 2 or ny < 2:
         return lax.psum(local_samples, ("gx", "gy"))
     vmem = pl.BlockSpec(memory_space=pltpu.VMEM)
     return pl.pallas_call(
@@ -286,10 +282,11 @@
         in_specs=[vmem],
         out_specs=vmem,
         scratch_shapes=[
-            pltpu.VMEM((rounds,) + local_samples.shape, jnp.float32),
-            pltpu.VMEM((rounds,) + local_samples.shape, jnp.float32),
-            pltpu.SemaphoreType.DMA((rounds,)),
-            pltpu.SemaphoreType.DMA((rounds,)),
+            pltpu.VMEM(local_samples.shape, jnp.float32),
+            pltpu.VMEM((nx - 1,) + local_samples.shape, jnp.float32),
+            pltpu.VMEM((ny - 1,) + local_samples.shape, jnp.float32),
+            pltpu.SemaphoreType.DMA((nx + ny - 2,)),
+            pltpu.SemaphoreType.DMA((nx + ny - 2,)),
         ],
         compiler_params=pltpu.CompilerParams(collective_id=1, has_side_effects=True),
     )(local_samples)

time: 119 us -> 112 us (0.941)
  Pallas kernels: 91.5 us -> 85.2 us
    pallas_call x1, Pallas kernels: 23.5 us -> 15.6 us  [gathered_samples(): pl.pallas_call(functools.partial(samples_kernel, nx, ny), out_shape=jax.S...]
    pallas_call x1, Pallas kernels: 68 us -> 69.6 us  [shards(): pl.pallas_call(kernel, out_shape=(jax.ShapeDtypeStruct((4, width_x, width...]
  transfers between devices with their start and end apart: 4 -> 4, of which waited for: 0 -> 0; matrix products, arithmetic and copies ran while one was open for 8% -> 9% of each run, Pallas kernels for 20% -> 14%
where the time goes in v6:
time: 112 us
  Pallas kernels  85.2 us (76%)
  starting transfers between devices  9.81 us (9%)
  local copies, waits for them, and re-layouts  9.29 us (8%)
  other arithmetic  4.28 us (4%)
  matrix products  1.76 us (2%)
  between operations  1.55 us (1%)
    pallas_call x1, Pallas kernels, shards(): pl.pallas_call(kernel, out_shape=(jax.ShapeDtypeStruct((4, width_x, width...  69.6 us
    pallas_call x1, Pallas kernels, gathered_samples(): pl.pallas_call(functools.partial(samples_kernel, nx, ny), out_shape=jax.S...  15.6 us
    ppermute x1, starting transfers between devices, shards(): lax.ppermute(forward_field[:, :, :, width_y - 1:width_y, :], 'gy', up)  3.74 us
    ppermute x1, starting transfers between devices, neighbours(): before = lax.ppermute(last, axis, up)  3.48 us
    slice x1, local copies, waits for them, and re-layouts, shards(): forward_field[:, :, :, width_y - 1:width_y, :]  3.39 us
  transfers between devices with their start and end apart: 4, of which 0 were waited for; matrix products, arithmetic and copies ran while one was open for 9% of the time, Pallas kernels for 14%

profile of v6, /device:TPU:0, one launch (start us, length us, event | category | flops | bytes accessed | tf_op | source)
XLA Modules:
  0.0 111.9 jit_solution(6786279415967526108)
XLA Ops:
  0.6 0.0 copy-start.3
  0.6 0.0 copy-start.5
  0.7 0.0 copy-start.6
  0.7 2.0 %fusion.16 = (bf16[4,4,1,8,1024]{4,3,2,1,0:T(8,128)(2,1)}, bf16[4,4,1,8,1024]{4,3,2,1,0:T(8,128)(2,1)}) fusion(bf16[4,4,8,8,1024]{4,3,2,1,0:T(8,128)(2,1)} %param.10), kind=kLoop, calls=%fused_computation.31 | loop fusion | bytes 1048576 | tf_op jit(solution)/shard_map/slice | solution.py:18
  2.7 3.5 %collective-permute-start = (bf16[4,4,1,8,1024]{4,3,2,1,0:T(8,128)(2,1)}, bf16[4,4,1,8,1024]{4,3,2,1,0:T(8,128)(2,1)S(1)}, u32[]{:S(2)}, u32[]{:S(2)}) collective-permute-start(bf16[4,4,1,8,1024]{4,3,2,1,0:T(8,128)(2,1)} %get-tuple-element.8), channel_id=1, source_target_pairs={{0,8},{8,16},{16,24},{24,32},{32,40},{40,48},{48,56},{1,9},{9,17},... | collective-permute-start | bytes 786440 | tf_op jit(solution)/shard_map/ppermute | solution.py:20
  6.2 1.3 %collective-permute-start.1 = (bf16[4,4,1,8,1024]{4,3,2,1,0:T(8,128)(2,1)}, bf16[4,4,1,8,1024]{4,3,2,1,0:T(8,128)(2,1)S(1)}, u32[]{:S(2)}, u32[]{:S(2)}) collective-permute-start(bf16[4,4,1,8,1024]{4,3,2,1,0:T(8,128)(2,1)} %get-tuple-element.9), channel_id=1, source_target_pairs={{8,0},{16,8},{24,16},{32,24},{40,32},{48,40},{56,48},{9,1},{17,9},... | collective-permute-start | bytes 786440 | tf_op jit(solution)/shard_map/ppermute | solution.py:21
  7.5 3.4 %fusion.15 = (bf16[4,4,8,1,1024]{4,3,2,1,0:T(2,128)(2,1)S(1)}, bf16[4,4,8,1,1024]{4,3,2,1,0:T(2,128)(2,1)S(1)}) fusion(bf16[4,4,8,8,1024]{4,3,2,1,0:T(8,128)(2,1)} %param.10), kind=kLoop, calls=%fused_computation.30 | loop fusion | bytes 1048576 | tf_op jit(solution)/shard_map/slice | solution.py:337
  10.8 0.1 copy.24
  10.9 1.3 %collective-permute-start.3 = (bf16[4,4,8,1,1024]{4,2,1,0,3:T(8,128)(2,1)S(1)}, bf16[4,4,8,1,1024]{4,2,1,0,3:T(8,128)(2,1)S(1)}, u32[]{:S(2)}, u32[]{:S(2)}) collective-permute-start(bf16[4,4,8,1,1024]{4,2,1,0,3:T(8,128)(2,1)S(1)} %copy.24), channel_id=1, source_target_pairs={{1,0},{2,1},{3,2},{4,3},{5,4},{6,5},{7,6},{9,8},{10,9},{11,10},{12... | collective-permute-start | bytes 786440 | tf_op jit(solution)/shard_map/ppermute | solution.py:338
  12.2 0.1 copy.23
  12.3 3.7 %collective-permute-start.2 = (bf16[4,4,8,1,1024]{4,2,1,0,3:T(8,128)(2,1)S(1)}, bf16[4,4,8,1,1024]{4,2,1,0,3:T(8,128)(2,1)}, u32[]{:S(2)}, u32[]{:S(2)}) collective-permute-start(bf16[4,4,8,1,1024]{4,2,1,0,3:T(8,128)(2,1)S(1)} %copy.23), channel_id=1, source_target_pairs={{0,1},{1,2},{2,3},{3,4},{4,5},{5,6},{6,7},{8,9},{9,10},{10,11},{11... | collective-permute-start | bytes 786440 | tf_op jit(solution)/shard_map/ppermute | solution.py:337
  16.7 0.0 copy-done.5
  16.7 0.0 copy-done.6
  16.8 0.0 copy-done.3
  16.9 0.0 copy-start.4
  16.9 1.0 fusion.1.local_ref
  17.9 15.6 %shard_map.95 = f32[4,256]{1,0:T(4,128)} custom-call(f32[4,256]{1,0:T(4,128)} %fusion.1.local_ref), custom_call_target="tpu_custom_call" | custom-call | tf_op jit(solution)/shard_map/pallas_call | solution.py:279
  33.5 0.0 copy-done.4
  33.5 0.7 fusion.14
  34.2 0.8 fusion.5.inj
  34.9 0.0 collective-permute-done.3
  35.0 0.5 copy.19
  35.4 0.0 collective-permute-done.2
  35.5 1.4 %copy.18 = bf16[4,1,4,8,1,1024]{5,4,3,2,1,0:T(2,128)(2,1)S(1)} copy(bf16[4,1,4,8,1,1024]{5,3,2,0,4,1:T(8,128)(2,1)} %bitcast.1) | data formatting | bytes 524288 | tf_op jit(solution)/shard_map/stack | solution.py:339
  36.9 1.7 %pad_maximum_fusion.1.fyr = bf16[4,2,4,8,1,1024]{5,4,3,2,1,0:T(2,128)(2,1)S(1)} fusion(bf16[4,1,4,8,1,1024]{5,4,3,2,1,0:T(2,128)(2,1)S(1)} %copy.19, bf16[4,1,4,8,1,1024]{5,4,3,2,1,0:T(2,128)(2,1)S(1)} %copy.18), kind=kLoop, calls=%fused_computation.4 | loop fusion | flops 262144 | bytes 1048576 | tf_op jit(solution)/shard_map/stack | solution.py:339
  38.6 0.0 copy-start
  38.6 0.0 copy-start.1
  38.6 0.0 copy-start.2
  38.6 0.0 collective-permute-done
  38.7 0.0 collective-permute-done.1
  38.7 1.8 %pad_maximum_fusion.fpad = bf16[4,4,10,8,1024]{4,3,2,1,0:T(8,128)(2,1)} fusion(bf16[4,4,1,8,1024]{4,3,2,1,0:T(8,128)(2,1)S(1)} %collective-permute-done.1, bf16[4,4,8,8,1024]{4,3,2,1,0:T(8,128)(2,1)S(1)} %copy-done.3, bf16[4,4,1,8,1024]{4,3,2,1,0:T(8,128)(2,1)S(1)} %collective-permute-done), kind=kLoop, calls=%fused_computation | loop fusion | flops 2621440 | bytes 5242880 | tf_op jit(solution)/shard_map/concatenate | solution.py:334
  40.5 0.0 copy-done
  40.5 0.0 copy-done.1
  40.5 0.0 copy-done.2
  40.5 69.6 %shard_map.96 = (f32[4,8,8,1024]{3,2,1,0:T(8,128)S(1)}, f32[4,8,8,512]{3,2,1,0:T(8,128)S(1)}) custom-call(f32[4,8,8,1024]{3,2,1,0:T(8,128)S(1)} %bitcast.38, f32[8,8,1024]{2,1,0:T(8,128)S(1)} %copy-done.1, f32[3,1024]{1,0:T(4,128)S(1)} %copy-done.2, bf16[4,4,10,8,1024]{4,3,2,1,0:T(8,128)(2,1)} %pad_maximum_fusion.fpad, ...), custom_call_target="tpu_custom_call" | custom-call | tf_op jit(solution)/shard_map/pallas_call | solution.py:345
  110.1 0.8 copy.29
  110.9 1.0 copy.30
  (8 shorter events, 0.1 us)
Async XLA Ops:
  0.6 16.2 %copy-start.3 = (bf16[4,4,8,8,1024]{4,3,2,1,0:T(8,128)(2,1)S(1)}, bf16[4,4,8,8,1024]{4,3,2,1,0:T(8,128)(2,1)}, u32[]{:S(2)}) copy-start(bf16[4,4,8,8,1024]{4,3,2,1,0:T(8,128)(2,1)} %param.10) | copy-start | bytes 6291460
  0.6 16.1 %copy-start.5 = (s32[256,3]{0,1:T(4,128)S(1)}, s32[256,3]{0,1:T(4,128)}, u32[]{:S(2)}) copy-start(s32[256,3]{0,1:T(4,128)} %param.14) | copy-start | bytes 9220
  0.7 16.1 %copy-start.6 = (s32[256,3]{0,1:T(4,128)S(1)}, s32[256,3]{0,1:T(4,128)}, u32[]{:S(2)}) copy-start(s32[256,3]{0,1:T(4,128)} %param.13) | copy-start | bytes 9220
  2.7 36.0 %collective-permute-start = (bf16[4,4,1,8,1024]{4,3,2,1,0:T(8,128)(2,1)}, bf16[4,4,1,8,1024]{4,3,2,1,0:T(8,128)(2,1)S(1)}, u32[]{:S(2)}, u32[]{:S(2)}) collective-permute-start(bf16[4,4,1,8,1024]{4,3,2,1,0:T(8,128)(2,1)} %get-tuple-element.8), channel_id=1, source_target_pairs={{0,8},{8,16},{16,24},{24,32},{32,40},{40,48},{48,56},{1,9},{9,17},... | collective-permute-start | bytes 786440 | tf_op jit(solution)/shard_map/ppermute | solution.py:20
  6.2 32.5 %collective-permute-start.1 = (bf16[4,4,1,8,1024]{4,3,2,1,0:T(8,128)(2,1)}, bf16[4,4,1,8,1024]{4,3,2,1,0:T(8,128)(2,1)S(1)}, u32[]{:S(2)}, u32[]{:S(2)}) collective-permute-start(bf16[4,4,1,8,1024]{4,3,2,1,0:T(8,128)(2,1)} %get-tuple-element.9), channel_id=1, source_target_pairs={{8,0},{16,8},{24,16},{32,24},{40,32},{48,40},{56,48},{9,1},{17,9},... | collective-permute-start | bytes 786440 | tf_op jit(solution)/shard_map/ppermute | solution.py:21
  10.9 24.0 %collective-permute-start.3 = (bf16[4,4,8,1,1024]{4,2,1,0,3:T(8,128)(2,1)S(1)}, bf16[4,4,8,1,1024]{4,2,1,0,3:T(8,128)(2,1)S(1)}, u32[]{:S(2)}, u32[]{:S(2)}) collective-permute-start(bf16[4,4,8,1,1024]{4,2,1,0,3:T(8,128)(2,1)S(1)} %copy.24), channel_id=1, source_target_pairs={{1,0},{2,1},{3,2},{4,3},{5,4},{6,5},{7,6},{9,8},{10,9},{11,10},{12... | collective-permute-start | bytes 786440 | tf_op jit(solution)/shard_map/ppermute | solution.py:338
  12.3 23.1 %collective-permute-start.2 = (bf16[4,4,8,1,1024]{4,2,1,0,3:T(8,128)(2,1)S(1)}, bf16[4,4,8,1,1024]{4,2,1,0,3:T(8,128)(2,1)}, u32[]{:S(2)}, u32[]{:S(2)}) collective-permute-start(bf16[4,4,8,1,1024]{4,2,1,0,3:T(8,128)(2,1)S(1)} %copy.23), channel_id=1, source_target_pairs={{0,1},{1,2},{2,3},{3,4},{4,5},{5,6},{6,7},{8,9},{9,10},{10,11},{11... | collective-permute-start | bytes 786440 | tf_op jit(solution)/shard_map/ppermute | solution.py:337
  16.9 16.6 %copy-start.4 = (f32[256,4]{0,1:T(4,128)S(1)}, f32[256,4]{0,1:T(4,128)}, u32[]{:S(2)}) copy-start(f32[256,4]{0,1:T(4,128)} %param.15) | copy-start | bytes 12292
  38.6 1.9 %copy-start = (f32[1,4,8,8,1024]{4,3,2,1,0:T(8,128)S(1)}, f32[1,4,8,8,1024]{4,3,2,1,0:T(8,128)}, u32[]{:S(2)}) copy-start(f32[1,4,8,8,1024]{4,3,2,1,0:T(8,128)} %param.11) | copy-start | bytes 3145732
  38.6 1.9 %copy-start.1 = (f32[8,8,1024]{2,1,0:T(8,128)S(1)}, f32[8,8,1024]{2,1,0:T(8,128)}, u32[]{:S(2)}) copy-start(f32[8,8,1024]{2,1,0:T(8,128)} %sound.1) | copy-start | bytes 786436
  38.6 1.9 %copy-start.2 = (f32[3,1024]{1,0:T(4,128)S(1)}, f32[3,1024]{1,0:T(4,128)}, u32[]{:S(2)}) copy-start(f32[3,1024]{1,0:T(4,128)} %wind.1) | copy-start | bytes 36868

commit v7 on v6

--- a/solution.py
+++ b/solution.py
@@ -36,9 +36,10 @@
 
 def stencil_kernel(
     nx, ny, steps,
-    state_in, sound, wind, fpad, fyr, inj,
+    state_in, sound, wind, forward, inj,
     state_out, kernel_out,
-    pads, pbuf, ysend, yrecv, ypsend, yprecv, acc_out, ksend, krecv, ss, rs, ps, pr, ks, kr,
+    pads, pbuf, ysend, yrecv, ypsend, yprecv, acc_out, ksend, krecv, fpad, fysend, fyr,
+    ss, rs, ps, pr, ks, kr, fs, fr, local_sem,
 ):
     _, width_x, width_y, depth = state_in.shape
     me_p = lax.axis_index("pair")
@@ -64,6 +65,25 @@
                 yrecv[par, side, c] = jnp.zeros((width_x, 1, depth), jnp.float32)
     pbuf[0] = zero_slab
     pbuf[width_x + 1] = zero_slab
+    zero_forward = jnp.zeros((width_y, depth), fpad.dtype)
+    for t in range(steps):
+        for c in range(4):
+            fpad[t, c, 0] = zero_forward
+            fpad[t, c, width_x + 1] = zero_forward
+            for side in range(2):
+                fyr[side, t, c] = jnp.zeros((width_x, 1, depth), jnp.float32)
+
+    def forward_rows(x, carry):
+        for t in range(steps):
+            for c in range(4):
+                f = forward[t, c, x].astype(jnp.float32)
+                fysend[0, t, c, x] = f[width_y - 1:width_y, :]
+                fysend[1, t, c, x] = f[0:1, :]
+        return carry
+
+    lax.fori_loop(0, width_x, forward_rows, 0)
+    interior = pltpu.make_async_copy(forward, fpad.at[:, :, pl.ds(1, width_x)], local_sem.at[0])
+    interior.start()
     for side in range(2):
         yprecv[side] = jnp.zeros((width_x, 1, depth), jnp.float32)
 
@@ -122,6 +142,23 @@
             @pl.when(arrives)
             def _():
                 copy.wait_recv()
+
+    forward_copies = []
+    for cond, src, dst, slot, dev in (
+        (has_hi_x, forward.at[:, :, pl.ds(width_x - 1, 1)], fpad.at[:, :, pl.ds(0, 1)], 0, dev_hi_x),
+        (has_lo_x, forward.at[:, :, pl.ds(0, 1)], fpad.at[:, :, pl.ds(width_x + 1, 1)], 1, dev_lo_x),
+        (has_hi_y, fysend.at[0], fyr.at[0], 2, dev_hi_y),
+        (has_lo_y, fysend.at[1], fyr.at[1], 3, dev_lo_y),
+    ):
+        copy = pltpu.make_async_remote_copy(
+            src_ref=src, dst_ref=dst, send_sem=fs.at[slot], recv_sem=fr.at[slot],
+            device_id=dev, device_id_type=MESH,
+        )
+        forward_copies.append((cond, copy))
+
+        @pl.when(cond)
+        def _():
+            copy.start()
 
     def fill_state(par, x, c, v):
         pads[par, c, x + 1] = v
@@ -169,6 +206,16 @@
             return carry
 
         lax.fori_loop(0, width_x, pressure_slab, 0)
+        if step == 0:
+            interior.wait()
+            for (cond, copy), arrives in zip(forward_copies, (has_lo_x, has_hi_x, has_lo_y, has_hi_y)):
+                @pl.when(cond)
+                def _():
+                    copy.wait_send()
+
+                @pl.when(arrives)
+                def _():
+                    copy.wait_recv()
         exchange(
             pbuf.at[pl.ds(1, 1)], pbuf.at[pl.ds(width_x, 1)],
             pbuf.at[pl.ds(0, 1)], pbuf.at[pl.ds(width_x + 1, 1)],
@@ -196,7 +243,7 @@
             for c in range(4):
                 f = fpad[snap, c, xp].astype(jnp.float32)
                 fe.append((fpad[snap, c, xp + 1].astype(jnp.float32) - fpad[snap, c, x].astype(jnp.float32)) * 0.5)
-                fn.append(dy(f, fyr[snap, 0, c, x].astype(jnp.float32), fyr[snap, 1, c, x].astype(jnp.float32)))
+                fn.append(dy(f, fyr[0, snap, c, x], fyr[1, snap, c, x]))
                 fu.append(dz(f))
             pieces = [p_new * (fe[1] + fn[2] + fu[3])]
             for along in (fe, fn, fu):
@@ -330,14 +377,6 @@
         "txyn,nz->txyz", spread, receiver_z, precision=lax.Precision.HIGHEST,
         preferred_element_type=jnp.float32,
     )
-    lo_x, hi_x = neighbours(forward_field, "gx", 2)
-    fpad = jnp.concatenate([lo_x, forward_field, hi_x], axis=2)
-    up = [(i, i + 1) for i in range(lax.axis_size("gy") - 1)]
-    down = [(i + 1, i) for i in range(lax.axis_size("gy") - 1)]
-    lo_y = lax.ppermute(forward_field[:, :, :, width_y - 1:width_y, :], "gy", up)
-    hi_y = lax.ppermute(forward_field[:, :, :, 0:1, :], "gy", down)
-    fyr = jnp.stack([lo_y, hi_y], axis=1)
-
     vmem = pl.BlockSpec(memory_space=pltpu.VMEM)
     kernel = functools.partial(
         stencil_kernel, lax.axis_size("gx"), lax.axis_size("gy"), steps_total
@@ -348,7 +387,7 @@
             jax.ShapeDtypeStruct((4, width_x, width_y, depth), jnp.float32),
             jax.ShapeDtypeStruct((4, width_x, width_y, depth // 2), jnp.float32),
         ),
-        in_specs=[vmem] * 6,
+        in_specs=[vmem] * 5,
         out_specs=(vmem, vmem),
         scratch_shapes=[
             pltpu.VMEM((2, 4, width_x + 2, width_y, depth), jnp.float32),
@@ -360,17 +399,23 @@
             pltpu.VMEM((4, width_x, width_y, depth), jnp.float32),
             pltpu.VMEM((width_x, 4, width_y, depth // 2), jnp.float32),
             pltpu.VMEM((width_x, 4, width_y, depth // 2), jnp.float32),
+            pltpu.VMEM((steps_total, 4, width_x + 2, width_y, depth), forward_field.dtype),
+            pltpu.VMEM((2, steps_total, 4, width_x, 1, depth), jnp.float32),
+            pltpu.VMEM((2, steps_total, 4, width_x, 1, depth), jnp.float32),
             pltpu.SemaphoreType.DMA((2, 4)),
             pltpu.SemaphoreType.DMA((2, 4)),
             pltpu.SemaphoreType.DMA((4,)),
             pltpu.SemaphoreType.DMA((4,)),
             pltpu.SemaphoreType.DMA((width_x,)),
             pltpu.SemaphoreType.DMA((width_x,)),
+            pltpu.SemaphoreType.DMA((4,)),
+            pltpu.SemaphoreType.DMA((4,)),
+            pltpu.SemaphoreType.DMA((1,)),
         ],
         compiler_params=pltpu.CompilerParams(
             collective_id=0, has_side_effects=True, vmem_limit_bytes=48 * 1024 * 1024
         ),
-    )(adjoint_state[0], sound_speed_sq, wind_profile, fpad, fyr, injected)
+    )(adjoint_state[0], sound_speed_sq, wind_profile, forward_field, injected)
     return (kernels, state_new[None])
 
 

time: 112 us -> 102 us (0.911)
  starting transfers between devices: 9.81 us -> 0 us
  Pallas kernels: 85.2 us -> 93.6 us
  local copies, waits for them, and re-layouts: 9.29 us -> 1.8 us
  other arithmetic: 4.28 us -> 1.55 us
  matrix products: 1.76 us -> 2.96 us
    ppermute x4 -> x0, starting transfers between devices: 9.81 us -> none  [the longest x1 3.74 us: shards(): lax.ppermute(forward_field[:, :, :, width_y - 1:width_y, :], 'gy', up)]
    pallas_call x1, Pallas kernels: 69.6 us -> 79.1 us  [shards(): pl.pallas_call(kernel, out_shape=(jax.ShapeDtypeStruct((4, width_x, width...]
    slice x2 -> x0, local copies, waits for them, and re-layouts: 5.39 us -> none  [the longest x1 3.39 us: shards(): forward_field[:, :, :, width_y - 1:width_y, :]]
    another operation x2 -> x0, local copies, waits for them, and re-layouts: 1.93 us -> none  [shards(): fyr = jnp.stack([lo_y, hi_y], axis=1)]
    concatenate x1 -> x0, other arithmetic: 1.84 us -> none  [shards(): fpad = jnp.concatenate([lo_x, forward_field, hi_x], axis=2)]
    another operation x1 -> x0, other arithmetic: 1.69 us -> none  [shards(): fyr = jnp.stack([lo_y, hi_y], axis=1)]
    dot_general x1, matrix products: 0.99 us -> 2.19 us  [shards(): jnp.einsum('txyz,zn->txyn', forward_field[:, 0], source_z, preferred_elem...]
  transfers between devices with their start and end apart: 4 -> 0, of which waited for: 0 -> 0; matrix products, arithmetic and copies ran while one was open for 9% -> 0% of each run, Pallas kernels for 14% -> 0%
where the time goes in v7:
time: 102 us; the launch traced here: 101 us
  Pallas kernels  93.6 us (92%)
  matrix products  2.96 us (3%)
  local copies, waits for them, and re-layouts  1.8 us (2%)
  other arithmetic  1.55 us (2%)
  between operations  1.43 us (1%)
    pallas_call x1, Pallas kernels, shards(): pl.pallas_call(kernel, out_shape=(jax.ShapeDtypeStruct((4, width_x, width...  79.1 us
    pallas_call x1, Pallas kernels, gathered_samples(): pl.pallas_call(functools.partial(samples_kernel, nx, ny), out_shape=jax.S...  14.6 us
    dot_general x1, matrix products, shards(): jnp.einsum('txyz,zn->txyn', forward_field[:, 0], source_z, preferred_elem...  2.19 us

profile of v7, /device:TPU:0, one launch (start us, length us, event | category | flops | bytes accessed | tf_op | source)
XLA Modules:
  0.0 101.4 jit_solution(3186953292121178150)
XLA Ops:
  1.3 0.8 slice_subtract_fusion.1
  2.2 0.0 copy-start.4
  2.2 0.0 copy-start
  2.2 0.0 copy-start.1
  2.2 0.0 copy-start.2
  2.2 0.0 copy-start.3
  2.2 2.2 %fusion.1.local_ref = f32[4,256]{1,0:T(4,128)} fusion(bf16[4,4,8,8,1024]{4,3,2,1,0:T(8,128)(2,1)} %forward.1, s32[256]{0:T(256)S(1)} %bitcast.40, f32[8,8,256]{2,1,0:T(8,128)S(1)} %and_convert_fusion.1), kind=kOutput, calls=%fused_computation.2 | convolution fusion | flops 134609920 | bytes 594944 | tf_op jit(solution)/shard_map/txyz,zn->txyn/dot_general | solution.py:368
  4.4 14.6 %shard_map.95 = f32[4,256]{1,0:T(4,128)} custom-call(f32[4,256]{1,0:T(4,128)} %fusion.1.local_ref), custom_call_target="tpu_custom_call" | custom-call | tf_op jit(solution)/shard_map/pallas_call | solution.py:326
  19.0 0.0 copy-done.4
  19.0 0.7 fusion.14
  19.7 0.8 fusion.5.inj
  20.5 0.0 copy-done
  20.5 0.0 copy-done.1
  20.5 0.0 copy-done.2
  20.5 0.0 copy-done.3
  20.5 79.1 %shard_map.96 = (f32[4,8,8,1024]{3,2,1,0:T(8,128)S(1)}, f32[4,8,8,512]{3,2,1,0:T(8,128)S(1)}) custom-call(f32[4,8,8,1024]{3,2,1,0:T(8,128)S(1)} %bitcast.33, f32[8,8,1024]{2,1,0:T(8,128)S(1)} %copy-done.2, f32[3,1024]{1,0:T(4,128)S(1)} %copy-done.3, bf16[4,4,8,8,1024]{4,3,2,1,0:T(8,128)(2,1)S(1)} %copy-done, f32[4,8,8,1024]{3,2,1,0:T(8,128)S(1)} %fusion.5.inj), custom_call_target="tpu_custom_call" | custom-call | tf_op jit(solution)/shard_map/pallas_call | solution.py:384
  99.6 0.8 copy.15
  100.4 1.0 copy.16
  (7 shorter events, 0.1 us)
Async XLA Ops:
  2.2 16.8 %copy-start.4 = (f32[256,4]{0,1:T(4,128)S(1)}, f32[256,4]{0,1:T(4,128)}, u32[]{:S(2)}) copy-start(f32[256,4]{0,1:T(4,128)} %param.15) | copy-start | bytes 12292
  2.2 18.3 %copy-start = (bf16[4,4,8,8,1024]{4,3,2,1,0:T(8,128)(2,1)S(1)}, bf16[4,4,8,8,1024]{4,3,2,1,0:T(8,128)(2,1)}, u32[]{:S(2)}) copy-start(bf16[4,4,8,8,1024]{4,3,2,1,0:T(8,128)(2,1)} %forward.1) | copy-start | bytes 6291460
  2.2 18.3 %copy-start.1 = (f32[1,4,8,8,1024]{4,3,2,1,0:T(8,128)S(1)}, f32[1,4,8,8,1024]{4,3,2,1,0:T(8,128)}, u32[]{:S(2)}) copy-start(f32[1,4,8,8,1024]{4,3,2,1,0:T(8,128)} %param.11) | copy-start | bytes 3145732
  2.2 18.3 %copy-start.2 = (f32[8,8,1024]{2,1,0:T(8,128)S(1)}, f32[8,8,1024]{2,1,0:T(8,128)}, u32[]{:S(2)}) copy-start(f32[8,8,1024]{2,1,0:T(8,128)} %sound.1) | copy-start | bytes 786436
  2.2 18.3 %copy-start.3 = (f32[3,1024]{1,0:T(4,128)S(1)}, f32[3,1024]{1,0:T(4,128)}, u32[]{:S(2)}) copy-start(f32[3,1024]{1,0:T(4,128)} %wind.1) | copy-start | bytes 36868

commit v8 on v7

--- a/solution.py
+++ b/solution.py
@@ -133,6 +133,9 @@
             @pl.when(cond)
             def _():
                 copy.start()
+        return copies
+
+    def settle(copies):
         incoming = (has_lo_x, has_hi_x, has_lo_y, has_hi_y)
         for (cond, copy), arrives in zip(copies, incoming):
             @pl.when(cond)
@@ -143,23 +146,6 @@
             def _():
                 copy.wait_recv()
 
-    forward_copies = []
-    for cond, src, dst, slot, dev in (
-        (has_hi_x, forward.at[:, :, pl.ds(width_x - 1, 1)], fpad.at[:, :, pl.ds(0, 1)], 0, dev_hi_x),
-        (has_lo_x, forward.at[:, :, pl.ds(0, 1)], fpad.at[:, :, pl.ds(width_x + 1, 1)], 1, dev_lo_x),
-        (has_hi_y, fysend.at[0], fyr.at[0], 2, dev_hi_y),
-        (has_lo_y, fysend.at[1], fyr.at[1], 3, dev_lo_y),
-    ):
-        copy = pltpu.make_async_remote_copy(
-            src_ref=src, dst_ref=dst, send_sem=fs.at[slot], recv_sem=fr.at[slot],
-            device_id=dev, device_id_type=MESH,
-        )
-        forward_copies.append((cond, copy))
-
-        @pl.when(cond)
-        def _():
-            copy.start()
-
     def fill_state(par, x, c, v):
         pads[par, c, x + 1] = v
         ysend[par, 0, c, x] = v[width_y - 1:width_y, :]
@@ -171,18 +157,62 @@
         return carry
 
     lax.fori_loop(0, width_x, copy_in, 0)
+    forward_copies = exchange(
+        forward.at[:, :, pl.ds(0, 1)], forward.at[:, :, pl.ds(width_x - 1, 1)],
+        fpad.at[:, :, pl.ds(0, 1)], fpad.at[:, :, pl.ds(width_x + 1, 1)],
+        fysend.at[0], fysend.at[1], fyr.at[0], fyr.at[1], fs, fr,
+    )
+
+    def increment_slab(x, carry, get, snap, first, last):
+        xp = x + 1
+        p_new = get(0, x)
+        a_new = [get(1 + i, x) for i in range(3)]
+        fe, fn, fu = [], [], []
+        for c in range(4):
+            f = fpad[snap, c, xp].astype(jnp.float32)
+            fe.append((fpad[snap, c, xp + 1].astype(jnp.float32) - fpad[snap, c, x].astype(jnp.float32)) * 0.5)
+            fn.append(dy(f, fyr[0, snap, c, x], fyr[1, snap, c, x]))
+            fu.append(dz(f))
+        pieces = [p_new * (fe[1] + fn[2] + fu[3])]
+        for along in (fe, fn, fu):
+            pieces.append(p_new * along[0] + a_new[0] * along[1] + a_new[1] * along[2] + a_new[2] * along[3])
+        for c in range(4):
+            total = pieces[c] if first else acc_out[c, x] + pieces[c]
+            if not last:
+                acc_out[c, x] = total
+                continue
+            low, high = total[:, :half], total[:, half:]
+            kernel_out[c, x] = jnp.where(me_p == 0, low, high)
+            ksend[x, c] = jnp.where(me_p == 0, high, low)
+        if last:
+            pltpu.make_async_remote_copy(
+                src_ref=ksend.at[x], dst_ref=krecv.at[x], send_sem=ks.at[x], recv_sem=kr.at[x],
+                device_id=dev_pair, device_id_type=MESH,
+            ).start()
+        return carry
+
+    def forward_ready():
+        interior.wait()
+        settle(forward_copies)
 
     for step in range(steps):
         par = step % 2
         nxt = 1 - par
         snap = steps - 1 - step
         last = step == steps - 1
-        exchange(
+        state_copies = exchange(
             pads.at[par, :, pl.ds(1, 1)], pads.at[par, :, pl.ds(width_x, 1)],
             pads.at[par, :, pl.ds(0, 1)], pads.at[par, :, pl.ds(width_x + 1, 1)],
             ysend.at[par, 0], ysend.at[par, 1], yrecv.at[par, 0], yrecv.at[par, 1],
             ss.at[par], rs.at[par],
         )
+        if step > 0:
+            if step == 1:
+                forward_ready()
+            lax.fori_loop(0, width_x, functools.partial(
+                increment_slab, get=lambda c, x, par=par: pads[par, c, x + 1],
+                snap=snap + 1, first=step == 1, last=False), 0)
+        settle(state_copies)
 
         def pressure_slab(x, carry, par=par, snap=snap):
             xp = x + 1
@@ -206,24 +236,14 @@
             return carry
 
         lax.fori_loop(0, width_x, pressure_slab, 0)
-        if step == 0:
-            interior.wait()
-            for (cond, copy), arrives in zip(forward_copies, (has_lo_x, has_hi_x, has_lo_y, has_hi_y)):
-                @pl.when(cond)
-                def _():
-                    copy.wait_send()
-
-                @pl.when(arrives)
-                def _():
-                    copy.wait_recv()
-        exchange(
+        settle(exchange(
             pbuf.at[pl.ds(1, 1)], pbuf.at[pl.ds(width_x, 1)],
             pbuf.at[pl.ds(0, 1)], pbuf.at[pl.ds(width_x + 1, 1)],
             ypsend.at[0], ypsend.at[1], yprecv.at[0], yprecv.at[1],
             ps, pr,
-        )
-
-        def velocity_slab(x, carry, par=par, nxt=nxt, snap=snap, last=last, step=step):
+        ))
+
+        def velocity_slab(x, carry, par=par, nxt=nxt, last=last):
             xp = x + 1
             old = pads.at[par]
             p_new = pbuf[xp]
@@ -232,36 +252,13 @@
                 dy(p_new, yprecv[0, x], yprecv[1, x]),
                 dz(p_new),
             )
-            a_new = []
+            new_state = [p_new]
             for i in range(3):
                 a = old[1 + i, xp]
                 dxa = (old[1 + i, xp + 1] - old[1 + i, x]) * 0.5
                 dya = dy(a, yrecv[par, 0, 1 + i, x], yrecv[par, 1, 1 + i, x])
                 dza = dz(a)
-                a_new.append(a + step_length * (grad[i] + we * dxa + wn * dya + wv * dza))
-            fe, fn, fu = [], [], []
-            for c in range(4):
-                f = fpad[snap, c, xp].astype(jnp.float32)
-                fe.append((fpad[snap, c, xp + 1].astype(jnp.float32) - fpad[snap, c, x].astype(jnp.float32)) * 0.5)
-                fn.append(dy(f, fyr[0, snap, c, x], fyr[1, snap, c, x]))
-                fu.append(dz(f))
-            pieces = [p_new * (fe[1] + fn[2] + fu[3])]
-            for along in (fe, fn, fu):
-                pieces.append(p_new * along[0] + a_new[0] * along[1] + a_new[1] * along[2] + a_new[2] * along[3])
-            for c in range(4):
-                total = pieces[c] if step == 0 else acc_out[c, x] + pieces[c]
-                if not last:
-                    acc_out[c, x] = total
-                    continue
-                low, high = total[:, :half], total[:, half:]
-                kernel_out[c, x] = jnp.where(me_p == 0, low, high)
-                ksend[x, c] = jnp.where(me_p == 0, high, low)
-            if last:
-                pltpu.make_async_remote_copy(
-                    src_ref=ksend.at[x], dst_ref=krecv.at[x], send_sem=ks.at[x], recv_sem=kr.at[x],
-                    device_id=dev_pair, device_id_type=MESH,
-                ).start()
-            new_state = [p_new] + a_new
+                new_state.append(a + step_length * (grad[i] + we * dxa + wn * dya + wv * dza))
             for c in range(4):
                 if last:
                     state_out[c, x] = new_state[c]
@@ -270,6 +267,11 @@
             return carry
 
         lax.fori_loop(0, width_x, velocity_slab, 0)
+
+    if steps == 1:
+        forward_ready()
+    lax.fori_loop(0, width_x, functools.partial(
+        increment_slab, get=lambda c, x: state_out[c, x], snap=0, first=steps == 1, last=True), 0)
 
     for x in range(width_x):
         copy = pltpu.make_async_remote_copy(

time: 102 us -> 102 us (level)
  no operation moved by 1% of the time
where the time goes in v8:
time: 102 us; the launch traced here: 101 us
  Pallas kernels  93.4 us (92%)
  matrix products  2.96 us (3%)
  local copies, waits for them, and re-layouts  1.8 us (2%)
  other arithmetic  1.55 us (2%)
  between operations  1.43 us (1%)
    pallas_call x1, Pallas kernels, shards(): pl.pallas_call(kernel, out_shape=(jax.ShapeDtypeStruct((4, width_x, width...  78.9 us
    pallas_call x1, Pallas kernels, gathered_samples(): pl.pallas_call(functools.partial(samples_kernel, nx, ny), out_shape=jax.S...  14.6 us
    dot_general x1, matrix products, shards(): jnp.einsum('txyz,zn->txyn', forward_field[:, 0], source_z, preferred_elem...  2.19 us

profile of v8, /device:TPU:0, one launch (start us, length us, event | category | flops | bytes accessed | tf_op | source)
XLA Modules:
  0.0 101.2 jit_solution(3751738150330190944)
XLA Ops:
  1.3 0.8 slice_subtract_fusion.1
  2.2 0.0 copy-start.4
  2.2 0.0 copy-start
  2.2 0.0 copy-start.1
  2.2 0.0 copy-start.2
  2.2 0.0 copy-start.3
  2.2 2.2 %fusion.1.local_ref = f32[4,256]{1,0:T(4,128)} fusion(bf16[4,4,8,8,1024]{4,3,2,1,0:T(8,128)(2,1)} %forward.1, s32[256]{0:T(256)S(1)} %bitcast.40, f32[8,8,256]{2,1,0:T(8,128)S(1)} %and_convert_fusion.1), kind=kOutput, calls=%fused_computation.2 | convolution fusion | flops 134609920 | bytes 594944 | tf_op jit(solution)/shard_map/txyz,zn->txyn/dot_general | solution.py:370
  4.4 14.6 %shard_map.95 = f32[4,256]{1,0:T(4,128)} custom-call(f32[4,256]{1,0:T(4,128)} %fusion.1.local_ref), custom_call_target="tpu_custom_call" | custom-call | tf_op jit(solution)/shard_map/pallas_call | solution.py:328
  19.0 0.0 copy-done.4
  19.0 0.7 fusion.14
  19.7 0.8 fusion.5.inj
  20.5 0.0 copy-done
  20.5 0.0 copy-done.1
  20.5 0.0 copy-done.2
  20.5 0.0 copy-done.3
  20.5 78.9 %shard_map.96 = (f32[4,8,8,1024]{3,2,1,0:T(8,128)S(1)}, f32[4,8,8,512]{3,2,1,0:T(8,128)S(1)}) custom-call(f32[4,8,8,1024]{3,2,1,0:T(8,128)S(1)} %bitcast.33, f32[8,8,1024]{2,1,0:T(8,128)S(1)} %copy-done.2, f32[3,1024]{1,0:T(4,128)S(1)} %copy-done.3, bf16[4,4,8,8,1024]{4,3,2,1,0:T(8,128)(2,1)S(1)} %copy-done, f32[4,8,8,1024]{3,2,1,0:T(8,128)S(1)} %fusion.5.inj), custom_call_target="tpu_custom_call" | custom-call | tf_op jit(solution)/shard_map/pallas_call | solution.py:386
  99.4 0.8 copy.15
  100.2 1.0 copy.16
  (7 shorter events, 0.1 us)
Async XLA Ops:
  2.2 16.8 %copy-start.4 = (f32[256,4]{0,1:T(4,128)S(1)}, f32[256,4]{0,1:T(4,128)}, u32[]{:S(2)}) copy-start(f32[256,4]{0,1:T(4,128)} %param.15) | copy-start | bytes 12292
  2.2 18.3 %copy-start = (bf16[4,4,8,8,1024]{4,3,2,1,0:T(8,128)(2,1)S(1)}, bf16[4,4,8,8,1024]{4,3,2,1,0:T(8,128)(2,1)}, u32[]{:S(2)}) copy-start(bf16[4,4,8,8,1024]{4,3,2,1,0:T(8,128)(2,1)} %forward.1) | copy-start | bytes 6291460
  2.2 18.3 %copy-start.1 = (f32[1,4,8,8,1024]{4,3,2,1,0:T(8,128)S(1)}, f32[1,4,8,8,1024]{4,3,2,1,0:T(8,128)}, u32[]{:S(2)}) copy-start(f32[1,4,8,8,1024]{4,3,2,1,0:T(8,128)} %param.11) | copy-start | bytes 3145732
  2.2 18.3 %copy-start.2 = (f32[8,8,1024]{2,1,0:T(8,128)S(1)}, f32[8,8,1024]{2,1,0:T(8,128)}, u32[]{:S(2)}) copy-start(f32[8,8,1024]{2,1,0:T(8,128)} %sound.1) | copy-start | bytes 786436
  2.2 18.3 %copy-start.3 = (f32[3,1024]{1,0:T(4,128)S(1)}, f32[3,1024]{1,0:T(4,128)}, u32[]{:S(2)}) copy-start(f32[3,1024]{1,0:T(4,128)} %wind.1) | copy-start | bytes 36868

commit v9 on v8

--- a/solution.py
+++ b/solution.py
@@ -62,7 +62,7 @@
             pads[par, c, 0] = zero_slab
             pads[par, c, width_x + 1] = zero_slab
             for side in range(2):
-                yrecv[par, side, c] = jnp.zeros((width_x, 1, depth), jnp.float32)
+                yrecv[par, side, c] = jnp.zeros((width_x, depth), jnp.float32)
     pbuf[0] = zero_slab
     pbuf[width_x + 1] = zero_slab
     zero_forward = jnp.zeros((width_y, depth), fpad.dtype)
@@ -71,21 +71,21 @@
             fpad[t, c, 0] = zero_forward
             fpad[t, c, width_x + 1] = zero_forward
             for side in range(2):
-                fyr[side, t, c] = jnp.zeros((width_x, 1, depth), jnp.float32)
+                fyr[side, t, c] = jnp.zeros((width_x, depth), jnp.float32)
 
     def forward_rows(x, carry):
         for t in range(steps):
             for c in range(4):
                 f = forward[t, c, x].astype(jnp.float32)
-                fysend[0, t, c, x] = f[width_y - 1:width_y, :]
-                fysend[1, t, c, x] = f[0:1, :]
+                fysend[0, t, c, x:x + 1, :] = f[width_y - 1:width_y, :]
+                fysend[1, t, c, x:x + 1, :] = f[0:1, :]
         return carry
 
-    lax.fori_loop(0, width_x, forward_rows, 0)
+    [forward_rows(x, 0) for x in range(width_x)]
     interior = pltpu.make_async_copy(forward, fpad.at[:, :, pl.ds(1, width_x)], local_sem.at[0])
     interior.start()
     for side in range(2):
-        yprecv[side] = jnp.zeros((width_x, 1, depth), jnp.float32)
+        yprecv[side] = jnp.zeros((width_x, depth), jnp.float32)
 
     barrier = pltpu.get_barrier_semaphore()
     pl.semaphore_signal(barrier, 1, device_id=dev_pair, device_id_type=MESH)
@@ -148,15 +148,15 @@
 
     def fill_state(par, x, c, v):
         pads[par, c, x + 1] = v
-        ysend[par, 0, c, x] = v[width_y - 1:width_y, :]
-        ysend[par, 1, c, x] = v[0:1, :]
+        ysend[par, 0, c, x:x + 1, :] = v[width_y - 1:width_y, :]
+        ysend[par, 1, c, x:x + 1, :] = v[0:1, :]
 
     def copy_in(x, carry):
         for c in range(4):
             fill_state(0, x, c, state_in[c, x])
         return carry
 
-    lax.fori_loop(0, width_x, copy_in, 0)
+    [copy_in(x, 0) for x in range(width_x)]
     forward_copies = exchange(
         forward.at[:, :, pl.ds(0, 1)], forward.at[:, :, pl.ds(width_x - 1, 1)],
         fpad.at[:, :, pl.ds(0, 1)], fpad.at[:, :, pl.ds(width_x + 1, 1)],
@@ -171,7 +171,7 @@
         for c in range(4):
             f = fpad[snap, c, xp].astype(jnp.float32)
             fe.append((fpad[snap, c, xp + 1].astype(jnp.float32) - fpad[snap, c, x].astype(jnp.float32)) * 0.5)
-            fn.append(dy(f, fyr[0, snap, c, x], fyr[1, snap, c, x]))
+            fn.append(dy(f, fyr[0, snap, c, x:x + 1, :], fyr[1, snap, c, x:x + 1, :]))
             fu.append(dz(f))
         pieces = [p_new * (fe[1] + fn[2] + fu[3])]
         for along in (fe, fn, fu):
@@ -209,9 +209,9 @@
         if step > 0:
             if step == 1:
                 forward_ready()
-            lax.fori_loop(0, width_x, functools.partial(
+            [(functools.partial(
                 increment_slab, get=lambda c, x, par=par: pads[par, c, x + 1],
-                snap=snap + 1, first=step == 1, last=False), 0)
+                snap=snap + 1, first=step == 1, last=False))(x, 0) for x in range(width_x)]
         settle(state_copies)
 
         def pressure_slab(x, carry, par=par, snap=snap):
@@ -220,8 +220,8 @@
             p = old[0, xp]
             dxp = (old[0, xp + 1] - old[0, x]) * 0.5
             dxa = (old[1, xp + 1] - old[1, x]) * 0.5
-            dyp = dy(p, yrecv[par, 0, 0, x], yrecv[par, 1, 0, x])
-            dya = dy(old[2, xp], yrecv[par, 0, 2, x], yrecv[par, 1, 2, x])
+            dyp = dy(p, yrecv[par, 0, 0, x:x + 1, :], yrecv[par, 1, 0, x:x + 1, :])
+            dya = dy(old[2, xp], yrecv[par, 0, 2, x:x + 1, :], yrecv[par, 1, 2, x:x + 1, :])
             dzp = dz(p)
             dza = dz(old[3, xp])
             divergence = dxa + dya + dza
@@ -231,11 +231,11 @@
                 + inj[snap, x]
             )
             pbuf[xp] = p_new
-            ypsend[0, x] = p_new[width_y - 1:width_y, :]
-            ypsend[1, x] = p_new[0:1, :]
+            ypsend[0, x:x + 1, :] = p_new[width_y - 1:width_y, :]
+            ypsend[1, x:x + 1, :] = p_new[0:1, :]
             return carry
 
-        lax.fori_loop(0, width_x, pressure_slab, 0)
+        [pressure_slab(x, 0) for x in range(width_x)]
         settle(exchange(
             pbuf.at[pl.ds(1, 1)], pbuf.at[pl.ds(width_x, 1)],
             pbuf.at[pl.ds(0, 1)], pbuf.at[pl.ds(width_x + 1, 1)],
@@ -249,14 +249,14 @@
             p_new = pbuf[xp]
             grad = (
                 (pbuf[xp + 1] - pbuf[x]) * 0.5,
-                dy(p_new, yprecv[0, x], yprecv[1, x]),
+                dy(p_new, yprecv[0, x:x + 1, :], yprecv[1, x:x + 1, :]),
                 dz(p_new),
             )
             new_state = [p_new]
             for i in range(3):
                 a = old[1 + i, xp]
                 dxa = (old[1 + i, xp + 1] - old[1 + i, x]) * 0.5
-                dya = dy(a, yrecv[par, 0, 1 + i, x], yrecv[par, 1, 1 + i, x])
+                dya = dy(a, yrecv[par, 0, 1 + i, x:x + 1, :], yrecv[par, 1, 1 + i, x:x + 1, :])
                 dza = dz(a)
                 new_state.append(a + step_length * (grad[i] + we * dxa + wn * dya + wv * dza))
             for c in range(4):
@@ -266,12 +266,12 @@
                     fill_state(nxt, x, c, new_state[c])
             return carry
 
-        lax.fori_loop(0, width_x, velocity_slab, 0)
+        [velocity_slab(x, 0) for x in range(width_x)]
 
     if steps == 1:
         forward_ready()
-    lax.fori_loop(0, width_x, functools.partial(
-        increment_slab, get=lambda c, x: state_out[c, x], snap=0, first=steps == 1, last=True), 0)
+    [(functools.partial(
+        increment_slab, get=lambda c, x: state_out[c, x], snap=0, first=steps == 1, last=True))(x, 0) for x in range(width_x)]
 
     for x in range(width_x):
         copy = pltpu.make_async_remote_copy(
@@ -286,7 +286,7 @@
             kernel_out[c, x] = kernel_out[c, x] + krecv[x, c]
         return carry
 
-    lax.fori_loop(0, width_x, add_partner, 0)
+    [add_partner(x, 0) for x in range(width_x)]
 
 
 def samples_kernel(nx, ny, local_ref, out_ref, sent, got_x, got_y, send_sem, recv_sem):
@@ -394,16 +394,16 @@
         scratch_shapes=[
             pltpu.VMEM((2, 4, width_x + 2, width_y, depth), jnp.float32),
             pltpu.VMEM((width_x + 2, width_y, depth), jnp.float32),
-            pltpu.VMEM((2, 2, 4, width_x, 1, depth), jnp.float32),
-            pltpu.VMEM((2, 2, 4, width_x, 1, depth), jnp.float32),
-            pltpu.VMEM((2, width_x, 1, depth), jnp.float32),
-            pltpu.VMEM((2, width_x, 1, depth), jnp.float32),
+            pltpu.VMEM((2, 2, 4, width_x, depth), jnp.float32),
+            pltpu.VMEM((2, 2, 4, width_x, depth), jnp.float32),
+            pltpu.VMEM((2, width_x, depth), jnp.float32),
+            pltpu.VMEM((2, width_x, depth), jnp.float32),
             pltpu.VMEM((4, width_x, width_y, depth), jnp.float32),
             pltpu.VMEM((width_x, 4, width_y, depth // 2), jnp.float32),
             pltpu.VMEM((width_x, 4, width_y, depth // 2), jnp.float32),
             pltpu.VMEM((steps_total, 4, width_x + 2, width_y, depth), forward_field.dtype),
-            pltpu.VMEM((2, steps_total, 4, width_x, 1, depth), jnp.float32),
-            pltpu.VMEM((2, steps_total, 4, width_x, 1, depth), jnp.float32),
+            pltpu.VMEM((2, steps_total, 4, width_x, depth), jnp.float32),
+            pltpu.VMEM((2, steps_total, 4, width_x, depth), jnp.float32),
             pltpu.SemaphoreType.DMA((2, 4)),
             pltpu.SemaphoreType.DMA((2, 4)),
             pltpu.SemaphoreType.DMA((4,)),

time: 102 us -> 99 us (0.971)
  Pallas kernels: 93.4 us -> 89.7 us
    pallas_call x1, Pallas kernels: 78.9 us -> 75.1 us  [shards(): pl.pallas_call(kernel, out_shape=(jax.ShapeDtypeStruct((4, width_x, width...]
where the time goes in v9:
time: 99 us; the launch traced here: 97.4 us
  Pallas kernels  89.7 us (91%)
  matrix products  2.96 us (3%)
  local copies, waits for them, and re-layouts  1.8 us (2%)
  other arithmetic  1.55 us (2%)
  between operations  1.43 us (1%)
    pallas_call x1, Pallas kernels, shards(): pl.pallas_call(kernel, out_shape=(jax.ShapeDtypeStruct((4, width_x, width...  75.1 us
    pallas_call x1, Pallas kernels, gathered_samples(): pl.pallas_call(functools.partial(samples_kernel, nx, ny), out_shape=jax.S...  14.6 us
    dot_general x1, matrix products, shards(): jnp.einsum('txyz,zn->txyn', forward_field[:, 0], source_z, preferred_elem...  2.19 us

profile of v9, /device:TPU:0, one launch (start us, length us, event | category | flops | bytes accessed | tf_op | source)
XLA Modules:
  0.0 97.4 jit_solution(1334957817587703093)
XLA Ops:
  1.3 0.8 slice_subtract_fusion.1
  2.2 0.0 copy-start.4
  2.2 0.0 copy-start
  2.2 0.0 copy-start.1
  2.2 0.0 copy-start.2
  2.2 0.0 copy-start.3
  2.2 2.2 %fusion.1.local_ref = f32[4,256]{1,0:T(4,128)} fusion(bf16[4,4,8,8,1024]{4,3,2,1,0:T(8,128)(2,1)} %forward.1, s32[256]{0:T(256)S(1)} %bitcast.40, f32[8,8,256]{2,1,0:T(8,128)S(1)} %and_convert_fusion.1), kind=kOutput, calls=%fused_computation.2 | convolution fusion | flops 134609920 | bytes 594944 | tf_op jit(solution)/shard_map/txyz,zn->txyn/dot_general | solution.py:370
  4.4 14.6 %shard_map.95 = f32[4,256]{1,0:T(4,128)} custom-call(f32[4,256]{1,0:T(4,128)} %fusion.1.local_ref), custom_call_target="tpu_custom_call" | custom-call | tf_op jit(solution)/shard_map/pallas_call | solution.py:328
  19.0 0.0 copy-done.4
  19.0 0.7 fusion.14
  19.7 0.8 fusion.5.inj
  20.5 0.0 copy-done
  20.5 0.0 copy-done.1
  20.5 0.0 copy-done.2
  20.5 0.0 copy-done.3
  20.5 75.1 %shard_map.96 = (f32[4,8,8,1024]{3,2,1,0:T(8,128)S(1)}, f32[4,8,8,512]{3,2,1,0:T(8,128)S(1)}) custom-call(f32[4,8,8,1024]{3,2,1,0:T(8,128)S(1)} %bitcast.33, f32[8,8,1024]{2,1,0:T(8,128)S(1)} %copy-done.2, f32[3,1024]{1,0:T(4,128)S(1)} %copy-done.3, bf16[4,4,8,8,1024]{4,3,2,1,0:T(8,128)(2,1)S(1)} %copy-done, f32[4,8,8,1024]{3,2,1,0:T(8,128)S(1)} %fusion.5.inj), custom_call_target="tpu_custom_call" | custom-call | tf_op jit(solution)/shard_map/pallas_call | solution.py:386
  95.7 0.8 copy.15
  96.5 1.0 copy.16
  (7 shorter events, 0.1 us)
Async XLA Ops:
  2.2 16.8 %copy-start.4 = (f32[256,4]{0,1:T(4,128)S(1)}, f32[256,4]{0,1:T(4,128)}, u32[]{:S(2)}) copy-start(f32[256,4]{0,1:T(4,128)} %param.15) | copy-start | bytes 12292
  2.2 18.3 %copy-start = (bf16[4,4,8,8,1024]{4,3,2,1,0:T(8,128)(2,1)S(1)}, bf16[4,4,8,8,1024]{4,3,2,1,0:T(8,128)(2,1)}, u32[]{:S(2)}) copy-start(bf16[4,4,8,8,1024]{4,3,2,1,0:T(8,128)(2,1)} %forward.1) | copy-start | bytes 6291460
  2.2 18.3 %copy-start.1 = (f32[1,4,8,8,1024]{4,3,2,1,0:T(8,128)S(1)}, f32[1,4,8,8,1024]{4,3,2,1,0:T(8,128)}, u32[]{:S(2)}) copy-start(f32[1,4,8,8,1024]{4,3,2,1,0:T(8,128)} %param.11) | copy-start | bytes 3145732
  2.2 18.3 %copy-start.2 = (f32[8,8,1024]{2,1,0:T(8,128)S(1)}, f32[8,8,1024]{2,1,0:T(8,128)}, u32[]{:S(2)}) copy-start(f32[8,8,1024]{2,1,0:T(8,128)} %sound.1) | copy-start | bytes 786436
  2.2 18.3 %copy-start.3 = (f32[3,1024]{1,0:T(4,128)S(1)}, f32[3,1024]{1,0:T(4,128)}, u32[]{:S(2)}) copy-start(f32[3,1024]{1,0:T(4,128)} %wind.1) | copy-start | bytes 36868

commit v10 on v9

--- a/solution.py
+++ b/solution.py
@@ -71,14 +71,15 @@
             fpad[t, c, 0] = zero_forward
             fpad[t, c, width_x + 1] = zero_forward
             for side in range(2):
-                fyr[side, t, c] = jnp.zeros((width_x, depth), jnp.float32)
+                fyr[side, t, c // 2, pl.ds((c % 2) * width_x, width_x), :] = jnp.zeros((width_x, depth), fyr.dtype)
 
     def forward_rows(x, carry):
         for t in range(steps):
             for c in range(4):
-                f = forward[t, c, x].astype(jnp.float32)
-                fysend[0, t, c, x:x + 1, :] = f[width_y - 1:width_y, :]
-                fysend[1, t, c, x:x + 1, :] = f[0:1, :]
+                f = forward[t, c, x]
+                row = (c % 2) * width_x + x
+                fysend[0, t, c // 2, row:row + 1, :] = f[width_y - 1:width_y, :]
+                fysend[1, t, c // 2, row:row + 1, :] = f[0:1, :]
         return carry
 
     [forward_rows(x, 0) for x in range(width_x)]
@@ -171,7 +172,9 @@
         for c in range(4):
             f = fpad[snap, c, xp].astype(jnp.float32)
             fe.append((fpad[snap, c, xp + 1].astype(jnp.float32) - fpad[snap, c, x].astype(jnp.float32)) * 0.5)
-            fn.append(dy(f, fyr[0, snap, c, x:x + 1, :], fyr[1, snap, c, x:x + 1, :]))
+            row = (c % 2) * width_x + x
+            fn.append(dy(f, fyr[0, snap, c // 2, row:row + 1, :].astype(jnp.float32),
+                         fyr[1, snap, c // 2, row:row + 1, :].astype(jnp.float32)))
             fu.append(dz(f))
         pieces = [p_new * (fe[1] + fn[2] + fu[3])]
         for along in (fe, fn, fu):
@@ -402,8 +405,8 @@
             pltpu.VMEM((width_x, 4, width_y, depth // 2), jnp.float32),
             pltpu.VMEM((width_x, 4, width_y, depth // 2), jnp.float32),
             pltpu.VMEM((steps_total, 4, width_x + 2, width_y, depth), forward_field.dtype),
-            pltpu.VMEM((2, steps_total, 4, width_x, depth), jnp.float32),
-            pltpu.VMEM((2, steps_total, 4, width_x, depth), jnp.float32),
+            pltpu.VMEM((2, steps_total, 2, 2 * width_x, depth), forward_field.dtype),
+            pltpu.VMEM((2, steps_total, 2, 2 * width_x, depth), forward_field.dtype),
             pltpu.SemaphoreType.DMA((2, 4)),
             pltpu.SemaphoreType.DMA((2, 4)),
             pltpu.SemaphoreType.DMA((4,)),

time: 99 us -> 98.9 us (level)
  no operation moved by 1% of the time
where the time goes in v10:
time: 98.9 us; the launch traced here: 97.4 us
  Pallas kernels  89.6 us (91%)
  matrix products  2.96 us (3%)
  local copies, waits for them, and re-layouts  1.8 us (2%)
  other arithmetic  1.55 us (2%)
  between operations  1.43 us (1%)
    pallas_call x1, Pallas kernels, shards(): pl.pallas_call(kernel, out_shape=(jax.ShapeDtypeStruct((4, width_x, width...  75.1 us
    pallas_call x1, Pallas kernels, gathered_samples(): pl.pallas_call(functools.partial(samples_kernel, nx, ny), out_shape=jax.S...  14.6 us
    dot_general x1, matrix products, shards(): jnp.einsum('txyz,zn->txyn', forward_field[:, 0], source_z, preferred_elem...  2.19 us

profile of v10, /device:TPU:0, one launch (start us, length us, event | category | flops | bytes accessed | tf_op | source)
XLA Modules:
  0.0 97.4 jit_solution(10979352757041919952)
XLA Ops:
  1.3 0.8 slice_subtract_fusion.1
  2.2 0.0 copy-start.4
  2.2 0.0 copy-start
  2.2 0.0 copy-start.1
  2.2 0.0 copy-start.2
  2.2 0.0 copy-start.3
  2.2 2.2 %fusion.1.local_ref = f32[4,256]{1,0:T(4,128)} fusion(bf16[4,4,8,8,1024]{4,3,2,1,0:T(8,128)(2,1)} %forward.1, s32[256]{0:T(256)S(1)} %bitcast.40, f32[8,8,256]{2,1,0:T(8,128)S(1)} %and_convert_fusion.1), kind=kOutput, calls=%fused_computation.2 | convolution fusion | flops 134609920 | bytes 594944 | tf_op jit(solution)/shard_map/txyz,zn->txyn/dot_general | solution.py:373
  4.4 14.6 %shard_map.95 = f32[4,256]{1,0:T(4,128)} custom-call(f32[4,256]{1,0:T(4,128)} %fusion.1.local_ref), custom_call_target="tpu_custom_call" | custom-call | tf_op jit(solution)/shard_map/pallas_call | solution.py:331
  19.0 0.0 copy-done.4
  19.0 0.7 fusion.14
  19.7 0.8 fusion.5.inj
  20.5 0.0 copy-done
  20.5 0.0 copy-done.1
  20.5 0.0 copy-done.2
  20.5 0.0 copy-done.3
  20.5 75.1 %shard_map.96 = (f32[4,8,8,1024]{3,2,1,0:T(8,128)S(1)}, f32[4,8,8,512]{3,2,1,0:T(8,128)S(1)}) custom-call(f32[4,8,8,1024]{3,2,1,0:T(8,128)S(1)} %bitcast.33, f32[8,8,1024]{2,1,0:T(8,128)S(1)} %copy-done.2, f32[3,1024]{1,0:T(4,128)S(1)} %copy-done.3, bf16[4,4,8,8,1024]{4,3,2,1,0:T(8,128)(2,1)S(1)} %copy-done, f32[4,8,8,1024]{3,2,1,0:T(8,128)S(1)} %fusion.5.inj), custom_call_target="tpu_custom_call" | custom-call | tf_op jit(solution)/shard_map/pallas_call | solution.py:389
  95.6 0.8 copy.15
  96.4 1.0 copy.16
  (7 shorter events, 0.1 us)
Async XLA Ops:
  2.2 16.8 %copy-start.4 = (f32[256,4]{0,1:T(4,128)S(1)}, f32[256,4]{0,1:T(4,128)}, u32[]{:S(2)}) copy-start(f32[256,4]{0,1:T(4,128)} %param.15) | copy-start | bytes 12292
  2.2 18.3 %copy-start = (bf16[4,4,8,8,1024]{4,3,2,1,0:T(8,128)(2,1)S(1)}, bf16[4,4,8,8,1024]{4,3,2,1,0:T(8,128)(2,1)}, u32[]{:S(2)}) copy-start(bf16[4,4,8,8,1024]{4,3,2,1,0:T(8,128)(2,1)} %forward.1) | copy-start | bytes 6291460
  2.2 18.3 %copy-start.1 = (f32[1,4,8,8,1024]{4,3,2,1,0:T(8,128)S(1)}, f32[1,4,8,8,1024]{4,3,2,1,0:T(8,128)}, u32[]{:S(2)}) copy-start(f32[1,4,8,8,1024]{4,3,2,1,0:T(8,128)} %param.11) | copy-start | bytes 3145732
  2.2 18.3 %copy-start.2 = (f32[8,8,1024]{2,1,0:T(8,128)S(1)}, f32[8,8,1024]{2,1,0:T(8,128)}, u32[]{:S(2)}) copy-start(f32[8,8,1024]{2,1,0:T(8,128)} %sound.1) | copy-start | bytes 786436
  2.2 18.3 %copy-start.3 = (f32[3,1024]{1,0:T(4,128)S(1)}, f32[3,1024]{1,0:T(4,128)}, u32[]{:S(2)}) copy-start(f32[3,1024]{1,0:T(4,128)} %wind.1) | copy-start | bytes 36868

commit v11 on v10

--- a/solution.py
+++ b/solution.py
@@ -8,6 +8,7 @@
 from jax.sharding import PartitionSpec as P
 
 step_length = 0.25
+Y_SLOT = (0, 2, 1, 3)
 MESH = pl.DeviceIdType.MESH
 
 
@@ -149,8 +150,8 @@
 
     def fill_state(par, x, c, v):
         pads[par, c, x + 1] = v
-        ysend[par, 0, c, x:x + 1, :] = v[width_y - 1:width_y, :]
-        ysend[par, 1, c, x:x + 1, :] = v[0:1, :]
+        ysend[par, 0, Y_SLOT[c], x:x + 1, :] = v[width_y - 1:width_y, :]
+        ysend[par, 1, Y_SLOT[c], x:x + 1, :] = v[0:1, :]
 
     def copy_in(x, carry):
         for c in range(4):
@@ -203,12 +204,17 @@
         nxt = 1 - par
         snap = steps - 1 - step
         last = step == steps - 1
-        state_copies = exchange(
-            pads.at[par, :, pl.ds(1, 1)], pads.at[par, :, pl.ds(width_x, 1)],
-            pads.at[par, :, pl.ds(0, 1)], pads.at[par, :, pl.ds(width_x + 1, 1)],
-            ysend.at[par, 0], ysend.at[par, 1], yrecv.at[par, 0], yrecv.at[par, 1],
-            ss.at[par], rs.at[par],
-        )
+        halves = []
+        for part in range(2):
+            comps = pl.ds(2 * part, 2)
+            halves.append(exchange(
+                pads.at[par, comps, pl.ds(1, 1)], pads.at[par, comps, pl.ds(width_x, 1)],
+                pads.at[par, comps, pl.ds(0, 1)], pads.at[par, comps, pl.ds(width_x + 1, 1)],
+                ysend.at[par, 0, comps], ysend.at[par, 1, comps],
+                yrecv.at[par, 0, comps], yrecv.at[par, 1, comps],
+                ss.at[par, part], rs.at[par, part],
+            ))
+        state_copies, velocity_copies = halves
         if step > 0:
             if step == 1:
                 forward_ready()
@@ -223,8 +229,8 @@
             p = old[0, xp]
             dxp = (old[0, xp + 1] - old[0, x]) * 0.5
             dxa = (old[1, xp + 1] - old[1, x]) * 0.5
-            dyp = dy(p, yrecv[par, 0, 0, x:x + 1, :], yrecv[par, 1, 0, x:x + 1, :])
-            dya = dy(old[2, xp], yrecv[par, 0, 2, x:x + 1, :], yrecv[par, 1, 2, x:x + 1, :])
+            dyp = dy(p, yrecv[par, 0, Y_SLOT[0], x:x + 1, :], yrecv[par, 1, Y_SLOT[0], x:x + 1, :])
+            dya = dy(old[2, xp], yrecv[par, 0, Y_SLOT[2], x:x + 1, :], yrecv[par, 1, Y_SLOT[2], x:x + 1, :])
             dzp = dz(p)
             dza = dz(old[3, xp])
             divergence = dxa + dya + dza
@@ -245,6 +251,8 @@
             ypsend.at[0], ypsend.at[1], yprecv.at[0], yprecv.at[1],
             ps, pr,
         ))
+
+        settle(velocity_copies)
 
         def velocity_slab(x, carry, par=par, nxt=nxt, last=last):
             xp = x + 1
@@ -259,7 +267,7 @@
             for i in range(3):
                 a = old[1 + i, xp]
                 dxa = (old[1 + i, xp + 1] - old[1 + i, x]) * 0.5
-                dya = dy(a, yrecv[par, 0, 1 + i, x:x + 1, :], yrecv[par, 1, 1 + i, x:x + 1, :])
+                dya = dy(a, yrecv[par, 0, Y_SLOT[1 + i], x:x + 1, :], yrecv[par, 1, Y_SLOT[1 + i], x:x + 1, :])
                 dza = dz(a)
                 new_state.append(a + step_length * (grad[i] + we * dxa + wn * dya + wv * dza))
             for c in range(4):
@@ -407,8 +415,8 @@
             pltpu.VMEM((steps_total, 4, width_x + 2, width_y, depth), forward_field.dtype),
             pltpu.VMEM((2, steps_total, 2, 2 * width_x, depth), forward_field.dtype),
             pltpu.VMEM((2, steps_total, 2, 2 * width_x, depth), forward_field.dtype),
-            pltpu.SemaphoreType.DMA((2, 4)),
-            pltpu.SemaphoreType.DMA((2, 4)),
+            pltpu.SemaphoreType.DMA((2, 2, 4)),
+            pltpu.SemaphoreType.DMA((2, 2, 4)),
             pltpu.SemaphoreType.DMA((4,)),
             pltpu.SemaphoreType.DMA((4,)),
             pltpu.SemaphoreType.DMA((width_x,)),

time: 98.9 us -> 92.1 us (0.931); the launches traced: 97.4 us -> 91.8 us
  Pallas kernels: 89.6 us -> 84.1 us
    pallas_call x1, Pallas kernels: 75.1 us -> 69.5 us  [shards(): pl.pallas_call(kernel, out_shape=(jax.ShapeDtypeStruct((4, width_x, width...]
where the time goes in v11:
time: 92.1 us; the launch traced here: 91.8 us
  Pallas kernels  84.1 us (91%)
  matrix products  2.96 us (3%)
  local copies, waits for them, and re-layouts  1.8 us (2%)
  other arithmetic  1.55 us (2%)
  between operations  1.43 us (2%)
    pallas_call x1, Pallas kernels, shards(): pl.pallas_call(kernel, out_shape=(jax.ShapeDtypeStruct((4, width_x, width...  69.5 us
    pallas_call x1, Pallas kernels, gathered_samples(): pl.pallas_call(functools.partial(samples_kernel, nx, ny), out_shape=jax.S...  14.6 us
    dot_general x1, matrix products, shards(): jnp.einsum('txyz,zn->txyn', forward_field[:, 0], source_z, preferred_elem...  2.19 us

profile of v11, /device:TPU:0, one launch (start us, length us, event | category | flops | bytes accessed | tf_op | source)
XLA Modules:
  0.0 91.8 jit_solution(11528942720092079630)
XLA Ops:
  1.3 0.8 slice_subtract_fusion.1
  2.2 0.0 copy-start.4
  2.2 0.0 copy-start
  2.2 0.0 copy-start.1
  2.2 0.0 copy-start.2
  2.2 0.0 copy-start.3
  2.2 2.2 %fusion.1.local_ref = f32[4,256]{1,0:T(4,128)} fusion(bf16[4,4,8,8,1024]{4,3,2,1,0:T(8,128)(2,1)} %forward.1, s32[256]{0:T(256)S(1)} %bitcast.40, f32[8,8,256]{2,1,0:T(8,128)S(1)} %and_convert_fusion.1), kind=kOutput, calls=%fused_computation.2 | convolution fusion | flops 134609920 | bytes 594944 | tf_op jit(solution)/shard_map/txyz,zn->txyn/dot_general | solution.py:381
  4.4 14.6 %shard_map.95 = f32[4,256]{1,0:T(4,128)} custom-call(f32[4,256]{1,0:T(4,128)} %fusion.1.local_ref), custom_call_target="tpu_custom_call" | custom-call | tf_op jit(solution)/shard_map/pallas_call | solution.py:339
  19.0 0.0 copy-done.4
  19.0 0.7 fusion.14
  19.7 0.8 fusion.5.inj
  20.5 0.0 copy-done
  20.5 0.0 copy-done.1
  20.5 0.0 copy-done.2
  20.5 0.0 copy-done.3
  20.5 69.5 %shard_map.96 = (f32[4,8,8,1024]{3,2,1,0:T(8,128)S(1)}, f32[4,8,8,512]{3,2,1,0:T(8,128)S(1)}) custom-call(f32[4,8,8,1024]{3,2,1,0:T(8,128)S(1)} %bitcast.33, f32[8,8,1024]{2,1,0:T(8,128)S(1)} %copy-done.2, f32[3,1024]{1,0:T(4,128)S(1)} %copy-done.3, bf16[4,4,8,8,1024]{4,3,2,1,0:T(8,128)(2,1)S(1)} %copy-done, f32[4,8,8,1024]{3,2,1,0:T(8,128)S(1)} %fusion.5.inj), custom_call_target="tpu_custom_call" | custom-call | tf_op jit(solution)/shard_map/pallas_call | solution.py:397
  90.1 0.8 copy.15
  90.9 1.0 %copy.16 = f32[1,4,8,8,1024]{4,3,2,1,0:T(8,128)} copy(f32[1,4,8,8,1024]{4,3,2,1,0:T(8,128)S(1)} %bitcast.34) | data formatting | bytes 2097152
  (7 shorter events, 0.1 us)
Async XLA Ops:
  2.2 16.8 %copy-start.4 = (f32[256,4]{0,1:T(4,128)S(1)}, f32[256,4]{0,1:T(4,128)}, u32[]{:S(2)}) copy-start(f32[256,4]{0,1:T(4,128)} %param.15) | copy-start | bytes 12292
  2.2 18.3 %copy-start = (bf16[4,4,8,8,1024]{4,3,2,1,0:T(8,128)(2,1)S(1)}, bf16[4,4,8,8,1024]{4,3,2,1,0:T(8,128)(2,1)}, u32[]{:S(2)}) copy-start(bf16[4,4,8,8,1024]{4,3,2,1,0:T(8,128)(2,1)} %forward.1) | copy-start | bytes 6291460
  2.2 18.3 %copy-start.1 = (f32[1,4,8,8,1024]{4,3,2,1,0:T(8,128)S(1)}, f32[1,4,8,8,1024]{4,3,2,1,0:T(8,128)}, u32[]{:S(2)}) copy-start(f32[1,4,8,8,1024]{4,3,2,1,0:T(8,128)} %param.11) | copy-start | bytes 3145732
  2.2 18.3 %copy-start.2 = (f32[8,8,1024]{2,1,0:T(8,128)S(1)}, f32[8,8,1024]{2,1,0:T(8,128)}, u32[]{:S(2)}) copy-start(f32[8,8,1024]{2,1,0:T(8,128)} %sound.1) | copy-start | bytes 786436
  2.2 18.3 %copy-start.3 = (f32[3,1024]{1,0:T(4,128)S(1)}, f32[3,1024]{1,0:T(4,128)}, u32[]{:S(2)}) copy-start(f32[3,1024]{1,0:T(4,128)} %wind.1) | copy-start | bytes 36868

commit v12 on v11

--- a/solution.py
+++ b/solution.py
@@ -64,8 +64,9 @@
             pads[par, c, width_x + 1] = zero_slab
             for side in range(2):
                 yrecv[par, side, c] = jnp.zeros((width_x, depth), jnp.float32)
-    pbuf[0] = zero_slab
-    pbuf[width_x + 1] = zero_slab
+    for par in range(2):
+        pbuf[par, 0] = zero_slab
+        pbuf[par, width_x + 1] = zero_slab
     zero_forward = jnp.zeros((width_y, depth), fpad.dtype)
     for t in range(steps):
         for c in range(4):
@@ -86,8 +87,9 @@
     [forward_rows(x, 0) for x in range(width_x)]
     interior = pltpu.make_async_copy(forward, fpad.at[:, :, pl.ds(1, width_x)], local_sem.at[0])
     interior.start()
-    for side in range(2):
-        yprecv[side] = jnp.zeros((width_x, depth), jnp.float32)
+    for par in range(2):
+        for side in range(2):
+            yprecv[par, side] = jnp.zeros((width_x, depth), jnp.float32)
 
     barrier = pltpu.get_barrier_semaphore()
     pl.semaphore_signal(barrier, 1, device_id=dev_pair, device_id_type=MESH)
@@ -206,7 +208,7 @@
         last = step == steps - 1
         halves = []
         for part in range(2):
-            comps = pl.ds(2 * part, 2)
+            comps = pl.ds(2 * part, 2) if (part or step == 0) else pl.ds(1, 1)
             halves.append(exchange(
                 pads.at[par, comps, pl.ds(1, 1)], pads.at[par, comps, pl.ds(width_x, 1)],
                 pads.at[par, comps, pl.ds(0, 1)], pads.at[par, comps, pl.ds(width_x + 1, 1)],
@@ -223,13 +225,19 @@
                 snap=snap + 1, first=step == 1, last=False))(x, 0) for x in range(width_x)]
         settle(state_copies)
 
-        def pressure_slab(x, carry, par=par, snap=snap):
+        def pressure_slab(x, carry, par=par, snap=snap, step=step):
             xp = x + 1
             old = pads.at[par]
-            p = old[0, xp]
-            dxp = (old[0, xp + 1] - old[0, x]) * 0.5
+            if step == 0:
+                p = old[0, xp]
+                dxp = (old[0, xp + 1] - old[0, x]) * 0.5
+                dyp = dy(p, yrecv[par, 0, Y_SLOT[0], x:x + 1, :], yrecv[par, 1, Y_SLOT[0], x:x + 1, :])
+            else:
+                held = pbuf.at[1 - par]
+                p = held[xp]
+                dxp = (held[xp + 1] - held[x]) * 0.5
+                dyp = dy(p, yprecv[1 - par, 0, x:x + 1, :], yprecv[1 - par, 1, x:x + 1, :])
             dxa = (old[1, xp + 1] - old[1, x]) * 0.5
-            dyp = dy(p, yrecv[par, 0, Y_SLOT[0], x:x + 1, :], yrecv[par, 1, Y_SLOT[0], x:x + 1, :])
             dya = dy(old[2, xp], yrecv[par, 0, Y_SLOT[2], x:x + 1, :], yrecv[par, 1, Y_SLOT[2], x:x + 1, :])
             dzp = dz(p)
             dza = dz(old[3, xp])
@@ -239,16 +247,16 @@
                 + step_length * (sound[x] * divergence + we * dxp + wn * dyp + wv * dzp)
                 + inj[snap, x]
             )
-            pbuf[xp] = p_new
+            pbuf[par, xp] = p_new
             ypsend[0, x:x + 1, :] = p_new[width_y - 1:width_y, :]
             ypsend[1, x:x + 1, :] = p_new[0:1, :]
             return carry
 
         [pressure_slab(x, 0) for x in range(width_x)]
         settle(exchange(
-            pbuf.at[pl.ds(1, 1)], pbuf.at[pl.ds(width_x, 1)],
-            pbuf.at[pl.ds(0, 1)], pbuf.at[pl.ds(width_x + 1, 1)],
-            ypsend.at[0], ypsend.at[1], yprecv.at[0], yprecv.at[1],
+            pbuf.at[par, pl.ds(1, 1)], pbuf.at[par, pl.ds(width_x, 1)],
+            pbuf.at[par, pl.ds(0, 1)], pbuf.at[par, pl.ds(width_x + 1, 1)],
+            ypsend.at[0], ypsend.at[1], yprecv.at[par, 0], yprecv.at[par, 1],
             ps, pr,
         ))
 
@@ -257,10 +265,10 @@
         def velocity_slab(x, carry, par=par, nxt=nxt, last=last):
             xp = x + 1
             old = pads.at[par]
-            p_new = pbuf[xp]
+            p_new = pbuf[par, xp]
             grad = (
-                (pbuf[xp + 1] - pbuf[x]) * 0.5,
-                dy(p_new, yprecv[0, x:x + 1, :], yprecv[1, x:x + 1, :]),
+                (pbuf[par, xp + 1] - pbuf[par, x]) * 0.5,
+                dy(p_new, yprecv[par, 0, x:x + 1, :], yprecv[par, 1, x:x + 1, :]),
                 dz(p_new),
             )
             new_state = [p_new]
@@ -404,11 +412,11 @@
         out_specs=(vmem, vmem),
         scratch_shapes=[
             pltpu.VMEM((2, 4, width_x + 2, width_y, depth), jnp.float32),
-            pltpu.VMEM((width_x + 2, width_y, depth), jnp.float32),
+            pltpu.VMEM((2, width_x + 2, width_y, depth), jnp.float32),
             pltpu.VMEM((2, 2, 4, width_x, depth), jnp.float32),
             pltpu.VMEM((2, 2, 4, width_x, depth), jnp.float32),
             pltpu.VMEM((2, width_x, depth), jnp.float32),
-            pltpu.VMEM((2, width_x, depth), jnp.float32),
+            pltpu.VMEM((2, 2, width_x, depth), jnp.float32),
             pltpu.VMEM((4, width_x, width_y, depth), jnp.float32),
             pltpu.VMEM((width_x, 4, width_y, depth // 2), jnp.float32),
             pltpu.VMEM((width_x, 4, width_y, depth // 2), jnp.float32),

time: 92.1 us -> 87.8 us (0.953)
  Pallas kernels: 84.1 us -> 79.8 us
    pallas_call x1, Pallas kernels: 69.5 us -> 65.3 us  [shards(): pl.pallas_call(kernel, out_shape=(jax.ShapeDtypeStruct((4, width_x, width...]
where the time goes in v12:
time: 87.8 us; the launch traced here: 87.6 us
  Pallas kernels  79.8 us (91%)
  matrix products  2.96 us (3%)
  local copies, waits for them, and re-layouts  1.8 us (2%)
  other arithmetic  1.55 us (2%)
  between operations  1.43 us (2%)
    pallas_call x1, Pallas kernels, shards(): pl.pallas_call(kernel, out_shape=(jax.ShapeDtypeStruct((4, width_x, width...  65.3 us
    pallas_call x1, Pallas kernels, gathered_samples(): pl.pallas_call(functools.partial(samples_kernel, nx, ny), out_shape=jax.S...  14.6 us
    dot_general x1, matrix products, shards(): jnp.einsum('txyz,zn->txyn', forward_field[:, 0], source_z, preferred_elem...  2.19 us
    unnamed x12, local copies, waits for them, and re-layouts  1.8 us

profile of v12, /device:TPU:0, one launch (start us, length us, event | category | flops | bytes accessed | tf_op | source)
XLA Modules:
  0.0 87.6 jit_solution(7438199200678835912)
XLA Ops:
  1.3 0.8 slice_subtract_fusion.1
  2.2 0.0 copy-start.4
  2.2 0.0 copy-start
  2.2 0.0 copy-start.1
  2.2 0.0 copy-start.2
  2.2 0.0 copy-start.3
  2.2 2.2 %fusion.1.local_ref = f32[4,256]{1,0:T(4,128)} fusion(bf16[4,4,8,8,1024]{4,3,2,1,0:T(8,128)(2,1)} %forward.1, s32[256]{0:T(256)S(1)} %bitcast.40, f32[8,8,256]{2,1,0:T(8,128)S(1)} %and_convert_fusion.1), kind=kOutput, calls=%fused_computation.2 | convolution fusion | flops 134609920 | bytes 594944 | tf_op jit(solution)/shard_map/txyz,zn->txyn/dot_general | solution.py:389
  4.4 14.6 %shard_map.95 = f32[4,256]{1,0:T(4,128)} custom-call(f32[4,256]{1,0:T(4,128)} %fusion.1.local_ref), custom_call_target="tpu_custom_call" | custom-call | tf_op jit(solution)/shard_map/pallas_call | solution.py:347
  19.0 0.0 copy-done.4
  19.0 0.7 fusion.14
  19.7 0.8 fusion.5.inj
  20.5 0.0 copy-done
  20.5 0.0 copy-done.1
  20.5 0.0 copy-done.2
  20.5 0.0 copy-done.3
  20.5 65.3 %shard_map.96 = (f32[4,8,8,1024]{3,2,1,0:T(8,128)S(1)}, f32[4,8,8,512]{3,2,1,0:T(8,128)S(1)}) custom-call(f32[4,8,8,1024]{3,2,1,0:T(8,128)S(1)} %bitcast.33, f32[8,8,1024]{2,1,0:T(8,128)S(1)} %copy-done.2, f32[3,1024]{1,0:T(4,128)S(1)} %copy-done.3, bf16[4,4,8,8,1024]{4,3,2,1,0:T(8,128)(2,1)S(1)} %copy-done, f32[4,8,8,1024]{3,2,1,0:T(8,128)S(1)} %fusion.5.inj), custom_call_target="tpu_custom_call" | custom-call | tf_op jit(solution)/shard_map/pallas_call | solution.py:405
  85.8 0.8 copy.15
  86.6 1.0 %copy.16 = f32[1,4,8,8,1024]{4,3,2,1,0:T(8,128)} copy(f32[1,4,8,8,1024]{4,3,2,1,0:T(8,128)S(1)} %bitcast.34) | data formatting | bytes 2097152
  (7 shorter events, 0.1 us)
Async XLA Ops:
  2.2 16.8 %copy-start.4 = (f32[256,4]{0,1:T(4,128)S(1)}, f32[256,4]{0,1:T(4,128)}, u32[]{:S(2)}) copy-start(f32[256,4]{0,1:T(4,128)} %param.15) | copy-start | bytes 12292
  2.2 18.3 %copy-start = (bf16[4,4,8,8,1024]{4,3,2,1,0:T(8,128)(2,1)S(1)}, bf16[4,4,8,8,1024]{4,3,2,1,0:T(8,128)(2,1)}, u32[]{:S(2)}) copy-start(bf16[4,4,8,8,1024]{4,3,2,1,0:T(8,128)(2,1)} %forward.1) | copy-start | bytes 6291460
  2.2 18.3 %copy-start.1 = (f32[1,4,8,8,1024]{4,3,2,1,0:T(8,128)S(1)}, f32[1,4,8,8,1024]{4,3,2,1,0:T(8,128)}, u32[]{:S(2)}) copy-start(f32[1,4,8,8,1024]{4,3,2,1,0:T(8,128)} %param.11) | copy-start | bytes 3145732
  2.2 18.3 %copy-start.2 = (f32[8,8,1024]{2,1,0:T(8,128)S(1)}, f32[8,8,1024]{2,1,0:T(8,128)}, u32[]{:S(2)}) copy-start(f32[8,8,1024]{2,1,0:T(8,128)} %sound.1) | copy-start | bytes 786436
  2.2 18.3 %copy-start.3 = (f32[3,1024]{1,0:T(4,128)S(1)}, f32[3,1024]{1,0:T(4,128)}, u32[]{:S(2)}) copy-start(f32[3,1024]{1,0:T(4,128)} %wind.1) | copy-start | bytes 36868

commit v13 on v12

--- a/solution.py
+++ b/solution.py
@@ -161,11 +161,14 @@
         return carry
 
     [copy_in(x, 0) for x in range(width_x)]
-    forward_copies = exchange(
-        forward.at[:, :, pl.ds(0, 1)], forward.at[:, :, pl.ds(width_x - 1, 1)],
-        fpad.at[:, :, pl.ds(0, 1)], fpad.at[:, :, pl.ds(width_x + 1, 1)],
-        fysend.at[0], fysend.at[1], fyr.at[0], fyr.at[1], fs, fr,
-    )
+    forward_copies = {}
+
+    def send_forward(t):
+        forward_copies[t] = exchange(
+            forward.at[t, :, pl.ds(0, 1)], forward.at[t, :, pl.ds(width_x - 1, 1)],
+            fpad.at[t, :, pl.ds(0, 1)], fpad.at[t, :, pl.ds(width_x + 1, 1)],
+            fysend.at[0, t], fysend.at[1, t], fyr.at[0, t], fyr.at[1, t], fs.at[t], fr.at[t],
+        )
 
     def increment_slab(x, carry, get, snap, first, last):
         xp = x + 1
@@ -197,9 +200,10 @@
             ).start()
         return carry
 
-    def forward_ready():
-        interior.wait()
-        settle(forward_copies)
+    def forward_ready(t, first):
+        if first:
+            interior.wait()
+        settle(forward_copies[t])
 
     for step in range(steps):
         par = step % 2
@@ -218,8 +222,7 @@
             ))
         state_copies, velocity_copies = halves
         if step > 0:
-            if step == 1:
-                forward_ready()
+            forward_ready(snap + 1, step == 1)
             [(functools.partial(
                 increment_slab, get=lambda c, x, par=par: pads[par, c, x + 1],
                 snap=snap + 1, first=step == 1, last=False))(x, 0) for x in range(width_x)]
@@ -253,12 +256,14 @@
             return carry
 
         [pressure_slab(x, 0) for x in range(width_x)]
-        settle(exchange(
+        pressure_copies = exchange(
             pbuf.at[par, pl.ds(1, 1)], pbuf.at[par, pl.ds(width_x, 1)],
             pbuf.at[par, pl.ds(0, 1)], pbuf.at[par, pl.ds(width_x + 1, 1)],
             ypsend.at[0], ypsend.at[1], yprecv.at[par, 0], yprecv.at[par, 1],
             ps, pr,
-        ))
+        )
+        send_forward(snap)
+        settle(pressure_copies)
 
         settle(velocity_copies)
 
@@ -287,8 +292,7 @@
 
         [velocity_slab(x, 0) for x in range(width_x)]
 
-    if steps == 1:
-        forward_ready()
+    forward_ready(0, steps == 1)
     [(functools.partial(
         increment_slab, get=lambda c, x: state_out[c, x], snap=0, first=steps == 1, last=True))(x, 0) for x in range(width_x)]
 
@@ -429,8 +433,8 @@
             pltpu.SemaphoreType.DMA((4,)),
             pltpu.SemaphoreType.DMA((width_x,)),
             pltpu.SemaphoreType.DMA((width_x,)),
-            pltpu.SemaphoreType.DMA((4,)),
-            pltpu.SemaphoreType.DMA((4,)),
+            pltpu.SemaphoreType.DMA((steps_total, 4)),
+            pltpu.SemaphoreType.DMA((steps_total, 4)),
             pltpu.SemaphoreType.DMA((1,)),
         ],
         compiler_params=pltpu.CompilerParams(

time: 87.8 us -> 78 us (0.89)
  Pallas kernels: 79.8 us -> 70 us
    pallas_call x1, Pallas kernels: 65.3 us -> 55.4 us  [shards(): pl.pallas_call(kernel, out_shape=(jax.ShapeDtypeStruct((4, width_x, width...]
where the time goes in v13:
time: 78 us; the launch traced here: 77.7 us
  Pallas kernels  70 us (90%)
  matrix products  2.96 us (4%)
  local copies, waits for them, and re-layouts  1.8 us (2%)
  other arithmetic  1.55 us (2%)
  between operations  1.43 us (2%)
    pallas_call x1, Pallas kernels, shards(): pl.pallas_call(kernel, out_shape=(jax.ShapeDtypeStruct((4, width_x, width...  55.4 us
    pallas_call x1, Pallas kernels, gathered_samples(): pl.pallas_call(functools.partial(samples_kernel, nx, ny), out_shape=jax.S...  14.6 us
    dot_general x1, matrix products, shards(): jnp.einsum('txyz,zn->txyn', forward_field[:, 0], source_z, preferred_elem...  2.19 us
    unnamed x12, local copies, waits for them, and re-layouts  1.8 us

profile of v13, /device:TPU:0, one launch (start us, length us, event | category | flops | bytes accessed | tf_op | source)
XLA Modules:
  0.0 77.7 jit_solution(782452720961926685)
XLA Ops:
  1.3 0.8 %slice_subtract_fusion.1 = (s32[256,1]{0,1:T(1,128)S(1)}, s32[256,1]{0,1:T(1,128)S(1)}, s32[256,1]{0,1:T(1,128)S(1)}, s32[256,1]{0,1:T(1,128)S(1)}, s32[256,1]{0,1:T(1,128)S(1)}, /*index=5*/s32[256,1]{0,1:T(1,128)S(1)}) fusion(s32[256,3]{0,1:T(4,128)} %param.14, s32[]{:T(128)S(6)} %mul.38, s32[]{:T(128)S(6)} %mul.39, s32[256,3]{0,1:T(4,128)} %param.13), kind=kLoop, calls=%fused_computation.25 | loop fusion | flops 1024 | bytes 12296 | tf_op jit(solution)/shard_map/sub | solution.py:388
  2.2 0.0 copy-start.4
  2.2 0.0 copy-start
  2.2 0.0 copy-start.1
  2.2 0.0 copy-start.2
  2.2 0.0 copy-start.3
  2.2 2.2 %fusion.1.local_ref = f32[4,256]{1,0:T(4,128)} fusion(bf16[4,4,8,8,1024]{4,3,2,1,0:T(8,128)(2,1)} %forward.1, s32[256]{0:T(256)S(1)} %bitcast.40, f32[8,8,256]{2,1,0:T(8,128)S(1)} %and_convert_fusion.1), kind=kOutput, calls=%fused_computation.2 | convolution fusion | flops 134609920 | bytes 594944 | tf_op jit(solution)/shard_map/txyz,zn->txyn/dot_general | solution.py:393
  4.4 14.6 %shard_map.95 = f32[4,256]{1,0:T(4,128)} custom-call(f32[4,256]{1,0:T(4,128)} %fusion.1.local_ref), custom_call_target="tpu_custom_call" | custom-call | tf_op jit(solution)/shard_map/pallas_call | solution.py:351
  19.0 0.0 copy-done.4
  19.0 0.7 fusion.14
  19.7 0.8 fusion.5.inj
  20.5 0.0 copy-done
  20.5 0.0 copy-done.1
  20.5 0.0 copy-done.2
  20.5 0.0 copy-done.3
  20.5 55.4 %shard_map.96 = (f32[4,8,8,1024]{3,2,1,0:T(8,128)S(1)}, f32[4,8,8,512]{3,2,1,0:T(8,128)S(1)}) custom-call(f32[4,8,8,1024]{3,2,1,0:T(8,128)S(1)} %bitcast.33, f32[8,8,1024]{2,1,0:T(8,128)S(1)} %copy-done.2, f32[3,1024]{1,0:T(4,128)S(1)} %copy-done.3, bf16[4,4,8,8,1024]{4,3,2,1,0:T(8,128)(2,1)S(1)} %copy-done, f32[4,8,8,1024]{3,2,1,0:T(8,128)S(1)} %fusion.5.inj), custom_call_target="tpu_custom_call" | custom-call | tf_op jit(solution)/shard_map/pallas_call | solution.py:409
  76.0 0.8 %copy.15 = f32[4,8,8,512]{3,2,1,0:T(8,128)} copy(f32[4,8,8,512]{3,2,1,0:T(8,128)S(1)} %get-tuple-element.17) | data formatting | bytes 1048576
  76.8 1.0 %copy.16 = f32[1,4,8,8,1024]{4,3,2,1,0:T(8,128)} copy(f32[1,4,8,8,1024]{4,3,2,1,0:T(8,128)S(1)} %bitcast.34) | data formatting | bytes 2097152
  (7 shorter events, 0.1 us)
Async XLA Ops:
  2.2 16.8 %copy-start.4 = (f32[256,4]{0,1:T(4,128)S(1)}, f32[256,4]{0,1:T(4,128)}, u32[]{:S(2)}) copy-start(f32[256,4]{0,1:T(4,128)} %param.15) | copy-start | bytes 12292
  2.2 18.3 %copy-start = (bf16[4,4,8,8,1024]{4,3,2,1,0:T(8,128)(2,1)S(1)}, bf16[4,4,8,8,1024]{4,3,2,1,0:T(8,128)(2,1)}, u32[]{:S(2)}) copy-start(bf16[4,4,8,8,1024]{4,3,2,1,0:T(8,128)(2,1)} %forward.1) | copy-start | bytes 6291460
  2.2 18.3 %copy-start.1 = (f32[1,4,8,8,1024]{4,3,2,1,0:T(8,128)S(1)}, f32[1,4,8,8,1024]{4,3,2,1,0:T(8,128)}, u32[]{:S(2)}) copy-start(f32[1,4,8,8,1024]{4,3,2,1,0:T(8,128)} %param.11) | copy-start | bytes 3145732
  2.2 18.3 %copy-start.2 = (f32[8,8,1024]{2,1,0:T(8,128)S(1)}, f32[8,8,1024]{2,1,0:T(8,128)}, u32[]{:S(2)}) copy-start(f32[8,8,1024]{2,1,0:T(8,128)} %sound.1) | copy-start | bytes 786436
  2.2 18.3 %copy-start.3 = (f32[3,1024]{1,0:T(4,128)S(1)}, f32[3,1024]{1,0:T(4,128)}, u32[]{:S(2)}) copy-start(f32[3,1024]{1,0:T(4,128)} %wind.1) | copy-start | bytes 36868

commit v14 on v13

--- a/solution.py
+++ b/solution.py
@@ -84,7 +84,6 @@
                 fysend[1, t, c // 2, row:row + 1, :] = f[0:1, :]
         return carry
 
-    [forward_rows(x, 0) for x in range(width_x)]
     interior = pltpu.make_async_copy(forward, fpad.at[:, :, pl.ds(1, width_x)], local_sem.at[0])
     interior.start()
     for par in range(2):
@@ -101,7 +100,6 @@
         (gx + nx - 1) // nx + (2 * nx - 2 - gx) // nx
         + (gy + ny - 1) // ny + (2 * ny - 2 - gy) // ny
     )
-    pl.semaphore_wait(barrier, peers)
 
     iy = lax.broadcasted_iota(jnp.int32, (width_y, depth), 0)
     iz = lax.broadcasted_iota(jnp.int32, (width_y, depth), 1)
@@ -161,6 +159,7 @@
         return carry
 
     [copy_in(x, 0) for x in range(width_x)]
+    pl.semaphore_wait(barrier, peers)
     forward_copies = {}
 
     def send_forward(t):
@@ -221,6 +220,8 @@
                 ss.at[par, part], rs.at[par, part],
             ))
         state_copies, velocity_copies = halves
+        if step == 0:
+            [forward_rows(x, 0) for x in range(width_x)]
         if step > 0:
             forward_ready(snap + 1, step == 1)
             [(functools.partial(

time: 78 us -> 77.3 us (level)
  no operation moved by 1% of the time
where the time goes in v14:
time: 77.3 us; the launch traced here: 77 us
  Pallas kernels  69.3 us (90%)
  matrix products  2.96 us (4%)
  local copies, waits for them, and re-layouts  1.8 us (2%)
  other arithmetic  1.55 us (2%)
  between operations  1.43 us (2%)
    pallas_call x1, Pallas kernels, shards(): pl.pallas_call(kernel, out_shape=(jax.ShapeDtypeStruct((4, width_x, width...  54.7 us
    pallas_call x1, Pallas kernels, gathered_samples(): pl.pallas_call(functools.partial(samples_kernel, nx, ny), out_shape=jax.S...  14.6 us
    dot_general x1, matrix products, shards(): jnp.einsum('txyz,zn->txyn', forward_field[:, 0], source_z, preferred_elem...  2.19 us
    unnamed x12, local copies, waits for them, and re-layouts  1.8 us

profile of v14, /device:TPU:0, one launch (start us, length us, event | category | flops | bytes accessed | tf_op | source)
XLA Modules:
  0.0 77.0 jit_solution(2675790950157518171)
XLA Ops:
  1.3 0.8 %slice_subtract_fusion.1 = (s32[256,1]{0,1:T(1,128)S(1)}, s32[256,1]{0,1:T(1,128)S(1)}, s32[256,1]{0,1:T(1,128)S(1)}, s32[256,1]{0,1:T(1,128)S(1)}, s32[256,1]{0,1:T(1,128)S(1)}, /*index=5*/s32[256,1]{0,1:T(1,128)S(1)}) fusion(s32[256,3]{0,1:T(4,128)} %param.14, s32[]{:T(128)S(6)} %mul.38, s32[]{:T(128)S(6)} %mul.39, s32[256,3]{0,1:T(4,128)} %param.13), kind=kLoop, calls=%fused_computation.25 | loop fusion | flops 1024 | bytes 12296 | tf_op jit(solution)/shard_map/sub | solution.py:389
  2.2 0.0 copy-start.4
  2.2 0.0 copy-start
  2.2 0.0 copy-start.1
  2.2 0.0 copy-start.2
  2.2 0.0 copy-start.3
  2.2 2.2 %fusion.1.local_ref = f32[4,256]{1,0:T(4,128)} fusion(bf16[4,4,8,8,1024]{4,3,2,1,0:T(8,128)(2,1)} %forward.1, s32[256]{0:T(256)S(1)} %bitcast.40, f32[8,8,256]{2,1,0:T(8,128)S(1)} %and_convert_fusion.1), kind=kOutput, calls=%fused_computation.2 | convolution fusion | flops 134609920 | bytes 594944 | tf_op jit(solution)/shard_map/txyz,zn->txyn/dot_general | solution.py:394
  4.4 14.6 %shard_map.95 = f32[4,256]{1,0:T(4,128)} custom-call(f32[4,256]{1,0:T(4,128)} %fusion.1.local_ref), custom_call_target="tpu_custom_call" | custom-call | tf_op jit(solution)/shard_map/pallas_call | solution.py:352
  19.0 0.0 copy-done.4
  19.0 0.7 fusion.14
  19.7 0.8 %fusion.5.inj = f32[4,8,8,1024]{3,2,1,0:T(8,128)S(1)} fusion(s32[256]{0:T(256)S(1)} %bitcast.35, f32[8,8,256]{2,1,0:T(8,128)S(1)} %and_convert_fusion, f32[4,256]{1,0:T(4,128)S(1)} %fusion.14), kind=kOutput, calls=%fused_computation.7 | convolution fusion | flops 805634048 | bytes 1119232 | tf_op jit(solution)/shard_map/txyn,nz->txyz/dot_general | solution.py:402
  20.5 0.0 copy-done
  20.5 0.0 copy-done.1
  20.5 0.0 copy-done.2
  20.5 0.0 copy-done.3
  20.5 54.7 %shard_map.96 = (f32[4,8,8,1024]{3,2,1,0:T(8,128)S(1)}, f32[4,8,8,512]{3,2,1,0:T(8,128)S(1)}) custom-call(f32[4,8,8,1024]{3,2,1,0:T(8,128)S(1)} %bitcast.33, f32[8,8,1024]{2,1,0:T(8,128)S(1)} %copy-done.2, f32[3,1024]{1,0:T(4,128)S(1)} %copy-done.3, bf16[4,4,8,8,1024]{4,3,2,1,0:T(8,128)(2,1)S(1)} %copy-done, f32[4,8,8,1024]{3,2,1,0:T(8,128)S(1)} %fusion.5.inj), custom_call_target="tpu_custom_call" | custom-call | tf_op jit(solution)/shard_map/pallas_call | solution.py:410
  75.3 0.8 %copy.15 = f32[4,8,8,512]{3,2,1,0:T(8,128)} copy(f32[4,8,8,512]{3,2,1,0:T(8,128)S(1)} %get-tuple-element.17) | data formatting | bytes 1048576
  76.1 1.0 %copy.16 = f32[1,4,8,8,1024]{4,3,2,1,0:T(8,128)} copy(f32[1,4,8,8,1024]{4,3,2,1,0:T(8,128)S(1)} %bitcast.34) | data formatting | bytes 2097152
  (7 shorter events, 0.1 us)
Async XLA Ops:
  2.2 16.8 %copy-start.4 = (f32[256,4]{0,1:T(4,128)S(1)}, f32[256,4]{0,1:T(4,128)}, u32[]{:S(2)}) copy-start(f32[256,4]{0,1:T(4,128)} %param.15) | copy-start | bytes 12292
  2.2 18.3 %copy-start = (bf16[4,4,8,8,1024]{4,3,2,1,0:T(8,128)(2,1)S(1)}, bf16[4,4,8,8,1024]{4,3,2,1,0:T(8,128)(2,1)}, u32[]{:S(2)}) copy-start(bf16[4,4,8,8,1024]{4,3,2,1,0:T(8,128)(2,1)} %forward.1) | copy-start | bytes 6291460
  2.2 18.3 %copy-start.1 = (f32[1,4,8,8,1024]{4,3,2,1,0:T(8,128)S(1)}, f32[1,4,8,8,1024]{4,3,2,1,0:T(8,128)}, u32[]{:S(2)}) copy-start(f32[1,4,8,8,1024]{4,3,2,1,0:T(8,128)} %param.11) | copy-start | bytes 3145732
  2.2 18.3 %copy-start.2 = (f32[8,8,1024]{2,1,0:T(8,128)S(1)}, f32[8,8,1024]{2,1,0:T(8,128)}, u32[]{:S(2)}) copy-start(f32[8,8,1024]{2,1,0:T(8,128)} %sound.1) | copy-start | bytes 786436
  2.2 18.3 %copy-start.3 = (f32[3,1024]{1,0:T(4,128)S(1)}, f32[3,1024]{1,0:T(4,128)}, u32[]{:S(2)}) copy-start(f32[3,1024]{1,0:T(4,128)} %wind.1) | copy-start | bytes 36868

commit v15 on v14

--- a/solution.py
+++ b/solution.py
@@ -313,34 +313,31 @@
     [add_partner(x, 0) for x in range(width_x)]
 
 
-def samples_kernel(nx, ny, local_ref, out_ref, sent, got_x, got_y, send_sem, recv_sem):
+def samples_kernel(nx, ny, local_ref, out_ref, got, send_sem, recv_sem):
     me_p = lax.axis_index("pair")
     gx = lax.axis_index("gx")
     gy = lax.axis_index("gy")
-    peers_x = [(me_p, (gx + d) % nx, gy) for d in range(1, nx)]
-    peers_y = [(me_p, gx, (gy + d) % ny) for d in range(1, ny)]
+    peers = [
+        (me_p, (gx + dx) % nx, (gy + dy) % ny)
+        for dx in range(nx) for dy in range(ny) if dx or dy
+    ]
     barrier = pltpu.get_barrier_semaphore()
-    for dev in peers_x + peers_y:
+    for dev in peers:
         pl.semaphore_signal(barrier, 1, device_id=dev, device_id_type=MESH)
-    pl.semaphore_wait(barrier, len(peers_x) + len(peers_y))
-    rounds = ((local_ref, got_x, peers_x, 0), (sent, got_y, peers_y, nx - 1))
+    pl.semaphore_wait(barrier, len(peers))
+    copies = []
+    for i, dev in enumerate(peers):
+        copy = pltpu.make_async_remote_copy(
+            src_ref=local_ref, dst_ref=got.at[i], send_sem=send_sem.at[i],
+            recv_sem=recv_sem.at[i], device_id=dev, device_id_type=MESH,
+        )
+        copy.start()
+        copies.append(copy)
     total = local_ref[...]
-    for src, got, peers, base in rounds:
-        copies = []
-        for i, dev in enumerate(peers):
-            copy = pltpu.make_async_remote_copy(
-                src_ref=src, dst_ref=got.at[i], send_sem=send_sem.at[base + i],
-                recv_sem=recv_sem.at[base + i], device_id=dev, device_id_type=MESH,
-            )
-            copy.start()
-            copies.append(copy)
-        for copy in copies:
-            copy.wait_send()
-            copy.wait_recv()
-        for i in range(len(peers)):
-            total = total + got[i]
-        if base == 0:
-            sent[...] = total
+    for i, copy in enumerate(copies):
+        copy.wait_send()
+        copy.wait_recv()
+        total = total + got[i]
     out_ref[...] = total
 
 
@@ -355,11 +352,9 @@
         in_specs=[vmem],
         out_specs=vmem,
         scratch_shapes=[
-            pltpu.VMEM(local_samples.shape, jnp.float32),
-            pltpu.VMEM((nx - 1,) + local_samples.shape, jnp.float32),
-            pltpu.VMEM((ny - 1,) + local_samples.shape, jnp.float32),
-            pltpu.SemaphoreType.DMA((nx + ny - 2,)),
-            pltpu.SemaphoreType.DMA((nx + ny - 2,)),
+            pltpu.VMEM((nx * ny - 1,) + local_samples.shape, jnp.float32),
+            pltpu.SemaphoreType.DMA((nx * ny - 1,)),
+            pltpu.SemaphoreType.DMA((nx * ny - 1,)),
         ],
         compiler_params=pltpu.CompilerParams(collective_id=1, has_side_effects=True),
     )(local_samples)

time: 77.3 us -> 79.7 us (1.031)
  Pallas kernels: 69.3 us -> 71.7 us
    pallas_call x1, Pallas kernels: 14.6 us -> 16.3 us  [gathered_samples(): pl.pallas_call(functools.partial(samples_kernel, nx, ny), out_shape=jax.S...]
where the time goes in v15:
time: 79.7 us; the launch traced here: 79.5 us
  Pallas kernels  71.7 us (90%)
  matrix products  2.96 us (4%)
  local copies, waits for them, and re-layouts  1.8 us (2%)
  other arithmetic  1.55 us (2%)
  between operations  1.43 us (2%)
    pallas_call x1, Pallas kernels, shards(): pl.pallas_call(kernel, out_shape=(jax.ShapeDtypeStruct((4, width_x, width...  55.5 us
    pallas_call x1, Pallas kernels, gathered_samples(): pl.pallas_call(functools.partial(samples_kernel, nx, ny), out_shape=jax.S...  16.3 us
    dot_general x1, matrix products, shards(): jnp.einsum('txyz,zn->txyn', forward_field[:, 0], source_z, preferred_elem...  2.19 us
    unnamed x12, local copies, waits for them, and re-layouts  1.8 us

profile of v15, /device:TPU:0, one launch (start us, length us, event | category | flops | bytes accessed | tf_op | source)
XLA Modules:
  0.0 79.5 jit_solution(15616721781455090093)
XLA Ops:
  1.3 0.8 %slice_subtract_fusion.1 = (s32[256,1]{0,1:T(1,128)S(1)}, s32[256,1]{0,1:T(1,128)S(1)}, s32[256,1]{0,1:T(1,128)S(1)}, s32[256,1]{0,1:T(1,128)S(1)}, s32[256,1]{0,1:T(1,128)S(1)}, /*index=5*/s32[256,1]{0,1:T(1,128)S(1)}) fusion(s32[256,3]{0,1:T(4,128)} %param.14, s32[]{:T(128)S(6)} %mul.38, s32[]{:T(128)S(6)} %mul.39, s32[256,3]{0,1:T(4,128)} %param.13), kind=kLoop, calls=%fused_computation.25 | loop fusion | flops 1024 | bytes 12296 | tf_op jit(solution)/shard_map/sub | solution.py:384
  2.2 0.0 copy-start.4
  2.2 0.0 copy-start
  2.2 0.0 copy-start.1
  2.2 0.0 copy-start.2
  2.2 0.0 copy-start.3
  2.2 2.2 %fusion.1.local_ref = f32[4,256]{1,0:T(4,128)} fusion(bf16[4,4,8,8,1024]{4,3,2,1,0:T(8,128)(2,1)} %forward.1, s32[256]{0:T(256)S(1)} %bitcast.40, f32[8,8,256]{2,1,0:T(8,128)S(1)} %and_convert_fusion.1), kind=kOutput, calls=%fused_computation.2 | convolution fusion | flops 134609920 | bytes 594944 | tf_op jit(solution)/shard_map/txyz,zn->txyn/dot_general | solution.py:389
  4.4 16.3 %shard_map.95 = f32[4,256]{1,0:T(4,128)} custom-call(f32[4,256]{1,0:T(4,128)} %fusion.1.local_ref), custom_call_target="tpu_custom_call" | custom-call | tf_op jit(solution)/shard_map/pallas_call | solution.py:349
  20.7 0.0 copy-done.4
  20.7 0.7 fusion.14
  21.4 0.8 fusion.5.inj
  22.2 0.0 copy-done
  22.2 0.0 copy-done.1
  22.2 0.0 copy-done.2
  22.2 0.0 copy-done.3
  22.2 55.5 %shard_map.96 = (f32[4,8,8,1024]{3,2,1,0:T(8,128)S(1)}, f32[4,8,8,512]{3,2,1,0:T(8,128)S(1)}) custom-call(f32[4,8,8,1024]{3,2,1,0:T(8,128)S(1)} %bitcast.33, f32[8,8,1024]{2,1,0:T(8,128)S(1)} %copy-done.2, f32[3,1024]{1,0:T(4,128)S(1)} %copy-done.3, bf16[4,4,8,8,1024]{4,3,2,1,0:T(8,128)(2,1)S(1)} %copy-done, f32[4,8,8,1024]{3,2,1,0:T(8,128)S(1)} %fusion.5.inj), custom_call_target="tpu_custom_call" | custom-call | tf_op jit(solution)/shard_map/pallas_call | solution.py:405
  77.7 0.8 %copy.15 = f32[4,8,8,512]{3,2,1,0:T(8,128)} copy(f32[4,8,8,512]{3,2,1,0:T(8,128)S(1)} %get-tuple-element.17) | data formatting | bytes 1048576
  78.5 1.0 %copy.16 = f32[1,4,8,8,1024]{4,3,2,1,0:T(8,128)} copy(f32[1,4,8,8,1024]{4,3,2,1,0:T(8,128)S(1)} %bitcast.34) | data formatting | bytes 2097152
  (7 shorter events, 0.1 us)
Async XLA Ops:
  2.2 18.5 %copy-start.4 = (f32[256,4]{0,1:T(4,128)S(1)}, f32[256,4]{0,1:T(4,128)}, u32[]{:S(2)}) copy-start(f32[256,4]{0,1:T(4,128)} %param.15) | copy-start | bytes 12292
  2.2 20.0 %copy-start = (bf16[4,4,8,8,1024]{4,3,2,1,0:T(8,128)(2,1)S(1)}, bf16[4,4,8,8,1024]{4,3,2,1,0:T(8,128)(2,1)}, u32[]{:S(2)}) copy-start(bf16[4,4,8,8,1024]{4,3,2,1,0:T(8,128)(2,1)} %forward.1) | copy-start | bytes 6291460
  2.2 20.0 %copy-start.1 = (f32[1,4,8,8,1024]{4,3,2,1,0:T(8,128)S(1)}, f32[1,4,8,8,1024]{4,3,2,1,0:T(8,128)}, u32[]{:S(2)}) copy-start(f32[1,4,8,8,1024]{4,3,2,1,0:T(8,128)} %param.11) | copy-start | bytes 3145732
  2.2 20.0 %copy-start.2 = (f32[8,8,1024]{2,1,0:T(8,128)S(1)}, f32[8,8,1024]{2,1,0:T(8,128)}, u32[]{:S(2)}) copy-start(f32[8,8,1024]{2,1,0:T(8,128)} %sound.1) | copy-start | bytes 786436
  2.2 20.0 %copy-start.3 = (f32[3,1024]{1,0:T(4,128)S(1)}, f32[3,1024]{1,0:T(4,128)}, u32[]{:S(2)}) copy-start(f32[3,1024]{1,0:T(4,128)} %wind.1) | copy-start | bytes 36868

commit v16 on v13

--- a/solution.py
+++ b/solution.py
@@ -39,7 +39,7 @@
     nx, ny, steps,
     state_in, sound, wind, forward, inj,
     state_out, kernel_out,
-    pads, pbuf, ysend, yrecv, ypsend, yprecv, acc_out, ksend, krecv, fpad, fysend, fyr,
+    pads, pbuf, ysend, yrecv, ypsend, yprecv, acc_out, ksend, krecv, fpad, fysend, fyr, advect,
     ss, rs, ps, pr, ks, kr, fs, fr, local_sem,
 ):
     _, width_x, width_y, depth = state_in.shape
@@ -263,9 +263,21 @@
             ps, pr,
         )
         send_forward(snap)
+        settle(velocity_copies)
+
+        def advection_slab(x, carry, par=par):
+            xp = x + 1
+            old = pads.at[par]
+            for i in range(3):
+                a = old[1 + i, xp]
+                dxa = (old[1 + i, xp + 1] - old[1 + i, x]) * 0.5
+                dya = dy(a, yrecv[par, 0, Y_SLOT[1 + i], x:x + 1, :], yrecv[par, 1, Y_SLOT[1 + i], x:x + 1, :])
+                dza = dz(a)
+                advect[i, x] = we * dxa + wn * dya + wv * dza
+            return carry
+
+        [advection_slab(x, 0) for x in range(width_x)]
         settle(pressure_copies)
-
-        settle(velocity_copies)
 
         def velocity_slab(x, carry, par=par, nxt=nxt, last=last):
             xp = x + 1
@@ -278,11 +290,7 @@
             )
             new_state = [p_new]
             for i in range(3):
-                a = old[1 + i, xp]
-                dxa = (old[1 + i, xp + 1] - old[1 + i, x]) * 0.5
-                dya = dy(a, yrecv[par, 0, Y_SLOT[1 + i], x:x + 1, :], yrecv[par, 1, Y_SLOT[1 + i], x:x + 1, :])
-                dza = dz(a)
-                new_state.append(a + step_length * (grad[i] + we * dxa + wn * dya + wv * dza))
+                new_state.append(old[1 + i, xp] + step_length * (grad[i] + advect[i, x]))
             for c in range(4):
                 if last:
                     state_out[c, x] = new_state[c]
@@ -427,6 +435,7 @@
             pltpu.VMEM((steps_total, 4, width_x + 2, width_y, depth), forward_field.dtype),
             pltpu.VMEM((2, steps_total, 2, 2 * width_x, depth), forward_field.dtype),
             pltpu.VMEM((2, steps_total, 2, 2 * width_x, depth), forward_field.dtype),
+            pltpu.VMEM((3, width_x, width_y, depth), jnp.float32),
             pltpu.SemaphoreType.DMA((2, 2, 4)),
             pltpu.SemaphoreType.DMA((2, 2, 4)),
             pltpu.SemaphoreType.DMA((4,)),

time: 78 us -> 76.8 us (0.985)
  Pallas kernels: 70 us -> 68.8 us
    pallas_call x1, Pallas kernels: 55.4 us -> 54.2 us  [shards(): pl.pallas_call(kernel, out_shape=(jax.ShapeDtypeStruct((4, width_x, width...]
where the time goes in v16:
time: 76.8 us; the launch traced here: 76.5 us
  Pallas kernels  68.8 us (90%)
  matrix products  2.96 us (4%)
  local copies, waits for them, and re-layouts  1.8 us (2%)
  other arithmetic  1.55 us (2%)
  between operations  1.43 us (2%)
    pallas_call x1, Pallas kernels, shards(): pl.pallas_call(kernel, out_shape=(jax.ShapeDtypeStruct((4, width_x, width...  54.2 us
    pallas_call x1, Pallas kernels, gathered_samples(): pl.pallas_call(functools.partial(samples_kernel, nx, ny), out_shape=jax.S...  14.6 us
    dot_general x1, matrix products, shards(): jnp.einsum('txyz,zn->txyn', forward_field[:, 0], source_z, preferred_elem...  2.19 us
    unnamed x12, local copies, waits for them, and re-layouts  1.8 us

profile of v16, /device:TPU:0, one launch (start us, length us, event | category | flops | bytes accessed | tf_op | source)
XLA Modules:
  0.0 76.5 jit_solution(5437698561709804984)
XLA Ops:
  1.3 0.8 %slice_subtract_fusion.1 = (s32[256,1]{0,1:T(1,128)S(1)}, s32[256,1]{0,1:T(1,128)S(1)}, s32[256,1]{0,1:T(1,128)S(1)}, s32[256,1]{0,1:T(1,128)S(1)}, s32[256,1]{0,1:T(1,128)S(1)}, /*index=5*/s32[256,1]{0,1:T(1,128)S(1)}) fusion(s32[256,3]{0,1:T(4,128)} %param.14, s32[]{:T(128)S(6)} %mul.38, s32[]{:T(128)S(6)} %mul.39, s32[256,3]{0,1:T(4,128)} %param.13), kind=kLoop, calls=%fused_computation.25 | loop fusion | flops 1024 | bytes 12296 | tf_op jit(solution)/shard_map/sub | solution.py:396
  2.2 0.0 copy-start.4
  2.2 0.0 copy-start
  2.2 0.0 copy-start.1
  2.2 0.0 copy-start.2
  2.2 0.0 copy-start.3
  2.2 2.2 %fusion.1.local_ref = f32[4,256]{1,0:T(4,128)} fusion(bf16[4,4,8,8,1024]{4,3,2,1,0:T(8,128)(2,1)} %forward.1, s32[256]{0:T(256)S(1)} %bitcast.40, f32[8,8,256]{2,1,0:T(8,128)S(1)} %and_convert_fusion.1), kind=kOutput, calls=%fused_computation.2 | convolution fusion | flops 134609920 | bytes 594944 | tf_op jit(solution)/shard_map/txyz,zn->txyn/dot_general | solution.py:401
  4.4 14.6 %shard_map.95 = f32[4,256]{1,0:T(4,128)} custom-call(f32[4,256]{1,0:T(4,128)} %fusion.1.local_ref), custom_call_target="tpu_custom_call" | custom-call | tf_op jit(solution)/shard_map/pallas_call | solution.py:359
  19.0 0.0 copy-done.4
  19.0 0.7 fusion.14
  19.7 0.8 %fusion.5.inj = f32[4,8,8,1024]{3,2,1,0:T(8,128)S(1)} fusion(s32[256]{0:T(256)S(1)} %bitcast.35, f32[8,8,256]{2,1,0:T(8,128)S(1)} %and_convert_fusion, f32[4,256]{1,0:T(4,128)S(1)} %fusion.14), kind=kOutput, calls=%fused_computation.7 | convolution fusion | flops 805634048 | bytes 1119232 | tf_op jit(solution)/shard_map/txyn,nz->txyz/dot_general | solution.py:409
  20.5 0.0 copy-done
  20.5 0.0 copy-done.1
  20.5 0.0 copy-done.2
  20.5 0.0 copy-done.3
  20.5 54.2 %shard_map.96 = (f32[4,8,8,1024]{3,2,1,0:T(8,128)S(1)}, f32[4,8,8,512]{3,2,1,0:T(8,128)S(1)}) custom-call(f32[4,8,8,1024]{3,2,1,0:T(8,128)S(1)} %bitcast.33, f32[8,8,1024]{2,1,0:T(8,128)S(1)} %copy-done.2, f32[3,1024]{1,0:T(4,128)S(1)} %copy-done.3, bf16[4,4,8,8,1024]{4,3,2,1,0:T(8,128)(2,1)S(1)} %copy-done, f32[4,8,8,1024]{3,2,1,0:T(8,128)S(1)} %fusion.5.inj), custom_call_target="tpu_custom_call" | custom-call | tf_op jit(solution)/shard_map/pallas_call | solution.py:417
  74.8 0.8 %copy.15 = f32[4,8,8,512]{3,2,1,0:T(8,128)} copy(f32[4,8,8,512]{3,2,1,0:T(8,128)S(1)} %get-tuple-element.17) | data formatting | bytes 1048576
  75.6 1.0 %copy.16 = f32[1,4,8,8,1024]{4,3,2,1,0:T(8,128)} copy(f32[1,4,8,8,1024]{4,3,2,1,0:T(8,128)S(1)} %bitcast.34) | data formatting | bytes 2097152
  (7 shorter events, 0.1 us)
Async XLA Ops:
  2.2 16.8 %copy-start.4 = (f32[256,4]{0,1:T(4,128)S(1)}, f32[256,4]{0,1:T(4,128)}, u32[]{:S(2)}) copy-start(f32[256,4]{0,1:T(4,128)} %param.15) | copy-start | bytes 12292
  2.2 18.3 %copy-start = (bf16[4,4,8,8,1024]{4,3,2,1,0:T(8,128)(2,1)S(1)}, bf16[4,4,8,8,1024]{4,3,2,1,0:T(8,128)(2,1)}, u32[]{:S(2)}) copy-start(bf16[4,4,8,8,1024]{4,3,2,1,0:T(8,128)(2,1)} %forward.1) | copy-start | bytes 6291460
  2.2 18.3 %copy-start.1 = (f32[1,4,8,8,1024]{4,3,2,1,0:T(8,128)S(1)}, f32[1,4,8,8,1024]{4,3,2,1,0:T(8,128)}, u32[]{:S(2)}) copy-start(f32[1,4,8,8,1024]{4,3,2,1,0:T(8,128)} %param.11) | copy-start | bytes 3145732
  2.2 18.3 %copy-start.2 = (f32[8,8,1024]{2,1,0:T(8,128)S(1)}, f32[8,8,1024]{2,1,0:T(8,128)}, u32[]{:S(2)}) copy-start(f32[8,8,1024]{2,1,0:T(8,128)} %sound.1) | copy-start | bytes 786436
  2.2 18.3 %copy-start.3 = (f32[3,1024]{1,0:T(4,128)S(1)}, f32[3,1024]{1,0:T(4,128)}, u32[]{:S(2)}) copy-start(f32[3,1024]{1,0:T(4,128)} %wind.1) | copy-start | bytes 36868

commit v17 on v16

--- a/solution.py
+++ b/solution.py
@@ -39,7 +39,7 @@
     nx, ny, steps,
     state_in, sound, wind, forward, inj,
     state_out, kernel_out,
-    pads, pbuf, ysend, yrecv, ypsend, yprecv, acc_out, ksend, krecv, fpad, fysend, fyr, advect,
+    pads, pbuf, ysend, yrecv, ypsend, yprecv, acc_out, ksend, krecv, fpad, fysend, fyr, advect, early,
     ss, rs, ps, pr, ks, kr, fs, fr, local_sem,
 ):
     _, width_x, width_y, depth = state_in.shape
@@ -226,30 +226,37 @@
             [(functools.partial(
                 increment_slab, get=lambda c, x, par=par: pads[par, c, x + 1],
                 snap=snap + 1, first=step == 1, last=False))(x, 0) for x in range(width_x)]
+        if step > 0:
+            def early_slab(x, carry, par=par):
+                xp = x + 1
+                held = pbuf.at[1 - par]
+                p = held[xp]
+                dxp = (held[xp + 1] - held[x]) * 0.5
+                dyp = dy(p, yprecv[1 - par, 0, x:x + 1, :], yprecv[1 - par, 1, x:x + 1, :])
+                early[0, x] = we * dxp + wn * dyp + wv * dz(p)
+                early[1, x] = dz(pads[par, 3, xp])
+                return carry
+
+            [early_slab(x, 0) for x in range(width_x)]
         settle(state_copies)
 
         def pressure_slab(x, carry, par=par, snap=snap, step=step):
             xp = x + 1
             old = pads.at[par]
+            dxa = (old[1, xp + 1] - old[1, x]) * 0.5
+            dya = dy(old[2, xp], yrecv[par, 0, Y_SLOT[2], x:x + 1, :], yrecv[par, 1, Y_SLOT[2], x:x + 1, :])
             if step == 0:
                 p = old[0, xp]
                 dxp = (old[0, xp + 1] - old[0, x]) * 0.5
                 dyp = dy(p, yrecv[par, 0, Y_SLOT[0], x:x + 1, :], yrecv[par, 1, Y_SLOT[0], x:x + 1, :])
+                rest = we * dxp + wn * dyp + wv * dz(p)
+                dza = dz(old[3, xp])
             else:
-                held = pbuf.at[1 - par]
-                p = held[xp]
-                dxp = (held[xp + 1] - held[x]) * 0.5
-                dyp = dy(p, yprecv[1 - par, 0, x:x + 1, :], yprecv[1 - par, 1, x:x + 1, :])
-            dxa = (old[1, xp + 1] - old[1, x]) * 0.5
-            dya = dy(old[2, xp], yrecv[par, 0, Y_SLOT[2], x:x + 1, :], yrecv[par, 1, Y_SLOT[2], x:x + 1, :])
-            dzp = dz(p)
-            dza = dz(old[3, xp])
+                p = pbuf[1 - par, xp]
+                rest = early[0, x]
+                dza = early[1, x]
             divergence = dxa + dya + dza
-            p_new = (
-                p
-                + step_length * (sound[x] * divergence + we * dxp + wn * dyp + wv * dzp)
-                + inj[snap, x]
-            )
+            p_new = p + step_length * (sound[x] * divergence + rest) + inj[snap, x]
             pbuf[par, xp] = p_new
             ypsend[0, x:x + 1, :] = p_new[width_y - 1:width_y, :]
             ypsend[1, x:x + 1, :] = p_new[0:1, :]
@@ -436,6 +443,7 @@
             pltpu.VMEM((2, steps_total, 2, 2 * width_x, depth), forward_field.dtype),
             pltpu.VMEM((2, steps_total, 2, 2 * width_x, depth), forward_field.dtype),
             pltpu.VMEM((3, width_x, width_y, depth), jnp.float32),
+            pltpu.VMEM((2, width_x, width_y, depth), jnp.float32),
             pltpu.SemaphoreType.DMA((2, 2, 4)),
             pltpu.SemaphoreType.DMA((2, 2, 4)),
             pltpu.SemaphoreType.DMA((4,)),

time: 76.8 us -> 76 us (0.990)
  Pallas kernels: 68.8 us -> 68 us
    pallas_call x1, Pallas kernels: 54.2 us -> 53.4 us  [shards(): pl.pallas_call(kernel, out_shape=(jax.ShapeDtypeStruct((4, width_x, width...]
where the time goes in v17:
time: 76 us; the launch traced here: 75.8 us
  Pallas kernels  68 us (89%)
  matrix products  2.96 us (4%)
  local copies, waits for them, and re-layouts  1.8 us (2%)
  other arithmetic  1.55 us (2%)
  between operations  1.43 us (2%)
    pallas_call x1, Pallas kernels, shards(): pl.pallas_call(kernel, out_shape=(jax.ShapeDtypeStruct((4, width_x, width...  53.4 us
    pallas_call x1, Pallas kernels, gathered_samples(): pl.pallas_call(functools.partial(samples_kernel, nx, ny), out_shape=jax.S...  14.6 us
    dot_general x1, matrix products, shards(): jnp.einsum('txyz,zn->txyn', forward_field[:, 0], source_z, preferred_elem...  2.19 us
    unnamed x12, local copies, waits for them, and re-layouts  1.8 us

profile of v17, /device:TPU:0, one launch (start us, length us, event | category | flops | bytes accessed | tf_op | source)
XLA Modules:
  0.0 75.8 jit_solution(12021097602897908122)
XLA Ops:
  1.3 0.8 %slice_subtract_fusion.1 = (s32[256,1]{0,1:T(1,128)S(1)}, s32[256,1]{0,1:T(1,128)S(1)}, s32[256,1]{0,1:T(1,128)S(1)}, s32[256,1]{0,1:T(1,128)S(1)}, s32[256,1]{0,1:T(1,128)S(1)}, /*index=5*/s32[256,1]{0,1:T(1,128)S(1)}) fusion(s32[256,3]{0,1:T(4,128)} %param.14, s32[]{:T(128)S(6)} %mul.38, s32[]{:T(128)S(6)} %mul.39, s32[256,3]{0,1:T(4,128)} %param.13), kind=kLoop, calls=%fused_computation.25 | loop fusion | flops 1024 | bytes 12296 | tf_op jit(solution)/shard_map/sub | solution.py:403
  2.2 0.0 copy-start.4
  2.2 0.0 copy-start
  2.2 0.0 copy-start.1
  2.2 0.0 copy-start.2
  2.2 0.0 copy-start.3
  2.2 2.2 %fusion.1.local_ref = f32[4,256]{1,0:T(4,128)} fusion(bf16[4,4,8,8,1024]{4,3,2,1,0:T(8,128)(2,1)} %forward.1, s32[256]{0:T(256)S(1)} %bitcast.40, f32[8,8,256]{2,1,0:T(8,128)S(1)} %and_convert_fusion.1), kind=kOutput, calls=%fused_computation.2 | convolution fusion | flops 134609920 | bytes 594944 | tf_op jit(solution)/shard_map/txyz,zn->txyn/dot_general | solution.py:408
  4.4 14.6 %shard_map.95 = f32[4,256]{1,0:T(4,128)} custom-call(f32[4,256]{1,0:T(4,128)} %fusion.1.local_ref), custom_call_target="tpu_custom_call" | custom-call | tf_op jit(solution)/shard_map/pallas_call | solution.py:366
  19.0 0.0 copy-done.4
  19.0 0.7 fusion.14
  19.7 0.8 %fusion.5.inj = f32[4,8,8,1024]{3,2,1,0:T(8,128)S(1)} fusion(s32[256]{0:T(256)S(1)} %bitcast.35, f32[8,8,256]{2,1,0:T(8,128)S(1)} %and_convert_fusion, f32[4,256]{1,0:T(4,128)S(1)} %fusion.14), kind=kOutput, calls=%fused_computation.7 | convolution fusion | flops 805634048 | bytes 1119232 | tf_op jit(solution)/shard_map/txyn,nz->txyz/dot_general | solution.py:416
  20.5 0.0 copy-done
  20.5 0.0 copy-done.1
  20.5 0.0 copy-done.2
  20.5 0.0 copy-done.3
  20.5 53.4 %shard_map.96 = (f32[4,8,8,1024]{3,2,1,0:T(8,128)S(1)}, f32[4,8,8,512]{3,2,1,0:T(8,128)S(1)}) custom-call(f32[4,8,8,1024]{3,2,1,0:T(8,128)S(1)} %bitcast.33, f32[8,8,1024]{2,1,0:T(8,128)S(1)} %copy-done.2, f32[3,1024]{1,0:T(4,128)S(1)} %copy-done.3, bf16[4,4,8,8,1024]{4,3,2,1,0:T(8,128)(2,1)S(1)} %copy-done, f32[4,8,8,1024]{3,2,1,0:T(8,128)S(1)} %fusion.5.inj), custom_call_target="tpu_custom_call" | custom-call | tf_op jit(solution)/shard_map/pallas_call | solution.py:424
  74.0 0.8 %copy.15 = f32[4,8,8,512]{3,2,1,0:T(8,128)} copy(f32[4,8,8,512]{3,2,1,0:T(8,128)S(1)} %get-tuple-element.17) | data formatting | bytes 1048576
  74.8 1.0 %copy.16 = f32[1,4,8,8,1024]{4,3,2,1,0:T(8,128)} copy(f32[1,4,8,8,1024]{4,3,2,1,0:T(8,128)S(1)} %bitcast.34) | data formatting | bytes 2097152
  (7 shorter events, 0.1 us)
Async XLA Ops:
  2.2 16.8 %copy-start.4 = (f32[256,4]{0,1:T(4,128)S(1)}, f32[256,4]{0,1:T(4,128)}, u32[]{:S(2)}) copy-start(f32[256,4]{0,1:T(4,128)} %param.15) | copy-start | bytes 12292
  2.2 18.3 %copy-start = (bf16[4,4,8,8,1024]{4,3,2,1,0:T(8,128)(2,1)S(1)}, bf16[4,4,8,8,1024]{4,3,2,1,0:T(8,128)(2,1)}, u32[]{:S(2)}) copy-start(bf16[4,4,8,8,1024]{4,3,2,1,0:T(8,128)(2,1)} %forward.1) | copy-start | bytes 6291460
  2.2 18.3 %copy-start.1 = (f32[1,4,8,8,1024]{4,3,2,1,0:T(8,128)S(1)}, f32[1,4,8,8,1024]{4,3,2,1,0:T(8,128)}, u32[]{:S(2)}) copy-start(f32[1,4,8,8,1024]{4,3,2,1,0:T(8,128)} %param.11) | copy-start | bytes 3145732
  2.2 18.3 %copy-start.2 = (f32[8,8,1024]{2,1,0:T(8,128)S(1)}, f32[8,8,1024]{2,1,0:T(8,128)}, u32[]{:S(2)}) copy-start(f32[8,8,1024]{2,1,0:T(8,128)} %sound.1) | copy-start | bytes 786436
  2.2 18.3 %copy-start.3 = (f32[3,1024]{1,0:T(4,128)S(1)}, f32[3,1024]{1,0:T(4,128)}, u32[]{:S(2)}) copy-start(f32[3,1024]{1,0:T(4,128)} %wind.1) | copy-start | bytes 36868

commit v18 on v17

--- a/solution.py
+++ b/solution.py
@@ -316,15 +316,10 @@
             src_ref=ksend.at[x], dst_ref=krecv.at[x], send_sem=ks.at[x], recv_sem=kr.at[x],
             device_id=dev_pair, device_id_type=MESH,
         )
+        copy.wait_recv()
+        for c in range(4):
+            kernel_out[c, x] = kernel_out[c, x] + krecv[x, c]
         copy.wait_send()
-        copy.wait_recv()
-
-    def add_partner(x, carry):
-        for c in range(4):
-            kernel_out[c, x] = kernel_out[c, x] + krecv[x, c]
-        return carry
-
-    [add_partner(x, 0) for x in range(width_x)]
 
 
 def samples_kernel(nx, ny, local_ref, out_ref, sent, got_x, got_y, send_sem, recv_sem):

time: 76 us -> 75.9 us (level)
  no operation moved by 1% of the time
where the time goes in v18:
time: 75.9 us; the launch traced here: 75.7 us
  Pallas kernels  68 us (90%)
  matrix products  2.96 us (4%)
  local copies, waits for them, and re-layouts  1.8 us (2%)
  other arithmetic  1.55 us (2%)
  between operations  1.43 us (2%)
    pallas_call x1, Pallas kernels, shards(): pl.pallas_call(kernel, out_shape=(jax.ShapeDtypeStruct((4, width_x, width...  53.4 us
    pallas_call x1, Pallas kernels, gathered_samples(): pl.pallas_call(functools.partial(samples_kernel, nx, ny), out_shape=jax.S...  14.6 us
    dot_general x1, matrix products, shards(): jnp.einsum('txyz,zn->txyn', forward_field[:, 0], source_z, preferred_elem...  2.19 us
    unnamed x12, local copies, waits for them, and re-layouts  1.8 us

profile of v18, /device:TPU:0, one launch (start us, length us, event | category | flops | bytes accessed | tf_op | source)
XLA Modules:
  0.0 75.7 jit_solution(12901351772339456635)
XLA Ops:
  1.3 0.8 %slice_subtract_fusion.1 = (s32[256,1]{0,1:T(1,128)S(1)}, s32[256,1]{0,1:T(1,128)S(1)}, s32[256,1]{0,1:T(1,128)S(1)}, s32[256,1]{0,1:T(1,128)S(1)}, s32[256,1]{0,1:T(1,128)S(1)}, /*index=5*/s32[256,1]{0,1:T(1,128)S(1)}) fusion(s32[256,3]{0,1:T(4,128)} %param.14, s32[]{:T(128)S(6)} %mul.38, s32[]{:T(128)S(6)} %mul.39, s32[256,3]{0,1:T(4,128)} %param.13), kind=kLoop, calls=%fused_computation.25 | loop fusion | flops 1024 | bytes 12296 | tf_op jit(solution)/shard_map/sub | solution.py:398
  2.2 0.0 copy-start.4
  2.2 0.0 copy-start
  2.2 0.0 copy-start.1
  2.2 0.0 copy-start.2
  2.2 0.0 copy-start.3
  2.2 2.2 %fusion.1.local_ref = f32[4,256]{1,0:T(4,128)} fusion(bf16[4,4,8,8,1024]{4,3,2,1,0:T(8,128)(2,1)} %forward.1, s32[256]{0:T(256)S(1)} %bitcast.40, f32[8,8,256]{2,1,0:T(8,128)S(1)} %and_convert_fusion.1), kind=kOutput, calls=%fused_computation.2 | convolution fusion | flops 134609920 | bytes 594944 | tf_op jit(solution)/shard_map/txyz,zn->txyn/dot_general | solution.py:403
  4.4 14.6 %shard_map.95 = f32[4,256]{1,0:T(4,128)} custom-call(f32[4,256]{1,0:T(4,128)} %fusion.1.local_ref), custom_call_target="tpu_custom_call" | custom-call | tf_op jit(solution)/shard_map/pallas_call | solution.py:361
  19.0 0.0 copy-done.4
  19.0 0.7 fusion.14
  19.7 0.8 %fusion.5.inj = f32[4,8,8,1024]{3,2,1,0:T(8,128)S(1)} fusion(s32[256]{0:T(256)S(1)} %bitcast.35, f32[8,8,256]{2,1,0:T(8,128)S(1)} %and_convert_fusion, f32[4,256]{1,0:T(4,128)S(1)} %fusion.14), kind=kOutput, calls=%fused_computation.7 | convolution fusion | flops 805634048 | bytes 1119232 | tf_op jit(solution)/shard_map/txyn,nz->txyz/dot_general | solution.py:411
  20.5 0.0 copy-done
  20.5 0.0 copy-done.1
  20.5 0.0 copy-done.2
  20.5 0.0 copy-done.3
  20.5 53.4 %shard_map.96 = (f32[4,8,8,1024]{3,2,1,0:T(8,128)S(1)}, f32[4,8,8,512]{3,2,1,0:T(8,128)S(1)}) custom-call(f32[4,8,8,1024]{3,2,1,0:T(8,128)S(1)} %bitcast.33, f32[8,8,1024]{2,1,0:T(8,128)S(1)} %copy-done.2, f32[3,1024]{1,0:T(4,128)S(1)} %copy-done.3, bf16[4,4,8,8,1024]{4,3,2,1,0:T(8,128)(2,1)S(1)} %copy-done, f32[4,8,8,1024]{3,2,1,0:T(8,128)S(1)} %fusion.5.inj), custom_call_target="tpu_custom_call" | custom-call | tf_op jit(solution)/shard_map/pallas_call | solution.py:419
  73.9 0.8 %copy.15 = f32[4,8,8,512]{3,2,1,0:T(8,128)} copy(f32[4,8,8,512]{3,2,1,0:T(8,128)S(1)} %get-tuple-element.17) | data formatting | bytes 1048576
  74.7 1.0 %copy.16 = f32[1,4,8,8,1024]{4,3,2,1,0:T(8,128)} copy(f32[1,4,8,8,1024]{4,3,2,1,0:T(8,128)S(1)} %bitcast.34) | data formatting | bytes 2097152
  (7 shorter events, 0.1 us)
Async XLA Ops:
  2.2 16.8 %copy-start.4 = (f32[256,4]{0,1:T(4,128)S(1)}, f32[256,4]{0,1:T(4,128)}, u32[]{:S(2)}) copy-start(f32[256,4]{0,1:T(4,128)} %param.15) | copy-start | bytes 12292
  2.2 18.3 %copy-start = (bf16[4,4,8,8,1024]{4,3,2,1,0:T(8,128)(2,1)S(1)}, bf16[4,4,8,8,1024]{4,3,2,1,0:T(8,128)(2,1)}, u32[]{:S(2)}) copy-start(bf16[4,4,8,8,1024]{4,3,2,1,0:T(8,128)(2,1)} %forward.1) | copy-start | bytes 6291460
  2.2 18.3 %copy-start.1 = (f32[1,4,8,8,1024]{4,3,2,1,0:T(8,128)S(1)}, f32[1,4,8,8,1024]{4,3,2,1,0:T(8,128)}, u32[]{:S(2)}) copy-start(f32[1,4,8,8,1024]{4,3,2,1,0:T(8,128)} %param.11) | copy-start | bytes 3145732
  2.2 18.3 %copy-start.2 = (f32[8,8,1024]{2,1,0:T(8,128)S(1)}, f32[8,8,1024]{2,1,0:T(8,128)}, u32[]{:S(2)}) copy-start(f32[8,8,1024]{2,1,0:T(8,128)} %sound.1) | copy-start | bytes 786436
  2.2 18.3 %copy-start.3 = (f32[3,1024]{1,0:T(4,128)S(1)}, f32[3,1024]{1,0:T(4,128)}, u32[]{:S(2)}) copy-start(f32[3,1024]{1,0:T(4,128)} %wind.1) | copy-start | bytes 36868

commit v19 on v18

--- a/solution.py
+++ b/solution.py
@@ -269,7 +269,10 @@
             ypsend.at[0], ypsend.at[1], yprecv.at[par, 0], yprecv.at[par, 1],
             ps, pr,
         )
-        send_forward(snap)
+        if step < steps - 1:
+            send_forward(snap)
+        if step == steps - 2:
+            send_forward(snap - 1)
         settle(velocity_copies)
 
         def advection_slab(x, carry, par=par):

time: 75.9 us -> 78.4 us (1.033)
  Pallas kernels: 68 us -> 70.5 us
    pallas_call x1, Pallas kernels: 53.4 us -> 55.9 us  [shards(): pl.pallas_call(kernel, out_shape=(jax.ShapeDtypeStruct((4, width_x, width...]
where the time goes in v19:
time: 78.4 us; the launch traced here: 78.2 us
  Pallas kernels  70.5 us (90%)
  matrix products  2.96 us (4%)
  local copies, waits for them, and re-layouts  1.8 us (2%)
  other arithmetic  1.55 us (2%)
  between operations  1.43 us (2%)
    pallas_call x1, Pallas kernels, shards(): pl.pallas_call(kernel, out_shape=(jax.ShapeDtypeStruct((4, width_x, width...  55.9 us
    pallas_call x1, Pallas kernels, gathered_samples(): pl.pallas_call(functools.partial(samples_kernel, nx, ny), out_shape=jax.S...  14.6 us
    dot_general x1, matrix products, shards(): jnp.einsum('txyz,zn->txyn', forward_field[:, 0], source_z, preferred_elem...  2.19 us
    unnamed x12, local copies, waits for them, and re-layouts  1.8 us

profile of v19, /device:TPU:0, one launch (start us, length us, event | category | flops | bytes accessed | tf_op | source)
XLA Modules:
  0.0 78.2 jit_solution(15070981574645344873)
XLA Ops:
  1.3 0.8 %slice_subtract_fusion.1 = (s32[256,1]{0,1:T(1,128)S(1)}, s32[256,1]{0,1:T(1,128)S(1)}, s32[256,1]{0,1:T(1,128)S(1)}, s32[256,1]{0,1:T(1,128)S(1)}, s32[256,1]{0,1:T(1,128)S(1)}, /*index=5*/s32[256,1]{0,1:T(1,128)S(1)}) fusion(s32[256,3]{0,1:T(4,128)} %param.14, s32[]{:T(128)S(6)} %mul.38, s32[]{:T(128)S(6)} %mul.39, s32[256,3]{0,1:T(4,128)} %param.13), kind=kLoop, calls=%fused_computation.25 | loop fusion | flops 1024 | bytes 12296 | tf_op jit(solution)/shard_map/sub | solution.py:401
  2.2 0.0 copy-start.4
  2.2 0.0 copy-start
  2.2 0.0 copy-start.1
  2.2 0.0 copy-start.2
  2.2 0.0 copy-start.3
  2.2 2.2 %fusion.1.local_ref = f32[4,256]{1,0:T(4,128)} fusion(bf16[4,4,8,8,1024]{4,3,2,1,0:T(8,128)(2,1)} %forward.1, s32[256]{0:T(256)S(1)} %bitcast.40, f32[8,8,256]{2,1,0:T(8,128)S(1)} %and_convert_fusion.1), kind=kOutput, calls=%fused_computation.2 | convolution fusion | flops 134609920 | bytes 594944 | tf_op jit(solution)/shard_map/txyz,zn->txyn/dot_general | solution.py:406
  4.4 14.6 %shard_map.95 = f32[4,256]{1,0:T(4,128)} custom-call(f32[4,256]{1,0:T(4,128)} %fusion.1.local_ref), custom_call_target="tpu_custom_call" | custom-call | tf_op jit(solution)/shard_map/pallas_call | solution.py:364
  19.0 0.0 copy-done.4
  19.0 0.7 fusion.14
  19.7 0.8 fusion.5.inj
  20.5 0.0 copy-done
  20.5 0.0 copy-done.1
  20.5 0.0 copy-done.2
  20.5 0.0 copy-done.3
  20.5 55.9 %shard_map.96 = (f32[4,8,8,1024]{3,2,1,0:T(8,128)S(1)}, f32[4,8,8,512]{3,2,1,0:T(8,128)S(1)}) custom-call(f32[4,8,8,1024]{3,2,1,0:T(8,128)S(1)} %bitcast.33, f32[8,8,1024]{2,1,0:T(8,128)S(1)} %copy-done.2, f32[3,1024]{1,0:T(4,128)S(1)} %copy-done.3, bf16[4,4,8,8,1024]{4,3,2,1,0:T(8,128)(2,1)S(1)} %copy-done, f32[4,8,8,1024]{3,2,1,0:T(8,128)S(1)} %fusion.5.inj), custom_call_target="tpu_custom_call" | custom-call | tf_op jit(solution)/shard_map/pallas_call | solution.py:422
  76.4 0.8 %copy.15 = f32[4,8,8,512]{3,2,1,0:T(8,128)} copy(f32[4,8,8,512]{3,2,1,0:T(8,128)S(1)} %get-tuple-element.17) | data formatting | bytes 1048576
  77.2 1.0 %copy.16 = f32[1,4,8,8,1024]{4,3,2,1,0:T(8,128)} copy(f32[1,4,8,8,1024]{4,3,2,1,0:T(8,128)S(1)} %bitcast.34) | data formatting | bytes 2097152
  (7 shorter events, 0.1 us)
Async XLA Ops:
  2.2 16.8 %copy-start.4 = (f32[256,4]{0,1:T(4,128)S(1)}, f32[256,4]{0,1:T(4,128)}, u32[]{:S(2)}) copy-start(f32[256,4]{0,1:T(4,128)} %param.15) | copy-start | bytes 12292
  2.2 18.3 %copy-start = (bf16[4,4,8,8,1024]{4,3,2,1,0:T(8,128)(2,1)S(1)}, bf16[4,4,8,8,1024]{4,3,2,1,0:T(8,128)(2,1)}, u32[]{:S(2)}) copy-start(bf16[4,4,8,8,1024]{4,3,2,1,0:T(8,128)(2,1)} %forward.1) | copy-start | bytes 6291460
  2.2 18.3 %copy-start.1 = (f32[1,4,8,8,1024]{4,3,2,1,0:T(8,128)S(1)}, f32[1,4,8,8,1024]{4,3,2,1,0:T(8,128)}, u32[]{:S(2)}) copy-start(f32[1,4,8,8,1024]{4,3,2,1,0:T(8,128)} %param.11) | copy-start | bytes 3145732
  2.2 18.3 %copy-start.2 = (f32[8,8,1024]{2,1,0:T(8,128)S(1)}, f32[8,8,1024]{2,1,0:T(8,128)}, u32[]{:S(2)}) copy-start(f32[8,8,1024]{2,1,0:T(8,128)} %sound.1) | copy-start | bytes 786436
  2.2 18.3 %copy-start.3 = (f32[3,1024]{1,0:T(4,128)S(1)}, f32[3,1024]{1,0:T(4,128)}, u32[]{:S(2)}) copy-start(f32[3,1024]{1,0:T(4,128)} %wind.1) | copy-start | bytes 36868

commit v20 on v18

--- a/solution.py
+++ b/solution.py
@@ -269,7 +269,8 @@
             ypsend.at[0], ypsend.at[1], yprecv.at[par, 0], yprecv.at[par, 1],
             ps, pr,
         )
-        send_forward(snap)
+        if not last:
+            send_forward(snap)
         settle(velocity_copies)
 
         def advection_slab(x, carry, par=par):
@@ -285,6 +286,8 @@
 
         [advection_slab(x, 0) for x in range(width_x)]
         settle(pressure_copies)
+        if last:
+            send_forward(snap)
 
         def velocity_slab(x, carry, par=par, nxt=nxt, last=last):
             xp = x + 1

time: 75.9 us -> 79 us (1.041)
  Pallas kernels: 68 us -> 71 us
    pallas_call x1, Pallas kernels: 53.4 us -> 56.4 us  [shards(): pl.pallas_call(kernel, out_shape=(jax.ShapeDtypeStruct((4, width_x, width...]
where the time goes in v20:
time: 79 us; the launch traced here: 78.7 us
  Pallas kernels  71 us (90%)
  matrix products  2.96 us (4%)
  local copies, waits for them, and re-layouts  1.8 us (2%)
  other arithmetic  1.55 us (2%)
  between operations  1.43 us (2%)
    pallas_call x1, Pallas kernels, shards(): pl.pallas_call(kernel, out_shape=(jax.ShapeDtypeStruct((4, width_x, width...  56.4 us
    pallas_call x1, Pallas kernels, gathered_samples(): pl.pallas_call(functools.partial(samples_kernel, nx, ny), out_shape=jax.S...  14.6 us
    dot_general x1, matrix products, shards(): jnp.einsum('txyz,zn->txyn', forward_field[:, 0], source_z, preferred_elem...  2.19 us
    unnamed x12, local copies, waits for them, and re-layouts  1.8 us

profile of v20, /device:TPU:0, one launch (start us, length us, event | category | flops | bytes accessed | tf_op | source)
XLA Modules:
  0.0 78.7 jit_solution(10222095748174979162)
XLA Ops:
  1.3 0.8 %slice_subtract_fusion.1 = (s32[256,1]{0,1:T(1,128)S(1)}, s32[256,1]{0,1:T(1,128)S(1)}, s32[256,1]{0,1:T(1,128)S(1)}, s32[256,1]{0,1:T(1,128)S(1)}, s32[256,1]{0,1:T(1,128)S(1)}, /*index=5*/s32[256,1]{0,1:T(1,128)S(1)}) fusion(s32[256,3]{0,1:T(4,128)} %param.14, s32[]{:T(128)S(6)} %mul.38, s32[]{:T(128)S(6)} %mul.39, s32[256,3]{0,1:T(4,128)} %param.13), kind=kLoop, calls=%fused_computation.25 | loop fusion | flops 1024 | bytes 12296 | tf_op jit(solution)/shard_map/sub | solution.py:401
  2.2 0.0 copy-start.4
  2.2 0.0 copy-start
  2.2 0.0 copy-start.1
  2.2 0.0 copy-start.2
  2.2 0.0 copy-start.3
  2.2 2.2 %fusion.1.local_ref = f32[4,256]{1,0:T(4,128)} fusion(bf16[4,4,8,8,1024]{4,3,2,1,0:T(8,128)(2,1)} %forward.1, s32[256]{0:T(256)S(1)} %bitcast.40, f32[8,8,256]{2,1,0:T(8,128)S(1)} %and_convert_fusion.1), kind=kOutput, calls=%fused_computation.2 | convolution fusion | flops 134609920 | bytes 594944 | tf_op jit(solution)/shard_map/txyz,zn->txyn/dot_general | solution.py:406
  4.4 14.6 %shard_map.95 = f32[4,256]{1,0:T(4,128)} custom-call(f32[4,256]{1,0:T(4,128)} %fusion.1.local_ref), custom_call_target="tpu_custom_call" | custom-call | tf_op jit(solution)/shard_map/pallas_call | solution.py:364
  19.0 0.0 copy-done.4
  19.0 0.7 fusion.14
  19.7 0.8 fusion.5.inj
  20.5 0.0 copy-done
  20.5 0.0 copy-done.1
  20.5 0.0 copy-done.2
  20.5 0.0 copy-done.3
  20.5 56.4 %shard_map.96 = (f32[4,8,8,1024]{3,2,1,0:T(8,128)S(1)}, f32[4,8,8,512]{3,2,1,0:T(8,128)S(1)}) custom-call(f32[4,8,8,1024]{3,2,1,0:T(8,128)S(1)} %bitcast.33, f32[8,8,1024]{2,1,0:T(8,128)S(1)} %copy-done.2, f32[3,1024]{1,0:T(4,128)S(1)} %copy-done.3, bf16[4,4,8,8,1024]{4,3,2,1,0:T(8,128)(2,1)S(1)} %copy-done, f32[4,8,8,1024]{3,2,1,0:T(8,128)S(1)} %fusion.5.inj), custom_call_target="tpu_custom_call" | custom-call | tf_op jit(solution)/shard_map/pallas_call | solution.py:422
  77.0 0.8 %copy.15 = f32[4,8,8,512]{3,2,1,0:T(8,128)} copy(f32[4,8,8,512]{3,2,1,0:T(8,128)S(1)} %get-tuple-element.17) | data formatting | bytes 1048576
  77.8 1.0 %copy.16 = f32[1,4,8,8,1024]{4,3,2,1,0:T(8,128)} copy(f32[1,4,8,8,1024]{4,3,2,1,0:T(8,128)S(1)} %bitcast.34) | data formatting | bytes 2097152
  (7 shorter events, 0.1 us)
Async XLA Ops:
  2.2 16.8 %copy-start.4 = (f32[256,4]{0,1:T(4,128)S(1)}, f32[256,4]{0,1:T(4,128)}, u32[]{:S(2)}) copy-start(f32[256,4]{0,1:T(4,128)} %param.15) | copy-start | bytes 12292
  2.2 18.3 %copy-start = (bf16[4,4,8,8,1024]{4,3,2,1,0:T(8,128)(2,1)S(1)}, bf16[4,4,8,8,1024]{4,3,2,1,0:T(8,128)(2,1)}, u32[]{:S(2)}) copy-start(bf16[4,4,8,8,1024]{4,3,2,1,0:T(8,128)(2,1)} %forward.1) | copy-start | bytes 6291460
  2.2 18.3 %copy-start.1 = (f32[1,4,8,8,1024]{4,3,2,1,0:T(8,128)S(1)}, f32[1,4,8,8,1024]{4,3,2,1,0:T(8,128)}, u32[]{:S(2)}) copy-start(f32[1,4,8,8,1024]{4,3,2,1,0:T(8,128)} %param.11) | copy-start | bytes 3145732
  2.2 18.3 %copy-start.2 = (f32[8,8,1024]{2,1,0:T(8,128)S(1)}, f32[8,8,1024]{2,1,0:T(8,128)}, u32[]{:S(2)}) copy-start(f32[8,8,1024]{2,1,0:T(8,128)} %sound.1) | copy-start | bytes 786436
  2.2 18.3 %copy-start.3 = (f32[3,1024]{1,0:T(4,128)S(1)}, f32[3,1024]{1,0:T(4,128)}, u32[]{:S(2)}) copy-start(f32[3,1024]{1,0:T(4,128)} %wind.1) | copy-start | bytes 36868

commit v21 on v18

--- a/solution.py
+++ b/solution.py
@@ -270,6 +270,12 @@
             ps, pr,
         )
         send_forward(snap)
+        def vertical_slab(x, carry, par=par):
+            for i in range(3):
+                advect[i, x] = wv * dz(pads[par, 1 + i, x + 1])
+            return carry
+
+        [vertical_slab(x, 0) for x in range(width_x)]
         settle(velocity_copies)
 
         def advection_slab(x, carry, par=par):
@@ -279,8 +285,7 @@
                 a = old[1 + i, xp]
                 dxa = (old[1 + i, xp + 1] - old[1 + i, x]) * 0.5
                 dya = dy(a, yrecv[par, 0, Y_SLOT[1 + i], x:x + 1, :], yrecv[par, 1, Y_SLOT[1 + i], x:x + 1, :])
-                dza = dz(a)
-                advect[i, x] = we * dxa + wn * dya + wv * dza
+                advect[i, x] = we * dxa + wn * dya + advect[i, x]
             return carry
 
         [advection_slab(x, 0) for x in range(width_x)]

time: 75.9 us -> 75.9 us (level)
  no operation moved by 1% of the time
where the time goes in v21:
time: 75.9 us; the launch traced here: 75.7 us
  Pallas kernels  68 us (90%)
  matrix products  2.96 us (4%)
  local copies, waits for them, and re-layouts  1.8 us (2%)
  other arithmetic  1.55 us (2%)
  between operations  1.43 us (2%)
    pallas_call x1, Pallas kernels, shards(): pl.pallas_call(kernel, out_shape=(jax.ShapeDtypeStruct((4, width_x, width...  53.4 us
    pallas_call x1, Pallas kernels, gathered_samples(): pl.pallas_call(functools.partial(samples_kernel, nx, ny), out_shape=jax.S...  14.6 us
    dot_general x1, matrix products, shards(): jnp.einsum('txyz,zn->txyn', forward_field[:, 0], source_z, preferred_elem...  2.19 us
    unnamed x12, local copies, waits for them, and re-layouts  1.8 us

profile of v21, /device:TPU:0, one launch (start us, length us, event | category | flops | bytes accessed | tf_op | source)
XLA Modules:
  0.0 75.7 jit_solution(8265248050105594361)
XLA Ops:
  1.3 0.8 %slice_subtract_fusion.1 = (s32[256,1]{0,1:T(1,128)S(1)}, s32[256,1]{0,1:T(1,128)S(1)}, s32[256,1]{0,1:T(1,128)S(1)}, s32[256,1]{0,1:T(1,128)S(1)}, s32[256,1]{0,1:T(1,128)S(1)}, /*index=5*/s32[256,1]{0,1:T(1,128)S(1)}) fusion(s32[256,3]{0,1:T(4,128)} %param.14, s32[]{:T(128)S(6)} %mul.38, s32[]{:T(128)S(6)} %mul.39, s32[256,3]{0,1:T(4,128)} %param.13), kind=kLoop, calls=%fused_computation.25 | loop fusion | flops 1024 | bytes 12296 | tf_op jit(solution)/shard_map/sub | solution.py:403
  2.2 0.0 copy-start.4
  2.2 0.0 copy-start
  2.2 0.0 copy-start.1
  2.2 0.0 copy-start.2
  2.2 0.0 copy-start.3
  2.2 2.2 %fusion.1.local_ref = f32[4,256]{1,0:T(4,128)} fusion(bf16[4,4,8,8,1024]{4,3,2,1,0:T(8,128)(2,1)} %forward.1, s32[256]{0:T(256)S(1)} %bitcast.40, f32[8,8,256]{2,1,0:T(8,128)S(1)} %and_convert_fusion.1), kind=kOutput, calls=%fused_computation.2 | convolution fusion | flops 134609920 | bytes 594944 | tf_op jit(solution)/shard_map/txyz,zn->txyn/dot_general | solution.py:408
  4.4 14.6 %shard_map.95 = f32[4,256]{1,0:T(4,128)} custom-call(f32[4,256]{1,0:T(4,128)} %fusion.1.local_ref), custom_call_target="tpu_custom_call" | custom-call | tf_op jit(solution)/shard_map/pallas_call | solution.py:366
  19.0 0.0 copy-done.4
  19.0 0.7 fusion.14
  19.7 0.8 %fusion.5.inj = f32[4,8,8,1024]{3,2,1,0:T(8,128)S(1)} fusion(s32[256]{0:T(256)S(1)} %bitcast.35, f32[8,8,256]{2,1,0:T(8,128)S(1)} %and_convert_fusion, f32[4,256]{1,0:T(4,128)S(1)} %fusion.14), kind=kOutput, calls=%fused_computation.7 | convolution fusion | flops 805634048 | bytes 1119232 | tf_op jit(solution)/shard_map/txyn,nz->txyz/dot_general | solution.py:416
  20.5 0.0 copy-done
  20.5 0.0 copy-done.1
  20.5 0.0 copy-done.2
  20.5 0.0 copy-done.3
  20.5 53.4 %shard_map.96 = (f32[4,8,8,1024]{3,2,1,0:T(8,128)S(1)}, f32[4,8,8,512]{3,2,1,0:T(8,128)S(1)}) custom-call(f32[4,8,8,1024]{3,2,1,0:T(8,128)S(1)} %bitcast.33, f32[8,8,1024]{2,1,0:T(8,128)S(1)} %copy-done.2, f32[3,1024]{1,0:T(4,128)S(1)} %copy-done.3, bf16[4,4,8,8,1024]{4,3,2,1,0:T(8,128)(2,1)S(1)} %copy-done, f32[4,8,8,1024]{3,2,1,0:T(8,128)S(1)} %fusion.5.inj), custom_call_target="tpu_custom_call" | custom-call | tf_op jit(solution)/shard_map/pallas_call | solution.py:424
  73.9 0.8 %copy.15 = f32[4,8,8,512]{3,2,1,0:T(8,128)} copy(f32[4,8,8,512]{3,2,1,0:T(8,128)S(1)} %get-tuple-element.17) | data formatting | bytes 1048576
  74.7 1.0 %copy.16 = f32[1,4,8,8,1024]{4,3,2,1,0:T(8,128)} copy(f32[1,4,8,8,1024]{4,3,2,1,0:T(8,128)S(1)} %bitcast.34) | data formatting | bytes 2097152
  (7 shorter events, 0.1 us)
Async XLA Ops:
  2.2 16.8 %copy-start.4 = (f32[256,4]{0,1:T(4,128)S(1)}, f32[256,4]{0,1:T(4,128)}, u32[]{:S(2)}) copy-start(f32[256,4]{0,1:T(4,128)} %param.15) | copy-start | bytes 12292
  2.2 18.3 %copy-start = (bf16[4,4,8,8,1024]{4,3,2,1,0:T(8,128)(2,1)S(1)}, bf16[4,4,8,8,1024]{4,3,2,1,0:T(8,128)(2,1)}, u32[]{:S(2)}) copy-start(bf16[4,4,8,8,1024]{4,3,2,1,0:T(8,128)(2,1)} %forward.1) | copy-start | bytes 6291460
  2.2 18.3 %copy-start.1 = (f32[1,4,8,8,1024]{4,3,2,1,0:T(8,128)S(1)}, f32[1,4,8,8,1024]{4,3,2,1,0:T(8,128)}, u32[]{:S(2)}) copy-start(f32[1,4,8,8,1024]{4,3,2,1,0:T(8,128)} %param.11) | copy-start | bytes 3145732
  2.2 18.3 %copy-start.2 = (f32[8,8,1024]{2,1,0:T(8,128)S(1)}, f32[8,8,1024]{2,1,0:T(8,128)}, u32[]{:S(2)}) copy-start(f32[8,8,1024]{2,1,0:T(8,128)} %sound.1) | copy-start | bytes 786436
  2.2 18.3 %copy-start.3 = (f32[3,1024]{1,0:T(4,128)S(1)}, f32[3,1024]{1,0:T(4,128)}, u32[]{:S(2)}) copy-start(f32[3,1024]{1,0:T(4,128)} %wind.1) | copy-start | bytes 36868
